TPU v7x, 32 devices: a whole 2x2x4 slice. The times are simulated.
32 devices in a mesh: rows: 8 (over z, x), seq: 4 (over y, core).
Axes of the slice: x: 2, y: 2, z: 4, core: 2. Of those that a mesh axis runs over, the one named last changes fastest.
Arguments:
- layer_input: bfloat16 [8, 1024, 2048], P('rows', 'seq'), may hold values from -6 to 6
- doc_lengths: int32 [8, 2], P('rows'), may hold values from 1 to 768, 1024 in all within a row
- w_qkv: bfloat16 [2048, 6144], P(('rows', 'seq')), may hold values from -0.125 to 0.125
- w_out: bfloat16 [2048, 2048], P(('rows', 'seq')), may hold values from -0.125 to 0.125
- w_gate_up: bfloat16 [2048, 16384], P(('rows', 'seq')), may hold values from -0.125 to 0.125
- w_down: bfloat16 [8192, 2048], P(('rows', 'seq')), may hold values from -0.0625 to 0.0625
- norm_gains: float32 [4, 2048], replicated, may hold values from 0.5 to 1.5
- cotangent: bfloat16 [8, 1024, 2048], P('rows', 'seq'), may hold values from -6 to 6
Outputs:
- output: bfloat16 [8, 1024, 2048], P('rows', 'seq')
- grad_input: float32 [8, 1024, 2048], P('rows', 'seq')
- grad_qkv: float32 [2048, 6144], P(('rows', 'seq'))
- grad_out: float32 [2048, 2048], P(('rows', 'seq'))
- grad_gate_up: float32 [2048, 16384], P(('rows', 'seq'))
- grad_down: float32 [8192, 2048], P(('rows', 'seq'))
- grad_gains: float32 [4, 2048], replicated
Inputs may be any that keep to these rules, and one draw needn't show every extreme that they name: `doc_lengths`: each row's 2 lengths add up to 1024; no length exceeds 768.
All inputs are finite; a program needn't handle non-finite values.
Results may differ from a plain program's by a relative error of at most 0.017.
Values may be sent and summed in bfloat16 or wider, within the bound.
No kernel may reach another device: no remote copies, remote signals or barrier semaphores. Data moves between devices by JAX's collectives and lax.ppermute only.
A program may use at most 512 MiB of HBM per device.

v0:
```python
import jax
import jax.numpy as jnp
from jax import lax
from jax.sharding import PartitionSpec as P

HD = 128


eps = 1e-06
rope_base = 500000.0


def normalize(tensor, gain_row):
    inv_scale = lax.rsqrt(jnp.mean(tensor * tensor, axis=-1, keepdims=True) + eps)
    return (tensor * inv_scale * gain_row, inv_scale)


def norm_back(tensor, inv_scale, gain_row, upstream):
    scaled = upstream * gain_row
    average = jnp.mean(scaled * tensor, axis=-1, keepdims=True)
    grad_tensor = inv_scale * scaled - tensor * (inv_scale * inv_scale * inv_scale) * average
    gain_term = jnp.sum(upstream * tensor * inv_scale, axis=0)
    return (grad_tensor, gain_term)


def rope_tables(positions):
    half_width = HD // 2
    frequency = jnp.power(rope_base, -(jnp.arange(half_width, dtype=jnp.float32) * 2.0) / HD)
    angles = positions.astype(jnp.float32)[..., None] * frequency
    angles = jnp.concatenate([angles, angles], axis=-1)
    return (jnp.cos(angles)[:, :, None, :], jnp.sin(angles)[:, :, None, :])


def rotate(tensor, cosine, sine_table, turn_sign):
    half_width = HD // 2
    turned = jnp.concatenate([-tensor[..., half_width:], tensor[..., :half_width]], axis=-1)
    return tensor * cosine + turn_sign * turned * sine_table


def back_product(left_side, right_side):
    return lax.dot_general(
        left_side, right_side, (((1,), (1,)), ((), ())), preferred_element_type=jnp.float32
    )


def make_term(left_side, right_side):
    return lax.dot_general(
        left_side, right_side, (((0,), (0,)), ((), ())), preferred_element_type=jnp.float32
    )


def per_device(layer_input, doc_lengths, w_qkv, w_out, w_gate_up, w_down, norm_gains, cotangent):
    rows_dev, tok_local, model_width = layer_input.shape
    seq_parts = lax.axis_size("seq")
    row_length = tok_local * seq_parts
    head_count = model_width // HD
    tok_count = rows_dev * tok_local
    flat_in = layer_input.reshape(tok_count, model_width)
    weight_set = (w_qkv, w_out, w_gate_up, w_down)
    full_qkv, full_out, full_gu, full_down = (
        lax.all_gather(weight_set[0], ("rows", "seq"), axis=0, tiled=True),
        lax.all_gather(weight_set[1], ("rows", "seq"), axis=0, tiled=True),
        lax.all_gather(weight_set[2], ("rows", "seq"), axis=0, tiled=True),
        lax.all_gather(weight_set[3], ("rows", "seq"), axis=0, tiled=True),
    )
    doc_ends = jnp.cumsum(doc_lengths, axis=1)
    whole_places = jnp.arange(row_length, dtype=jnp.int32)
    segment = jnp.sum(
        (whole_places[None, :, None] >= doc_ends[:, None, :]).astype(jnp.int32), axis=-1
    )
    local_places = lax.axis_index("seq") * tok_local + jnp.arange(tok_local, dtype=jnp.int32)
    passed = (local_places[None, :, None] >= doc_ends[:, None, :]).astype(jnp.int32)
    doc_start = jnp.sum(passed * doc_lengths[:, None, :], axis=-1)
    positions = local_places[None, :] - doc_start
    cosine, sine_table = rope_tables(positions)
    mixed_all = jnp.dot(flat_in, full_qkv, preferred_element_type=jnp.float32)
    query_pre = mixed_all[:, :model_width]
    key_pre = mixed_all[:, model_width : 2 * model_width]
    query_normed, query_scale = normalize(query_pre, norm_gains[0])
    key_normed, key_scale = normalize(key_pre, norm_gains[1])
    shape4 = (rows_dev, tok_local, head_count, HD)
    query_low = rotate(query_normed.reshape(shape4), cosine, sine_table, 1.0).astype(jnp.bfloat16)
    key_low = rotate(key_normed.reshape(shape4), cosine, sine_table, 1.0).astype(jnp.bfloat16)
    value_low = mixed_all[:, 2 * model_width :].reshape(shape4).astype(jnp.bfloat16)
    query_heads, key_heads, value_heads = (
        lax.all_to_all(query_low, "seq", split_axis=2, concat_axis=1, tiled=True),
        lax.all_to_all(key_low, "seq", split_axis=2, concat_axis=1, tiled=True),
        lax.all_to_all(value_low, "seq", split_axis=2, concat_axis=1, tiled=True),
    )
    score_scale = 1.0 / HD**0.5
    causal = whole_places[:, None] >= whole_places[None, :]
    allowed = causal[None] & (segment[:, :, None] == segment[:, None, :])

    def score_block():
        raw_scores = (
            jnp.einsum(
                "bqhd,bkhd->bhqk", query_heads, key_heads, preferred_element_type=jnp.float32
            )
            * score_scale
        )
        return jnp.where(allowed[:, None], raw_scores, -1e30)

    scores = score_block()
    row_max = jnp.max(scores, axis=-1, keepdims=True)
    exponent = jnp.exp(scores - row_max)
    row_total = jnp.sum(exponent, axis=-1, keepdims=True)
    log_total = row_max + jnp.log(row_total)
    attn_probs = (exponent / row_total).astype(jnp.bfloat16)
    attended_heads = jnp.einsum(
        "bhqk,bkhd->bqhd", attn_probs, value_heads, preferred_element_type=jnp.float32
    ).astype(jnp.bfloat16)
    attended_seq = lax.all_to_all(attended_heads, "seq", split_axis=1, concat_axis=2, tiled=True)
    attended_flat = attended_seq.reshape(tok_count, model_width)
    branch = jnp.dot(attended_flat, full_out, preferred_element_type=jnp.float32)
    branch_normed, branch_scale = normalize(branch, norm_gains[2])
    hidden = flat_in.astype(jnp.float32) + branch_normed
    hidden_low = hidden.astype(jnp.bfloat16)
    gate_up = jnp.dot(hidden_low, full_gu, preferred_element_type=jnp.float32)
    ff_width = gate_up.shape[1] // 2
    gate_part = gate_up[:, :ff_width]
    up_part = gate_up[:, ff_width:]
    silu_gate = jax.nn.silu(gate_part)
    inner = (silu_gate * up_part).astype(jnp.bfloat16)
    branch2 = jnp.dot(inner, full_down, preferred_element_type=jnp.float32)
    branch2_normed, branch2_scale = normalize(branch2, norm_gains[3])
    output = (hidden + branch2_normed).astype(jnp.bfloat16).reshape(layer_input.shape)
    back_qkv, back_out, back_gu, back_down = (
        lax.all_gather(weight_set[0], ("rows", "seq"), axis=0, tiled=True),
        lax.all_gather(weight_set[1], ("rows", "seq"), axis=0, tiled=True),
        lax.all_gather(weight_set[2], ("rows", "seq"), axis=0, tiled=True),
        lax.all_gather(weight_set[3], ("rows", "seq"), axis=0, tiled=True),
    )
    upstream = cotangent.reshape(tok_count, model_width).astype(jnp.float32)
    grad_branch2, gain_mlp = norm_back(branch2, branch2_scale, norm_gains[3], upstream)
    grad_branch2 = grad_branch2.astype(jnp.bfloat16)
    grad_inner = back_product(grad_branch2, back_down)
    sigmoid_gate = jax.nn.sigmoid(gate_part)
    grad_gate = grad_inner * up_part * sigmoid_gate * (1.0 + gate_part * (1.0 - sigmoid_gate))
    grad_up = grad_inner * silu_gate
    grad_gu_low = jnp.concatenate([grad_gate, grad_up], axis=1).astype(jnp.bfloat16)
    grad_hidden = upstream + back_product(grad_gu_low, back_gu)
    grad_branch, gain_attn = norm_back(branch, branch_scale, norm_gains[2], grad_hidden)
    grad_branch = grad_branch.astype(jnp.bfloat16)
    grad_attended = back_product(grad_branch, back_out).astype(jnp.bfloat16).reshape(shape4)
    grad_att_heads = lax.all_to_all(grad_attended, "seq", split_axis=2, concat_axis=1, tiled=True)
    again_probs = jnp.exp(score_block() - log_total)
    grad_probs = jnp.einsum(
        "bqhd,bkhd->bhqk", grad_att_heads, value_heads, preferred_element_type=jnp.float32
    )
    grad_value_heads = jnp.einsum(
        "bhqk,bqhd->bkhd",
        again_probs.astype(jnp.bfloat16),
        grad_att_heads,
        preferred_element_type=jnp.float32,
    )
    row_sum = jnp.sum(again_probs * grad_probs, axis=-1, keepdims=True)
    grad_scores = (again_probs * (grad_probs - row_sum)).astype(jnp.bfloat16)
    grad_query_heads = (
        jnp.einsum("bhqk,bkhd->bqhd", grad_scores, key_heads, preferred_element_type=jnp.float32)
        * score_scale
    )
    grad_key_heads = (
        jnp.einsum("bhqk,bqhd->bkhd", grad_scores, query_heads, preferred_element_type=jnp.float32)
        * score_scale
    )
    grads_sent = (
        grad_query_heads.astype(jnp.bfloat16),
        grad_key_heads.astype(jnp.bfloat16),
        grad_value_heads.astype(jnp.bfloat16),
    )
    grad_query_seq, grad_key_seq, grad_value_seq = (
        lax.all_to_all(grads_sent[0], "seq", split_axis=1, concat_axis=2, tiled=True),
        lax.all_to_all(grads_sent[1], "seq", split_axis=1, concat_axis=2, tiled=True),
        lax.all_to_all(grads_sent[2], "seq", split_axis=1, concat_axis=2, tiled=True),
    )
    grad_query_n = rotate(grad_query_seq.astype(jnp.float32), cosine, sine_table, -1.0).reshape(
        tok_count, model_width
    )
    grad_key_n = rotate(grad_key_seq.astype(jnp.float32), cosine, sine_table, -1.0).reshape(
        tok_count, model_width
    )
    grad_query_pre, gain_query = norm_back(query_pre, query_scale, norm_gains[0], grad_query_n)
    grad_key_pre, gain_key = norm_back(key_pre, key_scale, norm_gains[1], grad_key_n)
    grad_mixed = jnp.concatenate(
        [
            grad_query_pre,
            grad_key_pre,
            grad_value_seq.reshape(tok_count, model_width).astype(jnp.float32),
        ],
        axis=1,
    ).astype(jnp.bfloat16)
    grad_input = (grad_hidden + back_product(grad_mixed, back_qkv)).reshape(layer_input.shape)
    grad_qkv = lax.psum_scatter(
        make_term(flat_in, grad_mixed), ("rows", "seq"), scatter_dimension=0, tiled=True
    )
    grad_out = lax.psum_scatter(
        make_term(attended_flat, grad_branch), ("rows", "seq"), scatter_dimension=0, tiled=True
    )
    grad_gate_up = lax.psum_scatter(
        make_term(hidden_low, grad_gu_low), ("rows", "seq"), scatter_dimension=0, tiled=True
    )
    grad_down = lax.psum_scatter(
        make_term(inner, grad_branch2), ("rows", "seq"), scatter_dimension=0, tiled=True
    )
    gain_terms = jnp.stack([gain_query, gain_key, gain_attn, gain_mlp])
    grad_gains = lax.psum(gain_terms, ("rows", "seq"))
    return (output, grad_input, grad_qkv, grad_out, grad_gate_up, grad_down, grad_gains)


def solution(mesh):
    placed = (
        P("rows", "seq", None),
        P("rows", None),
        P(("rows", "seq"), None),
        P(("rows", "seq"), None),
        P(("rows", "seq"), None),
        P(("rows", "seq"), None),
        P(),
        P("rows", "seq", None),
    )
    return jax.shard_map(
        per_device,
        mesh=mesh,
        in_specs=placed,
        out_specs=(
            P("rows", "seq", None),
            P("rows", "seq", None),
            P(("rows", "seq"), None),
            P(("rows", "seq"), None),
            P(("rows", "seq"), None),
            P(("rows", "seq"), None),
            P(),
        ),
        check_vma=False,
    )
```

profile of v0, /device:TPU:0, one launch (start us, length us, event | category | flops | bytes accessed | tf_op | source)
XLA Modules:
  0.0 3683.9 jit_solution(11323167887761450375)
XLA Ops:
  11.7 156.0 %all-gather.5.cloned.1.call-done = bf16[2048,6144]{1,0:T(8,128)(2,1)} async-done(((bf16[64,6144]{1,0:T(8,128)(2,1)}), bf16[2048,6144]{1,0:T(8,128)(2,1)}) %all-gather.5.cloned.1.call-update) | async-done | bytes 25165840 | tf_op jit(solution)/shard_map/all_gather | solution.py:61
  167.7 11.6 fusion.39
  205.3 22.0 all_to_all.102
  237.1 11.9 all-to-all-done.2
  275.4 18.4 all_to_all.103
  302.0 308.2 %all-gather.9.cloned.1.call-done = bf16[2048,16384]{1,0:T(8,128)(2,1)} async-done(((bf16[64,16384]{1,0:T(8,128)(2,1)}), bf16[2048,16384]{1,0:T(8,128)(2,1)}) %all-gather.9.cloned.1.call-update) | async-done | bytes 67108880 | tf_op jit(solution)/shard_map/all_gather | solution.py:63
  610.3 32.9 fusion.57
  652.0 153.3 %all-gather.11.cloned.1.call-done = bf16[8192,2048]{1,0:T(8,128)(2,1)} async-done(((bf16[256,2048]{1,0:T(8,128)(2,1)}), bf16[8192,2048]{1,0:T(8,128)(2,1)}) %all-gather.11.cloned.1.call-update) | async-done | bytes 33554448 | tf_op jit(solution)/shard_map/all_gather | solution.py:64
  805.3 16.4 multiply_reduce_fusion.7
  823.1 23.0 multiply_convert_fusion.2
  846.0 30.6 multiply_reduce_fusion.1
  902.8 26.0 all-to-all-done.4
  958.9 12.0 multiply_convert_fusion
  993.1 17.6 all-to-all-done.5
  1028.5 13.9 all-to-all-done.6
  1065.8 21.9 convolution_bitcast_fusion
  1087.6 49.1 %copy.144 = f32[2048,6144]{1,0:T(8,128)} copy(f32[2048,6144]{0,1:T(8,128)} %convolution_bitcast_fusion) | data formatting | bytes 100663296
  1137.9 40.9 %fusion.49 = f32[8192,2048]{1,0:T(8,128)} fusion(bf16[256,8192]{1,0:T(8,128)(2,1)} %multiply_convert_fusion.3, f32[256,2048]{1,0:T(8,128)S(1)} %get-tuple-element.94, bf16[1,256,2048]{2,1,0:T(8,128)(2,1)S(1)} %copy-done.16, f32[256]{0:T(256)S(1)} %copy-done.47, f32[256]{0:T(256)S(1)} %copy-done.45, f32[2048]{0:T(1024)S(1)} %bitcast.193, ...), kind=kOutput, calls=%fused_computation.120 | convolution fusion | flops 8593604608 | bytes 74460160 | tf_op jit(solution)/shard_map/dot_general | solution.py:47
  1180.1 58.0 %fusion.7 = f32[2048,16384]{1,0:T(8,128)} fusion(bf16[256,2048]{1,0:T(8,128)(2,1)S(1)} %copy-done.13, bf16[256,8192]{1,0:T(8,128)(2,1)} %get-tuple-element.57, bf16[256,8192]{1,0:T(8,128)(2,1)} %get-tuple-element.56), kind=kOutput, calls=%fused_computation.18 | convolution fusion | flops 17196646400 | bytes 143654912 | tf_op jit(solution)/shard_map/dot_general | solution.py:47
  1238.9 43.9 %psum.7 = f32[4,2048]{1,0:T(4,128)} all-reduce(f32[4,2048]{1,0:T(4,128)S(1)} %pad_maximum_fusion.11), channel_id=1, replica_groups=mesh['rows'=8,'seq'=4] {'rows','seq'}, use_global_device_ids=true, to_apply=%region_22.23 | all-reduce | flops 8192 | bytes 65536 | tf_op jit(solution)/shard_map/psum | solution.py:206
  1282.8 14.8 fusion.10
  1297.6 269.0 %reduce-scatter.14.cloned.1.call-done = f32[64,6144]{1,0:T(8,128)} async-done(((f32[2048,6144]{1,0:T(8,128)}), f32[64,6144]{1,0:T(8,128)}) %reduce-scatter.14.cloned.1.call-update) | async-done | bytes 1572880
  1566.6 704.5 %reduce-scatter.12.cloned.1.call-done = f32[256,2048]{1,0:T(8,128)} async-done(((f32[8192,2048]{1,0:T(8,128)}), f32[256,2048]{1,0:T(8,128)}) %reduce-scatter.12.cloned.1.call-update) | async-done | bytes 2097168 | tf_op jit(solution)/shard_map/reduce_scatter | solution.py:202
  2271.1 1405.5 %reduce-scatter.16.cloned.1.call-done = f32[64,16384]{1,0:T(8,128)} async-done(((f32[2048,16384]{1,0:T(8,128)}), f32[64,16384]{1,0:T(8,128)}) %reduce-scatter.16.cloned.1.call-update) | async-done | bytes 4194320
  (207 shorter events, 207.1 us)
Async XLA Ops:
  7.2 160.5 %all-gather.5.cloned.1.call-start = ((), (), s32[]{:S(2)}) async-start(), calls=%async_computation.12 | async-start | bytes 25952256 | tf_op jit(solution)/shard_map/all_gather | solution.py:61
  7.9 159.8 %copy-start.8 = (bf16[1,256,2048]{2,1,0:T(8,128)(2,1)S(1)}, bf16[1,256,2048]{2,1,0:T(8,128)(2,1)}, u32[]{:S(2)}) copy-start(bf16[1,256,2048]{2,1,0:T(8,128)(2,1)} %param.8) | copy-start | bytes 3145732
  7.9 286.5 %all-gather.7.cloned.1.call-start = ((), (), s32[]{:S(2)}) async-start(), calls=%async_computation.13 | async-start | bytes 8650752 | tf_op jit(solution)/shard_map/all_gather | solution.py:62
  8.7 601.6 %all-gather.9.cloned.1.call-start = ((), (), s32[]{:S(2)}) async-start(), calls=%async_computation.14 | async-start | bytes 69206016 | tf_op jit(solution)/shard_map/all_gather | solution.py:63
  9.4 795.9 %all-gather.11.cloned.1.call-start = ((), (), s32[]{:S(2)}) async-start(), calls=%async_computation.15 | async-start | bytes 34603008 | tf_op jit(solution)/shard_map/all_gather | solution.py:64
  11.6 185.1 %copy-start.24 = (f32[256,128]{1,0:T(8,128)}, f32[256,128]{1,0:T(8,128)S(1)}, u32[]{:S(2)}) copy-start(f32[256,128]{1,0:T(8,128)S(1)} %get-tuple-element.76) | copy-start | bytes 393220
  11.6 178.6 %copy-start.29 = (f32[1,2048]{1,0:T(1,128)}, f32[1,2048]{1,0:T(1,128)S(1)}, u32[]{:S(2)}) copy-start(f32[1,2048]{1,0:T(1,128)S(1)} %get-tuple-element.78) | copy-start | bytes 24580
  11.6 178.6 %copy-start.31 = (f32[1,2048]{1,0:T(1,128)}, f32[1,2048]{1,0:T(1,128)S(1)}, u32[]{:S(2)}) copy-start(f32[1,2048]{1,0:T(1,128)S(1)} %get-tuple-element.79) | copy-start | bytes 24580
  183.6 21.7 all-to-all-start
  227.4 21.7 all-to-all-start.2
  231.6 1066.0 %reduce-scatter.10.cloned.1.call-start = ((), (), s32[]{:S(2)}) async-start(), calls=%async_computation.16 | async-start | bytes 17301504 | tf_op jit(solution)/shard_map/reduce_scatter | solution.py:196
  302.0 341.2 %copy-start.12 = (bf16[256,2048]{1,0:T(8,128)(2,1)}, bf16[256,2048]{1,0:T(8,128)(2,1)S(1)}, u32[]{:S(2)}) copy-start(bf16[256,2048]{1,0:T(8,128)(2,1)S(1)} %fusion.35) | copy-start | bytes 3145732
  821.8 24.3 copy-start.44
  823.1 23.0 copy-start.46
  899.0 29.7 all-to-all-start.4
  943.2 35.8 all-to-all-start.7
  979.1 31.7 all-to-all-start.5
  1010.8 31.7 all-to-all-start.6
  1014.3 552.3 %reduce-scatter.14.cloned.1.call-start = ((), (), s32[]{:S(2)}) async-start(), calls=%async_computation.18 | async-start | bytes 51904512
  1136.7 1134.4 %reduce-scatter.12.cloned.1.call-start = ((), (), s32[]{:S(2)}) async-start(), calls=%async_computation.17 | async-start | bytes 69206016 | tf_op jit(solution)/shard_map/reduce_scatter | solution.py:202
  1178.8 2497.8 %reduce-scatter.16.cloned.1.call-start = ((), (), s32[]{:S(2)}) async-start(), calls=%async_computation.19 | async-start | bytes 138412032
  1238.2 44.6 %copy-start.14 = (bf16[256,2048]{1,0:T(8,128)(2,1)S(1)}, bf16[256,2048]{1,0:T(8,128)(2,1)}, u32[]{:S(2)}) copy-start(bf16[256,2048]{1,0:T(8,128)(2,1)} %convert_element_type.243) | copy-start | bytes 3145732
  1238.2 44.6 %copy-start.17 = (bf16[256,2048]{1,0:T(8,128)(2,1)S(1)}, bf16[256,2048]{1,0:T(8,128)(2,1)}, u32[]{:S(2)}) copy-start(bf16[256,2048]{1,0:T(8,128)(2,1)} %get-tuple-element.58) | copy-start | bytes 3145732
  1238.2 44.6 %copy-start.18 = (bf16[256,2048]{1,0:T(8,128)(2,1)S(1)}, bf16[256,2048]{1,0:T(8,128)(2,1)}, u32[]{:S(2)}) copy-start(bf16[256,2048]{1,0:T(8,128)(2,1)} %get-tuple-element.59) | copy-start | bytes 3145732
  (43 other events, 192.8 us)
Sparse Core Ops, SparseCore 0:
  10.9 156.7 all-gather.4
  170.5 82.4 all-gather.6
  255.9 354.2 all-gather.8
  613.0 192.3 all-gather.10
  890.4 228.0 reduce-scatter.9
  1136.8 429.7 reduce-scatter.13
  1569.5 701.5 reduce-scatter.11
  2274.1 1402.4 reduce-scatter.15
where the time goes:
time: 3700 us; the launch traced here: 3680 us
  waiting for transfers between devices  3070 us (83%)
  matrix products  316 us (9%)
  local copies, waits for them, and re-layouts  104 us (3%)
  blocking collectives  84.3 us (2%)
  other arithmetic  66 us (2%)
    unnamed x10, waiting for transfers between devices  1680 us
    reduce_scatter x1, waiting for transfers between devices, per_device(): lax.psum_scatter(make_term(inner, grad_branch2), ('rows', 'seq'), scatter...  705 us
    all_gather x1, waiting for transfers between devices, per_device(): lax.all_gather(weight_set[2], ('rows', 'seq'), axis=0, tiled=True)  308 us
    all_gather x1, waiting for transfers between devices, per_device(): lax.all_gather(weight_set[0], ('rows', 'seq'), axis=0, tiled=True)  156 us
    all_gather x1, waiting for transfers between devices, per_device(): lax.all_gather(weight_set[3], ('rows', 'seq'), axis=0, tiled=True)  153 us
    dot_general x4, matrix products, make_term(): lax.dot_general(left_side, right_side, (((0,), (0,)), ((), ())), preferre...  129 us
    dot_general x4, matrix products, back_product(): lax.dot_general(left_side, right_side, (((1,), (1,)), ((), ())), preferre...  74.4 us
  transfers between devices with their start and end apart: 14, of which 11 were waited for; matrix products, arithmetic and copies ran while one was open for 10% of the time, Pallas kernels for 0%

commit v1 on v0

v1 whole, which is shorter than its diff:
```python
import jax
import jax.numpy as jnp
from jax import lax
from jax.sharding import PartitionSpec as P

HD = 128
BF = jnp.bfloat16
F32 = jnp.float32

eps = 1e-06
rope_base = 500000.0


def rope_tables(positions):
    half_width = HD // 2
    frequency = jnp.power(rope_base, -(jnp.arange(half_width, dtype=F32) * 2.0) / HD)
    angles = positions.astype(F32)[:, None] * frequency
    angles = jnp.concatenate([angles, angles], axis=-1)
    return jnp.cos(angles)[:, None, :], jnp.sin(angles)[:, None, :]


def rotate(tensor, cosine, sine_table, turn_sign):
    half_width = HD // 2
    turned = jnp.concatenate([-tensor[..., half_width:], tensor[..., :half_width]], axis=-1)
    return tensor * cosine + turn_sign * turned * sine_table


def dot_nn(a, b):
    return lax.dot_general(a, b, (((1,), (0,)), ((), ())), preferred_element_type=F32)


def dot_nt(a, b):
    return lax.dot_general(a, b, (((1,), (1,)), ((), ())), preferred_element_type=F32)


def dot_tn(a, b):
    return lax.dot_general(a, b, (((0,), (0,)), ((), ())), preferred_element_type=F32)


def pick(array, index):
    return lax.dynamic_index_in_dim(array, index, 0, keepdims=False)


def after(value, *others):
    return lax.optimization_barrier((value,) + others)[0]


def norm_back(tensor, inv_scale, gain_row, upstream):
    scaled = upstream * gain_row
    average = jnp.mean(scaled * tensor, axis=-1, keepdims=True)
    grad_tensor = inv_scale * scaled - tensor * (inv_scale * inv_scale * inv_scale) * average
    gain_term = jnp.sum(upstream * tensor * inv_scale, axis=0)
    return grad_tensor, gain_term


class Comm:
    def __init__(self):
        self.rows = lax.axis_size("rows")
        self.seq = lax.axis_size("seq")
        self.zc = 4 if self.rows % 4 == 0 else self.rows
        self.xc = self.rows // self.zc
        row = lax.axis_index("rows")
        self.z, self.x = row // self.xc, row % self.xc
        self.s = lax.axis_index("seq")
        zc, xc = self.zc, self.xc
        self.zperm = [(z * xc + x, ((z + 1) % zc) * xc + x) for z in range(zc) for x in range(xc)]
        self.xperm = [(z * xc + x, z * xc + (x + 1) % xc) for z in range(zc) for x in range(xc)]

    def ring_z(self, v):
        return lax.ppermute(v, "rows", self.zperm)

    def ring_x(self, v):
        return lax.ppermute(v, "rows", self.xperm) if self.xc > 1 else v

    def swap_s(self, v, j):
        return lax.ppermute(v, "seq", [(i, i ^ j) for i in range(self.seq)])

    def zi(self, j):
        return (self.z + (self.zc - j)) % self.zc

    def xi(self, j):
        return (self.x + (self.xc - j % self.xc)) % self.xc

    def gather(self, block, x_first=False):
        n, m = block.shape
        full = jnp.zeros((self.zc, self.xc, n, m), block.dtype)

        def put(full, v, j, i):
            return lax.dynamic_update_slice(full, v[None, None], (self.zi(j), self.xi(i), 0, 0))

        zs = []
        if x_first:
            line = [block]
            for _ in range(self.xc - 1):
                line.append(self.ring_x(line[-1]))
            for j in range(self.zc):
                for i in range(self.xc):
                    full = put(full, line[i], j, i)
                if j < self.zc - 1:
                    line = [self.ring_z(v) for v in line]
                    zs.append(line[0])
        else:
            v = block
            for j in range(self.zc):
                u = v
                for i in range(self.xc):
                    full = put(full, u, j, i)
                    if i < self.xc - 1:
                        u = self.ring_x(u)
                if j < self.zc - 1:
                    v = self.ring_z(v)
                    zs.append(v)
        return full, zs

    def scatter(self, parts, z_first=False):
        zc, xc = self.zc, self.xc

        def add(moved, own):
            return moved.astype(F32) + own.astype(F32)

        if z_first:
            run = pick(parts, self.zi(1))
            for t in range(2, zc + 1):
                run = add(self.ring_z(run.astype(BF)), pick(parts, self.zi(t)))
            line = run
            run = pick(line, self.xi(1))
            for i in range(2, xc + 1):
                run = add(self.ring_x(run.astype(BF)), pick(line, self.xi(i)))
            return run

        def along_x(t):
            plane = pick(parts, self.zi(t))
            run = pick(plane, self.xi(1))
            for i in range(2, xc + 1):
                run = add(self.ring_x(run.astype(BF)), pick(plane, self.xi(i)))
            return run

        run = along_x(1)
        for t in range(2, zc + 1):
            run = add(self.ring_z(run.astype(BF)), along_x(t))
        return run

    def swap_tokens(self, v, j, axis=0):
        pieces = jnp.split(self.swap_s(v, j), self.seq, axis=axis)
        return jnp.concatenate([pieces[k ^ j] for k in range(self.seq)], axis=axis)

    def exchange(self, parts, tokens=False):
        swap = self.swap_tokens if tokens else self.swap_s
        out = parts
        for j in range(1, self.seq):
            moved = swap(pick(parts, self.s ^ j), j)
            out = lax.dynamic_update_index_in_dim(out, moved, self.s ^ j, 0)
        return out

    def gather_tokens(self, v):
        pieces = [v]
        bit = self.seq // 2
        got = {0: v}
        while bit:
            for k in sorted(got):
                got[k | bit] = self.swap_s(got[k], bit)
            bit //= 2
        return jnp.concatenate([got[k] for k in range(self.seq)], axis=0)

    def scatter_tokens(self, v):
        n = v.shape[0] // self.seq
        have = {k: v[k * n : (k + 1) * n] for k in range(self.seq)}
        bit = 1
        while bit < self.seq:
            keep = {k: have[k] for k in have if not k & bit}
            for k in sorted(keep, reverse=True):
                keep[k] = keep[k].astype(F32) + self.swap_s(have[k | bit].astype(BF), bit).astype(F32)
            have = keep
            bit *= 2
        return have[0]

    def sum_seq(self, v):
        bit = 1
        while bit < self.seq:
            v = v + self.swap_s(v, bit)
            bit *= 2
        return v

    def sum_tokens(self, v):
        bit = 1
        while bit < self.seq:
            v = v + self.swap_tokens(v, bit, 1)
            bit *= 2
        return v

    def sum_all(self, v):
        v = self.sum_seq(v)
        bit = 1
        while bit < self.rows:
            v = v + lax.ppermute(v, "rows", [(i, i ^ bit) for i in range(self.rows)])
            bit *= 2
        return v


def per_device(layer_input, doc_lengths, w_qkv, w_out, w_gate_up, w_down, norm_gains, cotangent):
    c = Comm()
    rows, seq, s = c.rows, c.seq, c.s
    _, tl, d = layer_input.shape
    toks = tl * seq
    heads = d // HD
    hl = heads // seq
    wide = hl * HD
    n_in, n_out, n_ff = w_qkv.shape[0], w_out.shape[0], w_down.shape[0]
    ff = n_ff * rows
    flat_in = layer_input.reshape(tl, d)
    pairs = n_out * seq == 2 * HD and seq == 4 and hl == rows // 2

    if pairs:
        send_qkv = w_qkv.reshape(n_in, 3, 2, hl, 2, HD).transpose(4, 2, 0, 1, 3, 5)
    else:
        send_qkv = w_qkv.reshape(n_in, 3, seq, wide).transpose(2, 0, 1, 3)
    slab_qkv = c.exchange(send_qkv.reshape(seq, n_in, 3 * wide)).reshape(seq * n_in, 3 * wide)
    send_gu = w_gate_up.reshape(n_in, 2, rows, seq, n_ff).transpose(3, 0, 1, 2, 4)
    slab_gu = c.exchange(send_gu.reshape(seq, n_in, 2 * ff)).reshape(seq * n_in, 2 * ff)
    x_full = c.gather_tokens(flat_in)

    full_qkv, z_qkv = c.gather(slab_qkv)
    full_qkv = full_qkv.reshape(d, 3 * wide)
    full_out, z_out = c.gather(w_out)
    full_out = full_out.reshape(wide, d)
    half = d // 2
    down_a, z_a = c.gather(after(w_down[:, :half], z_qkv[0]), True)
    full_gu, z_gu = c.gather(after(slab_gu, z_qkv[-1]))
    full_gu = full_gu.reshape(d, 2 * ff)
    down_b, z_b = c.gather(after(w_down[:, half:], z_gu[0]))
    full_down = jnp.concatenate([down_a.reshape(ff, half), down_b.reshape(ff, d - half)], axis=1)

    doc_ends = jnp.cumsum(doc_lengths, axis=1)[0]
    lengths = doc_lengths[0]
    places = jnp.concatenate(
        [(s ^ j) * tl + jnp.arange(tl, dtype=jnp.int32) for j in range(seq)]
    )
    passed = (places[:, None] >= doc_ends[None, :]).astype(jnp.int32)
    segment = jnp.sum(passed, axis=-1)
    positions = places - jnp.sum(passed * lengths[None, :], axis=-1)
    cosine, sine_table = rope_tables(positions)
    allowed = (places[:, None] >= places[None, :]) & (segment[:, None] == segment[None, :])
    if pairs:
        gains4 = norm_gains.reshape(4, 2, hl, 2, HD).transpose(3, 1, 0, 2, 4).reshape(seq, 4, wide)
    else:
        gains4 = norm_gains.reshape(4, seq, wide).transpose(1, 0, 2)
    gains_own = pick(gains4, s)

    mixed = dot_nn(x_full, full_qkv)
    query_pre, key_pre = mixed[:, :wide], mixed[:, wide : 2 * wide]
    squares = jnp.stack([jnp.sum(query_pre * query_pre, -1), jnp.sum(key_pre * key_pre, -1)])
    scales = lax.rsqrt(c.sum_tokens(squares) / d + eps)
    query_scale, key_scale = scales[0][:, None], scales[1][:, None]
    shape3 = (toks, hl, HD)
    query = rotate((query_pre * query_scale * gains_own[0]).reshape(shape3), cosine, sine_table, 1.0)
    key = rotate((key_pre * key_scale * gains_own[1]).reshape(shape3), cosine, sine_table, 1.0)
    query, key = query.astype(BF), key.astype(BF)
    value = mixed[:, 2 * wide :].reshape(shape3).astype(BF)
    score_scale = 1.0 / HD**0.5
    scores = jnp.einsum("qhd,khd->hqk", query, key, preferred_element_type=F32) * score_scale
    scores = jnp.where(allowed[None], scores, -1e30)
    row_max = jnp.max(scores, axis=-1, keepdims=True)
    exponent = jnp.exp(scores - row_max)
    probs = exponent / jnp.sum(exponent, axis=-1, keepdims=True)
    probs_low = probs.astype(BF)
    attended = jnp.einsum("hqk,khd->qhd", probs_low, value, preferred_element_type=F32).astype(BF)

    def to_out(v):
        if pairs:
            core = s % 2
            v = v.reshape(toks, hl, 2, HD // 2).transpose(2, 0, 1, 3).reshape(2, toks, wide // 2)
            own, got = pick(v, core), c.swap_tokens(pick(v, 1 - core), 1)
            first = jnp.where(core == 0, own, got)
            second = jnp.where(core == 0, got, own)
            return jnp.concatenate([first, second], axis=1)
        v = v.reshape(toks, wide // (seq * n_out), seq, n_out)
        v = c.exchange(v.transpose(2, 0, 1, 3).reshape(seq, toks, wide // seq), True)
        return v.transpose(1, 0, 2).reshape(toks, wide)

    def from_out(v):
        if pairs:
            core = s % 2
            v = v.reshape(toks, 2, wide // 2).transpose(1, 0, 2)
            own, got = pick(v, core), c.swap_tokens(pick(v, 1 - core), 1)
            first = jnp.where(core == 0, own, got).reshape(toks, hl, 1, HD // 2)
            second = jnp.where(core == 0, got, own).reshape(toks, hl, 1, HD // 2)
            return jnp.concatenate([first, second], axis=2).reshape(shape3)
        v = c.exchange(v.reshape(toks, seq, wide // seq).transpose(1, 0, 2), True)
        v = v.reshape(seq, toks, wide // (seq * n_out), n_out).transpose(1, 2, 0, 3)
        return v.reshape(shape3)

    attended = to_out(attended)
    branch = c.scatter_tokens(dot_nn(attended, full_out))
    branch_scale = lax.rsqrt(jnp.mean(branch * branch, axis=-1, keepdims=True) + eps)
    hidden = flat_in.astype(F32) + branch * branch_scale * norm_gains[2]
    hidden_low = c.gather_tokens(hidden.astype(BF))

    gate_up = dot_nn(hidden_low, full_gu)
    gate, up = gate_up[:, :ff], gate_up[:, ff:]
    sig = jax.nn.sigmoid(gate)
    silu_gate = gate * sig
    inner = (silu_gate * up).astype(BF)
    branch2 = c.scatter_tokens(dot_nn(inner, full_down))
    branch2_scale = lax.rsqrt(jnp.mean(branch2 * branch2, axis=-1, keepdims=True) + eps)
    output = (hidden + branch2 * branch2_scale * norm_gains[3]).astype(BF)

    upstream = cotangent.reshape(tl, d).astype(F32)
    grad_branch2, gain_mlp = norm_back(branch2, branch2_scale, norm_gains[3], upstream)
    grad_branch2 = c.gather_tokens(grad_branch2.astype(BF))
    zx = (c.zc, c.xc)
    g_down = dot_tn(inner, grad_branch2).astype(BF)
    sum_a = c.scatter(g_down[:, :half].reshape(zx + (n_ff, half)), True)
    sum_b = c.scatter(g_down[:, half:].reshape(zx + (n_ff, d - half)))
    grad_down = jnp.concatenate([sum_a, sum_b], axis=1)
    grad_inner = dot_nt(grad_branch2, full_down)
    grad_gate = grad_inner * up * sig * (1.0 + gate * (1.0 - sig))
    grad_gu = jnp.concatenate([grad_gate, grad_inner * silu_gate], axis=1).astype(BF)
    g_gu = dot_tn(hidden_low, grad_gu).astype(BF)
    sum_gu = c.scatter(g_gu.reshape(zx + (seq * n_in, 2 * ff)))
    grad_hidden = upstream + c.scatter_tokens(dot_nt(grad_gu, full_gu))
    grad_branch, gain_attn = norm_back(branch, branch_scale, norm_gains[2], grad_hidden)
    grad_branch = c.gather_tokens(grad_branch.astype(BF))
    g_out = dot_tn(attended, grad_branch).astype(BF)
    grad_out = c.scatter(g_out.reshape(zx + (n_out, d)))
    grad_att = from_out(dot_nt(grad_branch, full_out).astype(BF))
    grad_probs = jnp.einsum("qhd,khd->hqk", grad_att, value, preferred_element_type=F32)
    grad_value = jnp.einsum("hqk,qhd->khd", probs_low, grad_att, preferred_element_type=F32)
    row_sum = jnp.sum(probs * grad_probs, axis=-1, keepdims=True)
    grad_scores = (probs * (grad_probs - row_sum)).astype(BF)
    grad_query = jnp.einsum("hqk,khd->qhd", grad_scores, key, preferred_element_type=F32)
    grad_key = jnp.einsum("hqk,qhd->khd", grad_scores, query, preferred_element_type=F32)
    grad_query = (grad_query * score_scale).astype(BF).astype(F32)
    grad_key = (grad_key * score_scale).astype(BF).astype(F32)
    e_query = rotate(grad_query, cosine, sine_table, -1.0).reshape(toks, wide)
    e_key = rotate(grad_key, cosine, sine_table, -1.0).reshape(toks, wide)
    scaled_q, scaled_k = e_query * gains_own[0], e_key * gains_own[1]
    means = c.sum_tokens(
        jnp.stack([jnp.sum(scaled_q * query_pre, -1), jnp.sum(scaled_k * key_pre, -1)])
    )
    means = means / d
    grad_qp = query_scale * scaled_q - query_pre * query_scale**3 * means[0][:, None]
    grad_kp = key_scale * scaled_k - key_pre * key_scale**3 * means[1][:, None]
    gain_query = jnp.sum(e_query * query_pre * query_scale, axis=0)
    gain_key = jnp.sum(e_key * key_pre * key_scale, axis=0)
    grad_mixed = jnp.concatenate(
        [grad_qp.astype(BF), grad_kp.astype(BF), grad_value.astype(BF).reshape(toks, wide)], axis=1
    )
    g_qkv = dot_tn(x_full, grad_mixed).astype(BF)
    sum_qkv = c.scatter(g_qkv.reshape(zx + (seq * n_in, 3 * wide)))
    grad_input = grad_hidden + c.scatter_tokens(dot_nt(grad_mixed, full_qkv))

    back_gu = c.exchange(sum_gu.astype(BF).reshape(seq, n_in, 2 * ff)).astype(F32)
    grad_gate_up = back_gu.reshape(seq, n_in, 2, rows, n_ff).transpose(1, 2, 3, 0, 4)
    back_qkv = c.exchange(sum_qkv.astype(BF).reshape(seq, n_in, 3 * wide)).astype(F32)
    if pairs:
        grad_qkv = back_qkv.reshape(2, 2, n_in, 3, hl, HD).transpose(2, 3, 1, 4, 0, 5)
    else:
        grad_qkv = back_qkv.reshape(seq, n_in, 3, wide).transpose(1, 2, 0, 3)

    own_terms = jnp.zeros((seq, 2, wide), F32)
    own_terms = lax.dynamic_update_slice(own_terms, jnp.stack([gain_query, gain_key])[None], (s, 0, 0))
    if pairs:
        own_terms = own_terms.reshape(2, 2, 2, hl, HD).transpose(2, 1, 3, 0, 4)
    else:
        own_terms = own_terms.transpose(1, 0, 2)
    terms = jnp.concatenate([own_terms.reshape(2, d), jnp.stack([gain_attn, gain_mlp])])
    grad_gains = c.sum_all(terms)

    return (
        output.reshape(layer_input.shape),
        grad_input.reshape(layer_input.shape),
        grad_qkv.reshape(w_qkv.shape),
        grad_out,
        grad_gate_up.reshape(w_gate_up.shape),
        grad_down,
        grad_gains,
    )


def solution(mesh):
    both = P(("rows", "seq"), None)
    tokens = P("rows", "seq", None)
    return jax.shard_map(
        per_device,
        mesh=mesh,
        in_specs=(tokens, P("rows", None), both, both, both, both, P(), tokens),
        out_specs=(tokens, tokens, both, both, both, both, P()),
        check_vma=False,
    )
```

time: 3700 us -> 1170 us (0.32)
  waiting for transfers between devices: 3070 us -> 663 us
  matrix products: 316 us -> 195 us
  blocking collectives: 84.3 us -> 0 us
  starting transfers between devices: 24 us -> 95.3 us
    unnamed x10 -> x0, waiting for transfers between devices: 1680 us -> none
    reduce_scatter x2 -> x0, waiting for transfers between devices: 705 us -> none  [the longest x1 705 us: per_device(): lax.psum_scatter(make_term(inner, grad_branch2), ('rows', 'seq'), scatter...]
    ppermute x0 -> x114, waiting for transfers between devices: none -> 663 us  [the longest x33 288 us: ring_z(): return lax.ppermute(v, 'rows', self.zperm)]
    all_gather x4 -> x0, waiting for transfers between devices: 618 us -> none  [the longest x1 308 us: per_device(): lax.all_gather(weight_set[2], ('rows', 'seq'), axis=0, tiled=True)]
    dot_general x18 -> x17, matrix products: 316 us -> 183 us  [the longest x4 59.8 us: dot_nt(): lax.dot_general(a, b, (((1,), (1,)), ((), ())), preferred_element_type=F32)]
    ppermute x0 -> x114, starting transfers between devices: none -> 95.3 us  [the longest x34 44.4 us: ring_x(): return lax.ppermute(v, 'rows', self.xperm) if self.xc > 1 else v]
    all_to_all x6 -> x0, waiting for transfers between devices: 75.1 us -> none  [the longest x1 26 us: per_device(): lax.all_to_all(grad_attended, 'seq', split_axis=2, concat_axis=1, tiled=T...]
    unnamed x112 -> x151, local copies, waits for them, and re-layouts: 68 us -> 7.43 us
  transfers between devices with their start and end apart: 14 -> 114, of which waited for: 11 -> 49; matrix products, arithmetic and copies ran while one was open for 10% -> 25% of each run, Pallas kernels for 0% -> 0%
where the time goes in v1:
time: 1170 us; the launch traced here: 1160 us
  waiting for transfers between devices  663 us (57%)
  matrix products  195 us (17%)
  local copies, waits for them, and re-layouts  117 us (10%)
  starting transfers between devices  95.3 us (8%)
  other arithmetic  85.7 us (7%)
    ppermute x33, waiting for transfers between devices, ring_z(): return lax.ppermute(v, 'rows', self.zperm)  288 us
    ppermute x34, waiting for transfers between devices, ring_x(): return lax.ppermute(v, 'rows', self.xperm) if self.xc > 1 else v  279 us
    ppermute x44, waiting for transfers between devices, swap_s(): return lax.ppermute(v, 'seq', [(i, i ^ j) for i in range(self.seq)])  93.8 us
    dot_general x4, matrix products, dot_nt(): lax.dot_general(a, b, (((1,), (1,)), ((), ())), preferred_element_type=F32)  59.8 us
    dot_general x4, matrix products, dot_tn(): lax.dot_general(a, b, (((0,), (0,)), ((), ())), preferred_element_type=F32)  46.3 us
    dot_general x4, matrix products, dot_nn(): lax.dot_general(a, b, (((1,), (0,)), ((), ())), preferred_element_type=F32)  45.8 us
    ppermute x34, starting transfers between devices, ring_x(): return lax.ppermute(v, 'rows', self.xperm) if self.xc > 1 else v  44.4 us
    ppermute x33, starting transfers between devices, ring_z(): return lax.ppermute(v, 'rows', self.zperm)  34 us
  transfers between devices with their start and end apart: 114, of which 49 were waited for; matrix products, arithmetic and copies ran while one was open for 25% of the time, Pallas kernels for 0%

profile of v1, /device:TPU:0, one launch (start us, length us, event | category | flops | bytes accessed | tf_op | source)
XLA Modules:
  0.0 1159.0 jit_solution(5194744384762159885)
XLA Ops:
  36.7 14.0 %collective-permute-done.4 = bf16[64,1536]{1,0:T(8,128)(2,1)S(1)} collective-permute-done((bf16[64,1536]{1,0:T(8,128)(2,1)S(1)}, bf16[64,1536]{1,0:T(8,128)(2,1)S(1)}, u32[]{:S(2)}, u32[]{:S(2)}) %collective-permute-start.4) | collective-permute-done | bytes 196640 | tf_op jit(solution)/shard_map/ppermute | solution.py:76
  61.3 19.6 %collective-permute-done.20 = bf16[64,2048]{1,0:T(8,128)(2,1)S(1)} collective-permute-done((bf16[64,2048]{1,0:T(8,128)(2,1)S(1)}, bf16[64,2048]{1,0:T(8,128)(2,1)S(1)}, u32[]{:S(2)}, u32[]{:S(2)}) %collective-permute-start.20) | collective-permute-done | bytes 262176 | tf_op jit(solution)/shard_map/ppermute | solution.py:73
  122.8 16.7 %collective-permute-done.9 = bf16[256,1536]{1,0:T(8,128)(2,1)S(1)} collective-permute-done((bf16[256,1536]{1,0:T(8,128)(2,1)S(1)}, bf16[256,1536]{1,0:T(8,128)(2,1)S(1)}, u32[]{:S(2)}, u32[]{:S(2)}) %collective-permute-start.9) | collective-permute-done | bytes 786464 | tf_op jit(solution)/shard_map/ppermute | solution.py:70
  162.1 16.7 %collective-permute-done.11 = bf16[256,1536]{1,0:T(8,128)(2,1)S(1)} collective-permute-done((bf16[256,1536]{1,0:T(8,128)(2,1)S(1)}, bf16[256,1536]{1,0:T(8,128)(2,1)S(1)}, u32[]{:S(2)}, u32[]{:S(2)}) %collective-permute-start.11) | collective-permute-done | bytes 786464 | tf_op jit(solution)/shard_map/ppermute | solution.py:70
  180.8 15.6 %collective-permute-done.12 = bf16[256,1536]{1,0:T(8,128)(2,1)S(1)} collective-permute-done((bf16[256,1536]{1,0:T(8,128)(2,1)S(1)}, bf16[256,1536]{1,0:T(8,128)(2,1)S(1)}, u32[]{:S(2)}, u32[]{:S(2)}) %collective-permute-start.12) | collective-permute-done | bytes 786464 | tf_op jit(solution)/shard_map/ppermute | solution.py:73
  254.4 13.8 %collective-permute-done.45 = bf16[256,1024]{1,0:T(8,128)(2,1)} collective-permute-done((bf16[256,1024]{1,0:T(8,128)(2,1)}, bf16[256,1024]{1,0:T(8,128)(2,1)}, u32[]{:S(2)}, u32[]{:S(2)}) %collective-permute-start.45) | collective-permute-done | bytes 524320 | tf_op jit(solution)/shard_map/ppermute | solution.py:70
  304.9 42.0 %collective-permute-done.49 = bf16[256,1024]{1,0:T(8,128)(2,1)S(1)} collective-permute-done((bf16[256,1024]{1,0:T(8,128)(2,1)S(1)}, bf16[256,1024]{1,0:T(8,128)(2,1)S(1)}, u32[]{:S(2)}, u32[]{:S(2)}) %collective-permute-start.49) | collective-permute-done | bytes 524320 | tf_op jit(solution)/shard_map/ppermute | solution.py:70
  348.7 12.9 %collective-permute-done.51 = bf16[256,1024]{1,0:T(8,128)(2,1)S(1)} collective-permute-done((bf16[256,1024]{1,0:T(8,128)(2,1)S(1)}, bf16[256,1024]{1,0:T(8,128)(2,1)S(1)}, u32[]{:S(2)}, u32[]{:S(2)}) %collective-permute-start.51) | collective-permute-done | bytes 524320 | tf_op jit(solution)/shard_map/ppermute | solution.py:70
  377.0 32.8 %collective-permute-done.37 = bf16[256,4096]{1,0:T(8,128)(2,1)S(1)} collective-permute-done((bf16[256,4096]{1,0:T(8,128)(2,1)S(1)}, bf16[256,4096]{1,0:T(8,128)(2,1)S(1)}, u32[]{:S(2)}, u32[]{:S(2)}) %collective-permute-start.37) | collective-permute-done | bytes 2097184 | tf_op jit(solution)/shard_map/ppermute | solution.py:70
  425.1 37.8 %collective-permute-done.38 = bf16[256,4096]{1,0:T(8,128)(2,1)S(1)} collective-permute-done((bf16[256,4096]{1,0:T(8,128)(2,1)S(1)}, bf16[256,4096]{1,0:T(8,128)(2,1)S(1)}, u32[]{:S(2)}, u32[]{:S(2)}) %collective-permute-start.38) | collective-permute-done | bytes 2097184 | tf_op jit(solution)/shard_map/ppermute | solution.py:73
  465.7 20.4 %fusion.75 = f32[1024,4096]{1,0:T(8,128)S(1)} fusion(bf16[2048,4096]{1,0:T(8,128)(2,1)} %bitcast.61, bf16[256,2048]{1,0:T(8,128)(2,1)S(1)} %collective-permute-done.28, bf16[256,2048]{1,0:T(8,128)(2,1)S(1)} %collective-permute-done.27, bf16[256,2048]{1,0:T(8,128)(2,1)S(1)} %collective-permute-done.26, bf16[256,2048]{1,0:T(8,128)(2,1)S(1)} %fusion.61), kind=kOutput, calls=%fused_computation.179 | convolution fusion | flops 17196646400 | bytes 37748736 | tf_op jit(solution)/shard_map/dot_general | solution.py:29
  491.9 14.4 %fusion.127 = (bf16[1024,2048]{1,0:T(8,128)(2,1)}, f32[1024,2048]{1,0:T(8,128)S(1)}) fusion(bf16[1024,2048]{1,0:T(8,128)(2,1)S(1)} %multiply_convert_fusion.3, bf16[2048,1024]{1,0:T(8,128)(2,1)} %bitcast.403, bf16[2048,1024]{1,0:T(8,128)(2,1)} %bitcast.405), kind=kOutput, calls=%fused_computation.331 | convolution fusion | flops 8608808960 | bytes 25165824 | tf_op jit(solution)/shard_map/dot_general | solution.py:29
  512.1 24.1 %collective-permute-done.55 = bf16[256,2048]{1,0:T(8,128)(2,1)S(1)} collective-permute-done((bf16[256,2048]{1,0:T(8,128)(2,1)S(1)}, bf16[256,2048]{1,0:T(8,128)(2,1)S(1)}, u32[]{:S(2)}, u32[]{:S(2)}) %collective-permute-start.55) | collective-permute-done | bytes 1048608 | tf_op jit(solution)/shard_map/ppermute | solution.py:76
  539.9 24.4 %collective-permute-done.57 = bf16[256,2048]{1,0:T(8,128)(2,1)} collective-permute-done((bf16[256,2048]{1,0:T(8,128)(2,1)}, bf16[256,2048]{1,0:T(8,128)(2,1)}, u32[]{:S(2)}, u32[]{:S(2)}) %collective-permute-start.57) | collective-permute-done | bytes 1048608 | tf_op jit(solution)/shard_map/ppermute | solution.py:76
  567.3 20.6 %multiply_convert_fusion.2 = (bf16[1024,2048]{1,0:T(8,128)(2,1)}, bf16[1024,2048]{1,0:T(8,128)(2,1)}) fusion(f32[1024,4096]{1,0:T(8,128)} %copy-done.6, bf16[2048,1024]{1,0:T(8,128)(2,1)} %bitcast.404, bf16[2048,1024]{1,0:T(8,128)(2,1)} %bitcast.406, bf16[256,2048]{1,0:T(8,128)(2,1)} %collective-permute-done.58, ...), kind=kOutput, calls=%fused_computation.10 | convolution fusion | flops 8650752000 | bytes 37748736 | tf_op jit(solution)/shard_map/dot_general | solution.py:33
  587.9 24.2 %fusion.128 = (bf16[1024,2048]{1,0:T(8,128)(2,1)S(1)}, f32[1024,2048]{1,0:T(8,128)}) fusion(bf16[2048,4096]{1,0:T(8,128)(2,1)} %bitcast.61, bf16[1024,2048]{1,0:T(8,128)(2,1)} %get-tuple-element.33, bf16[1024,2048]{1,0:T(8,128)(2,1)} %get-tuple-element.32), kind=kOutput, calls=%fused_computation.332 | convolution fusion | flops 17198743552 | bytes 37748736 | tf_op jit(solution)/shard_map/dot_general | solution.py:33
  631.8 24.1 %convolution_convert_fusion = bf16[2048,4096]{1,0:T(8,128)(2,1)} fusion(bf16[1024,2048]{1,0:T(8,128)(2,1)} %get-tuple-element.33, bf16[1024,2048]{1,0:T(8,128)(2,1)} %get-tuple-element.32, bf16[256,2048]{1,0:T(8,128)(2,1)} %copy-done.70, bf16[256,2048]{1,0:T(8,128)(2,1)} %copy-done.68, bf16[256,2048]{1,0:T(8,128)(2,1)} %copy-done.69, ...), kind=kOutput, calls=%fused_computation.5 | convolution fusion | flops 17221812224 | bytes 29360128 | tf_op jit(solution)/shard_map/dot_general | solution.py:37
  676.6 18.2 %collective-permute-done.99 = bf16[2,256,1024]{2,1,0:T(8,128)(2,1)S(1)} collective-permute-done((bf16[2,256,1024]{2,1,0:T(8,128)(2,1)S(1)}, bf16[2,256,1024]{2,1,0:T(8,128)(2,1)S(1)}, u32[]{:S(2)}, u32[]{:S(2)}) %collective-permute-start.99) | collective-permute-done | bytes 1048608 | tf_op jit(solution)/shard_map/ppermute | solution.py:70
  712.0 22.1 %collective-permute-done.100 = bf16[2,256,1024]{2,1,0:T(8,128)(2,1)S(1)} collective-permute-done((bf16[2,256,1024]{2,1,0:T(8,128)(2,1)S(1)}, bf16[2,256,1024]{2,1,0:T(8,128)(2,1)S(1)}, u32[]{:S(2)}, u32[]{:S(2)}) %collective-permute-start.100) | collective-permute-done | bytes 1048608 | tf_op jit(solution)/shard_map/ppermute | solution.py:70
  768.2 30.2 %collective-permute-done.90 = bf16[256,4096]{1,0:T(8,128)(2,1)S(1)} collective-permute-done((bf16[256,4096]{1,0:T(8,128)(2,1)}, bf16[256,4096]{1,0:T(8,128)(2,1)S(1)}, u32[]{:S(2)}, u32[]{:S(2)}) %collective-permute-start.90) | collective-permute-done | bytes 2097184 | tf_op jit(solution)/shard_map/ppermute | solution.py:73
  806.3 42.7 %collective-permute-done.81 = bf16[64,2048]{1,0:T(8,128)(2,1)S(1)} collective-permute-done((bf16[64,2048]{1,0:T(8,128)(2,1)S(1)}, bf16[64,2048]{1,0:T(8,128)(2,1)S(1)}, u32[]{:S(2)}, u32[]{:S(2)}) %collective-permute-start.81) | collective-permute-done | bytes 262176 | tf_op jit(solution)/shard_map/ppermute | solution.py:73
  960.7 12.2 %collective-permute-done.73 = bf16[256,1536]{1,0:T(8,128)(2,1)S(1)} collective-permute-done((bf16[256,1536]{1,0:T(8,128)(2,1)}, bf16[256,1536]{1,0:T(8,128)(2,1)S(1)}, u32[]{:S(2)}, u32[]{:S(2)}) %collective-permute-start.73) | collective-permute-done | bytes 786464 | tf_op jit(solution)/shard_map/ppermute | solution.py:73
  980.0 57.6 %collective-permute-done.75 = bf16[256,1536]{1,0:T(8,128)(2,1)S(1)} collective-permute-done((bf16[256,1536]{1,0:T(8,128)(2,1)S(1)}, bf16[256,1536]{1,0:T(8,128)(2,1)S(1)}, u32[]{:S(2)}, u32[]{:S(2)}) %collective-permute-start.75) | collective-permute-done | bytes 786464 | tf_op jit(solution)/shard_map/ppermute | solution.py:73
  1057.8 49.0 %collective-permute-done.76 = bf16[256,1536]{1,0:T(8,128)(2,1)S(1)} collective-permute-done((bf16[256,1536]{1,0:T(8,128)(2,1)S(1)}, bf16[256,1536]{1,0:T(8,128)(2,1)S(1)}, u32[]{:S(2)}, u32[]{:S(2)}) %collective-permute-start.76) | collective-permute-done | bytes 786464 | tf_op jit(solution)/shard_map/ppermute | solution.py:70
  (562 shorter events, 549.7 us)
Async XLA Ops:
  20.3 120.9 %collective-permute-start.1 = (bf16[256,2048]{1,0:T(8,128)(2,1)}, bf16[256,2048]{1,0:T(8,128)(2,1)}, u32[]{:S(2)}, u32[]{:S(2)}) collective-permute-start(bf16[256,2048]{1,0:T(8,128)(2,1)} %bitcast.399), channel_id=1, source_target_pairs={{0,2},{1,3},{2,0},{3,1},{4,6},{5,7},{6,4},{7,5},{8,10},{9,11},{10,... | collective-permute-start | bytes 3145736 | tf_op jit(solution)/shard_map/ppermute | solution.py:76
  178.9 73.7 %collective-permute-start.44 = (bf16[256,1024]{1,0:T(8,128)(2,1)}, bf16[256,1024]{1,0:T(8,128)(2,1)}, u32[]{:S(2)}, u32[]{:S(2)}) collective-permute-start(bf16[256,1024]{1,0:T(8,128)(2,1)} %collective-permute-done.42), channel_id=1, source_target_pairs={{0,8},{4,12},{8,16},{12,20},{16,24},{20,28},{24,0},{28,4},{1,9},{5... | collective-permute-start | bytes 1572872 | tf_op jit(solution)/shard_map/ppermute | solution.py:70
  207.2 66.5 %collective-permute-start.33 = (bf16[256,4096]{1,0:T(8,128)(2,1)}, bf16[256,4096]{1,0:T(8,128)(2,1)}, u32[]{:S(2)}, u32[]{:S(2)}) collective-permute-start(bf16[256,4096]{1,0:T(8,128)(2,1)} %bitcast.52), channel_id=1, source_target_pairs={{0,8},{4,12},{8,16},{12,20},{16,24},{20,28},{24,0},{28,4},{1,9},{5... | collective-permute-start | bytes 6291464 | tf_op jit(solution)/shard_map/ppermute | solution.py:70
  207.3 68.2 %collective-permute-start.32 = (bf16[256,4096]{1,0:T(8,128)(2,1)}, bf16[256,4096]{1,0:T(8,128)(2,1)}, u32[]{:S(2)}, u32[]{:S(2)}) collective-permute-start(bf16[256,4096]{1,0:T(8,128)(2,1)} %bitcast.52), channel_id=1, source_target_pairs={{0,4},{4,0},{8,12},{12,8},{16,20},{20,16},{24,28},{28,24},{1,5},{5... | collective-permute-start | bytes 6291464 | tf_op jit(solution)/shard_map/ppermute | solution.py:73
  273.2 74.2 %collective-permute-start.23 = (bf16[256,2048]{1,0:T(8,128)(2,1)S(1)}, bf16[256,2048]{1,0:T(8,128)(2,1)S(1)}, u32[]{:S(2)}, u32[]{:S(2)}) collective-permute-start(bf16[256,2048]{1,0:T(8,128)(2,1)S(1)} %get-tuple-element.58), channel_id=1, source_target_pairs={{0,1},{1,0},{2,3},{3,2},{4,5},{5,4},{6,7},{7,6},{8,9},{9,8},{10,11... | collective-permute-start | bytes 3145736 | tf_op jit(solution)/shard_map/ppermute | solution.py:76
  275.4 87.7 %collective-permute-start.35 = (bf16[256,4096]{1,0:T(8,128)(2,1)}, bf16[256,4096]{1,0:T(8,128)(2,1)S(1)}, u32[]{:S(2)}, u32[]{:S(2)}) collective-permute-start(bf16[256,4096]{1,0:T(8,128)(2,1)} %collective-permute-done.33), channel_id=1, source_target_pairs={{0,8},{4,12},{8,16},{12,20},{16,24},{20,28},{24,0},{28,4},{1,9},{5... | collective-permute-start | bytes 6291464 | tf_op jit(solution)/shard_map/ppermute | solution.py:70
  282.3 65.2 %collective-permute-start.25 = (bf16[256,2048]{1,0:T(8,128)(2,1)S(1)}, bf16[256,2048]{1,0:T(8,128)(2,1)S(1)}, u32[]{:S(2)}, u32[]{:S(2)}) collective-permute-start(bf16[256,2048]{1,0:T(8,128)(2,1)S(1)} %fusion.35), channel_id=1, source_target_pairs={{0,2},{1,3},{2,0},{3,1},{4,6},{5,7},{6,4},{7,5},{8,10},{9,11},{10,... | collective-permute-start | bytes 3145736 | tf_op jit(solution)/shard_map/ppermute | solution.py:76
  303.3 72.0 %collective-permute-start.34 = (bf16[256,4096]{1,0:T(8,128)(2,1)}, bf16[256,4096]{1,0:T(8,128)(2,1)S(1)}, u32[]{:S(2)}, u32[]{:S(2)}) collective-permute-start(bf16[256,4096]{1,0:T(8,128)(2,1)} %collective-permute-done.33), channel_id=1, source_target_pairs={{0,4},{4,0},{8,12},{12,8},{16,20},{20,16},{24,28},{28,24},{1,5},{5... | collective-permute-start | bytes 6291464 | tf_op jit(solution)/shard_map/ppermute | solution.py:73
  363.6 100.8 %collective-permute-start.26 = (bf16[256,2048]{1,0:T(8,128)(2,1)S(1)}, bf16[256,2048]{1,0:T(8,128)(2,1)S(1)}, u32[]{:S(2)}, u32[]{:S(2)}) collective-permute-start(bf16[256,2048]{1,0:T(8,128)(2,1)S(1)} %fusion.61), channel_id=1, source_target_pairs={{0,1},{1,0},{2,3},{3,2},{4,5},{5,4},{6,7},{7,6},{8,9},{9,8},{10,11... | collective-permute-start | bytes 3145736 | tf_op jit(solution)/shard_map/ppermute | solution.py:76
  613.7 81.8 %collective-permute-start.59 = (bf16[256,2048]{1,0:T(8,128)(2,1)}, bf16[256,2048]{1,0:T(8,128)(2,1)}, u32[]{:S(2)}, u32[]{:S(2)}) collective-permute-start(bf16[256,2048]{1,0:T(8,128)(2,1)} %get-tuple-element.54), channel_id=1, source_target_pairs={{0,1},{1,0},{2,3},{3,2},{4,5},{5,4},{6,7},{7,6},{8,9},{9,8},{10,11... | collective-permute-start | bytes 3145736 | tf_op jit(solution)/shard_map/ppermute | solution.py:76
  673.8 60.8 %collective-permute-start.88 = (bf16[256,4096]{1,0:T(8,128)(2,1)S(1)}, bf16[256,4096]{1,0:T(8,128)(2,1)S(1)}, u32[]{:S(2)}, u32[]{:S(2)}) collective-permute-start(bf16[256,4096]{1,0:T(8,128)(2,1)S(1)} %get-tuple-element.34), channel_id=1, source_target_pairs={{0,4},{4,0},{8,12},{12,8},{16,20},{20,16},{24,28},{28,24},{1,5},{5... | collective-permute-start | bytes 6291464 | tf_op jit(solution)/shard_map/ppermute | solution.py:73
  743.8 232.0 %collective-permute-start.92 = (bf16[256,4096]{1,0:T(8,128)(2,1)}, bf16[256,4096]{1,0:T(8,128)(2,1)}, u32[]{:S(2)}, u32[]{:S(2)}) collective-permute-start(bf16[256,4096]{1,0:T(8,128)(2,1)} %get-tuple-element.36), channel_id=1, source_target_pairs={{0,4},{4,0},{8,12},{12,8},{16,20},{20,16},{24,28},{28,24},{1,5},{5... | collective-permute-start | bytes 6291464 | tf_op jit(solution)/shard_map/ppermute | solution.py:73
  762.9 88.5 %collective-permute-start.65 = (bf16[1024,256]{0,1:T(8,128)(2,1)S(1)}, bf16[1024,256]{0,1:T(8,128)(2,1)S(1)}, u32[]{:S(2)}, u32[]{:S(2)}) collective-permute-start(bf16[1024,256]{0,1:T(8,128)(2,1)S(1)} %get-tuple-element.86), channel_id=1, source_target_pairs={{0,1},{1,0},{2,3},{3,2},{4,5},{5,4},{6,7},{7,6},{8,9},{9,8},{10,11... | collective-permute-start | bytes 1572872 | tf_op jit(solution)/shard_map/ppermute | solution.py:76
  766.7 82.3 %collective-permute-start.81 = (bf16[64,2048]{1,0:T(8,128)(2,1)S(1)}, bf16[64,2048]{1,0:T(8,128)(2,1)S(1)}, u32[]{:S(2)}, u32[]{:S(2)}) collective-permute-start(bf16[64,2048]{1,0:T(8,128)(2,1)S(1)} %get-tuple-element.65), channel_id=1, source_target_pairs={{0,4},{4,0},{8,12},{12,8},{16,20},{20,16},{24,28},{28,24},{1,5},{5... | collective-permute-start | bytes 786440 | tf_op jit(solution)/shard_map/ppermute | solution.py:73
  802.6 173.4 %collective-permute-start.91 = (bf16[256,4096]{1,0:T(8,128)(2,1)}, bf16[256,4096]{1,0:T(8,128)(2,1)}, u32[]{:S(2)}, u32[]{:S(2)}) collective-permute-start(bf16[256,4096]{1,0:T(8,128)(2,1)} %fusion.14), channel_id=1, source_target_pairs={{0,8},{4,12},{8,16},{12,20},{16,24},{20,28},{24,0},{28,4},{1,9},{5... | collective-permute-start | bytes 6291464 | tf_op jit(solution)/shard_map/ppermute | solution.py:70
  804.8 99.0 %collective-permute-start.83 = (bf16[64,2048]{1,0:T(8,128)(2,1)}, bf16[64,2048]{1,0:T(8,128)(2,1)}, u32[]{:S(2)}, u32[]{:S(2)}) collective-permute-start(bf16[64,2048]{1,0:T(8,128)(2,1)} %get-tuple-element.68), channel_id=1, source_target_pairs={{0,4},{4,0},{8,12},{12,8},{16,20},{20,16},{24,28},{28,24},{1,5},{5... | collective-permute-start | bytes 786440 | tf_op jit(solution)/shard_map/ppermute | solution.py:73
  849.0 103.2 %collective-permute-start.85 = (bf16[64,2048]{1,0:T(8,128)(2,1)}, bf16[64,2048]{1,0:T(8,128)(2,1)S(1)}, u32[]{:S(2)}, u32[]{:S(2)}) collective-permute-start(bf16[64,2048]{1,0:T(8,128)(2,1)} %get-tuple-element.67), channel_id=1, source_target_pairs={{0,4},{4,0},{8,12},{12,8},{16,20},{20,16},{24,28},{28,24},{1,5},{5... | collective-permute-start | bytes 786440 | tf_op jit(solution)/shard_map/ppermute | solution.py:73
  958.1 149.2 %collective-permute-start.94 = (bf16[256,4096]{1,0:T(8,128)(2,1)S(1)}, bf16[256,4096]{1,0:T(8,128)(2,1)S(1)}, u32[]{:S(2)}, u32[]{:S(2)}) collective-permute-start(bf16[256,4096]{1,0:T(8,128)(2,1)S(1)} %copy-done.33), channel_id=1, source_target_pairs={{0,4},{4,0},{8,12},{12,8},{16,20},{20,16},{24,28},{28,24},{1,5},{5... | collective-permute-start | bytes 6291464 | tf_op jit(solution)/shard_map/ppermute | solution.py:73
  972.9 68.2 %collective-permute-start.87 = (bf16[64,2048]{1,0:T(8,128)(2,1)S(1)}, bf16[64,2048]{1,0:T(8,128)(2,1)S(1)}, u32[]{:S(2)}, u32[]{:S(2)}) collective-permute-start(bf16[64,2048]{1,0:T(8,128)(2,1)S(1)} %copy-done.44), channel_id=1, source_target_pairs={{0,4},{4,0},{8,12},{12,8},{16,20},{20,16},{24,28},{28,24},{1,5},{5... | collective-permute-start | bytes 786440 | tf_op jit(solution)/shard_map/ppermute | solution.py:73
  974.4 63.2 %collective-permute-start.75 = (bf16[256,1536]{1,0:T(8,128)(2,1)S(1)}, bf16[256,1536]{1,0:T(8,128)(2,1)S(1)}, u32[]{:S(2)}, u32[]{:S(2)}) collective-permute-start(bf16[256,1536]{1,0:T(8,128)(2,1)S(1)} %copy-done.41), channel_id=1, source_target_pairs={{0,4},{4,0},{8,12},{12,8},{16,20},{20,16},{24,28},{28,24},{1,5},{5... | collective-permute-start | bytes 2359304 | tf_op jit(solution)/shard_map/ppermute | solution.py:73
  975.9 74.7 %collective-permute-start.69 = (bf16[256,2048]{1,0:T(8,128)(2,1)S(1)}, bf16[256,2048]{1,0:T(8,128)(2,1)S(1)}, u32[]{:S(2)}, u32[]{:S(2)}) collective-permute-start(bf16[256,2048]{1,0:T(8,128)(2,1)S(1)} %get-tuple-element.53), channel_id=1, source_target_pairs={{0,1},{1,0},{2,3},{3,2},{4,5},{5,4},{6,7},{7,6},{8,9},{9,8},{10,11... | collective-permute-start | bytes 3145736 | tf_op jit(solution)/shard_map/ppermute | solution.py:76
  975.9 61.7 %collective-permute-start.74 = (bf16[256,1536]{1,0:T(8,128)(2,1)S(1)}, bf16[256,1536]{1,0:T(8,128)(2,1)S(1)}, u32[]{:S(2)}, u32[]{:S(2)}) collective-permute-start(bf16[256,1536]{1,0:T(8,128)(2,1)S(1)} %fusion.52), channel_id=1, source_target_pairs={{0,8},{4,12},{8,16},{12,20},{16,24},{20,28},{24,0},{28,4},{1,9},{5... | collective-permute-start | bytes 2359304 | tf_op jit(solution)/shard_map/ppermute | solution.py:70
  1037.6 69.7 %collective-permute-start.93 = (bf16[256,4096]{1,0:T(8,128)(2,1)S(1)}, bf16[256,4096]{1,0:T(8,128)(2,1)S(1)}, u32[]{:S(2)}, u32[]{:S(2)}) collective-permute-start(bf16[256,4096]{1,0:T(8,128)(2,1)S(1)} %fusion.12), channel_id=1, source_target_pairs={{0,8},{4,12},{8,16},{12,20},{16,24},{20,28},{24,0},{28,4},{1,9},{5... | collective-permute-start | bytes 6291464 | tf_op jit(solution)/shard_map/ppermute | solution.py:70
  1050.6 59.9 %collective-permute-start.68 = (bf16[256,2048]{1,0:T(8,128)(2,1)S(1)}, bf16[256,2048]{1,0:T(8,128)(2,1)S(1)}, u32[]{:S(2)}, u32[]{:S(2)}) collective-permute-start(bf16[256,2048]{1,0:T(8,128)(2,1)S(1)} %get-tuple-element.52), channel_id=1, source_target_pairs={{0,1},{1,0},{2,3},{3,2},{4,5},{5,4},{6,7},{7,6},{8,9},{9,8},{10,11... | collective-permute-start | bytes 3145736 | tf_op jit(solution)/shard_map/ppermute | solution.py:76
  (165 other events, 4576.0 us)

commit v2 on v1

v2 whole, which is shorter than its diff:
```python
import jax
import jax.numpy as jnp
from jax import lax
from jax.sharding import PartitionSpec as P

HD = 128
BF = jnp.bfloat16
F32 = jnp.float32

eps = 1e-06
rope_base = 500000.0


def rope_tables(positions):
    half_width = HD // 2
    frequency = jnp.power(rope_base, -(jnp.arange(half_width, dtype=F32) * 2.0) / HD)
    angles = positions.astype(F32)[:, None] * frequency
    angles = jnp.concatenate([angles, angles], axis=-1)
    return jnp.cos(angles)[:, None, :], jnp.sin(angles)[:, None, :]


def rotate(tensor, cosine, sine_table, turn_sign):
    half_width = HD // 2
    turned = jnp.concatenate([-tensor[..., half_width:], tensor[..., :half_width]], axis=-1)
    return tensor * cosine + turn_sign * turned * sine_table


def dot_nn(a, b):
    return lax.dot_general(a, b, (((1,), (0,)), ((), ())), preferred_element_type=F32)


def dot_nt(a, b):
    return lax.dot_general(a, b, (((1,), (1,)), ((), ())), preferred_element_type=F32)


def dot_tn(a, b):
    return lax.dot_general(a, b, (((0,), (0,)), ((), ())), preferred_element_type=F32)


def pick(array, index):
    return lax.dynamic_index_in_dim(array, index, 0, keepdims=False)


def after(value, *others):
    return lax.optimization_barrier((value,) + others)[0]


def norm_back(tensor, inv_scale, gain_row, upstream):
    scaled = upstream * gain_row
    average = jnp.mean(scaled * tensor, axis=-1, keepdims=True)
    grad_tensor = inv_scale * scaled - tensor * (inv_scale * inv_scale * inv_scale) * average
    gain_term = jnp.sum(upstream * tensor * inv_scale, axis=0)
    return grad_tensor, gain_term


class Comm:
    def __init__(self, group=8):
        rows, seq = lax.axis_size("rows"), lax.axis_size("seq")
        self.part = max(1, min(rows, group // seq))
        self.copies, self.size, self.count = rows // self.part, self.part * seq, rows * seq
        row, s = lax.axis_index("rows"), lax.axis_index("seq")
        self.d = row // self.part
        self.g = (row % self.part) * seq + s
        self.seq, self.t, self.s = seq, row % self.part, s
        bits = [1 << i for i in range(self.size.bit_length() - 1)]
        self.bits = bits
        self.order = list(range(0, self.size, 2)) + list(range(1, self.size, 2))

    def send(self, v, pairs):
        return lax.ppermute(v, ("rows", "seq"), pairs)

    def swap(self, v, j):
        return self.send(v, [(i, i ^ j) for i in range(self.count)])

    def ring(self, v):
        return self.send(v, [(i, (i + self.size) % self.count) for i in range(self.count)])

    def near(self, j):
        return (self.d + (self.copies - j)) % self.copies

    def gather(self, block, firsts=()):
        full = jnp.zeros((self.copies,) + block.shape, block.dtype)
        arrivals = []
        for j in range(self.copies):
            full = lax.dynamic_update_index_in_dim(full, block, self.near(j), 0)
            if j < self.copies - 1:
                if j < len(firsts):
                    block = after(block, firsts[j])
                block = self.ring(block)
                arrivals.append(block)
        return full, arrivals

    def scatter(self, parts):
        run = pick(parts, self.near(1))
        for j in range(2, self.copies + 1):
            run = self.ring(run.astype(BF)).astype(F32) + pick(parts, self.near(j)).astype(F32)
        return run

    def exchange(self, parts, tokens=False):
        swap = self.swap_tokens if tokens else self.swap
        for bit in self.bits:
            own = (self.g // bit) % 2
            shape = parts.shape
            parts = parts.reshape((self.size // (2 * bit), 2, bit) + shape[1:])
            other = lax.dynamic_index_in_dim(parts, 1 - own, 1, keepdims=False)
            axis = 2 if tokens else 0
            moved = swap(other, bit, axis) if tokens else swap(other, bit)
            parts = lax.dynamic_update_index_in_dim(parts, moved, 1 - own, 1).reshape(shape)
        return parts

    def swap_tokens(self, v, j, axis=0):
        pieces = jnp.split(self.swap(v, j), self.size, axis=axis)
        place = {k: p for p, k in enumerate(self.order)}
        return jnp.concatenate([pieces[place[k ^ j]] for k in self.order], axis=axis)

    def gather_tokens(self, v):
        got = {0: v}
        if self.size == 8:
            half = v.shape[0] // 2
            got[4], got[2] = self.swap(v, 4), self.swap(v, 2)
            got[1] = self.swap(v, 1)
            got[6] = jnp.concatenate([self.swap(got[4][:half], 2), self.swap(got[2][half:], 4)], axis=0)
            for k in (2, 4, 6):
                got[k + 1] = self.swap(got[k], 1)
        else:
            for bit in self.bits[::-1]:
                for k in sorted(got):
                    got[k | bit] = self.swap(got[k], bit)
        return jnp.concatenate([got[k] for k in self.order], axis=0)

    def scatter_tokens(self, tokens, make_dot):
        n = tokens.shape[0] // 2
        away = make_dot(tokens[n:]).astype(BF)
        m = n // (self.size // 2)
        moved = [self.swap(away[k * m : (k + 1) * m], 1) for k in range(self.size // 2)]
        kept = make_dot(tokens[:n])
        have = {2 * k: kept[k * m : (k + 1) * m] + moved[k].astype(F32) for k in range(self.size // 2)}
        if self.size == 8:
            half = m // 2
            last = have[6].astype(BF)
            four, two = self.swap(last[half:], 2), self.swap(last[:half], 4)
            mid4, mid2 = have[4].astype(BF), have[2].astype(BF)
            add4 = (have[4][half:] + four.astype(F32)).astype(BF)
            add2 = (have[2][:half] + two.astype(F32)).astype(BF)
            a = jnp.concatenate([self.swap(mid4[:half], 4), self.swap(add4, 4)], axis=0)
            b = jnp.concatenate([self.swap(add2, 2), self.swap(mid2[half:], 2)], axis=0)
            return have[0] + a.astype(F32) + b.astype(F32)
        for bit in self.bits[1:]:
            for k in [k for k in have if k & bit]:
                have[k ^ bit] = have[k ^ bit] + self.swap(have.pop(k).astype(BF), bit).astype(F32)
        return have[0]

    def sum_tokens(self, v):
        for bit in self.bits:
            v = v + self.swap_tokens(v, bit, 1)
        return v

    def sum_all(self, v):
        bit = 1
        while bit < self.count:
            v = v + self.swap(v, bit)
            bit *= 2
        return v


def per_device(layer_input, doc_lengths, w_qkv, w_out, w_gate_up, w_down, norm_gains, cotangent):
    c = Comm()
    copies, size, part = c.copies, c.size, c.part
    _, tl, d = layer_input.shape
    toks, row_len = tl * size, tl * c.seq
    heads = d // HD
    hl = heads // size
    wide = hl * HD
    n_in, n_out, n_ff = w_qkv.shape[0], w_out.shape[0], w_down.shape[0]
    chunks = 2
    piece = n_ff // chunks
    ffc = piece * copies
    flat_in = layer_input.reshape(tl, d)
    pairs = 2 * n_out == HD and 2 * hl == copies
    half_group = size // 2

    x_full = c.gather_tokens(flat_in)
    if pairs:
        send_qkv = w_qkv.reshape(n_in, 3, 2, hl, half_group, HD).transpose(4, 2, 0, 1, 3, 5)
    else:
        send_qkv = w_qkv.reshape(n_in, 3, size, wide).transpose(2, 0, 1, 3)
    slab_qkv = c.exchange(send_qkv.reshape(size, n_in, 3 * wide)).reshape(size * n_in, 3 * wide)
    send_gu = w_gate_up.reshape(n_in, 2, copies, size, chunks, piece).transpose(3, 4, 0, 1, 2, 5)
    slab_gu = c.exchange(send_gu.reshape(size, chunks, n_in, 2 * ffc))

    full_out, _ = c.gather(w_out)
    full_out = full_out.reshape(wide, d)
    full_qkv, z_qkv = c.gather(slab_qkv)
    full_qkv = full_qkv.reshape(d, 3 * wide)
    full_gu, full_down, last = [], [], z_qkv
    for k in range(chunks):
        full, last = c.gather(slab_gu[:, k].reshape(size * n_in, 2 * ffc), last[-2:])
        full_gu.append(full.reshape(d, 2 * ffc))
    for k in range(chunks):
        full, last = c.gather(w_down[k * piece : (k + 1) * piece], last[-2:])
        full_down.append(full.reshape(ffc, d))
    full_down = jnp.concatenate(full_down, axis=0)

    lengths = doc_lengths.astype(jnp.int32)
    other = [lengths]
    for j in range(1, part):
        other.append(c.swap(lengths, j * c.seq))
    lengths = jnp.concatenate(other, axis=0)
    doc_ends = jnp.cumsum(lengths, axis=1)
    near = [k % c.seq for k in c.order if k < c.seq]
    places = jnp.concatenate([(c.s ^ k) * tl + jnp.arange(tl, dtype=jnp.int32) for k in near])
    passed = (places[None, :, None] >= doc_ends[:, None, :]).astype(jnp.int32)
    segment = jnp.sum(passed, axis=-1)
    positions = places[None, :] - jnp.sum(passed * lengths[:, None, :], axis=-1)
    allowed = (places[:, None] >= places[None, :])[None] & (segment[:, :, None] == segment[:, None, :])

    def by_rows(v):
        v = v.reshape((2, part, c.seq // 2, tl) + v.shape[1:])
        return v.swapaxes(0, 1).reshape((part, row_len) + v.shape[4:])

    def by_tokens(v):
        v = v.reshape((part, 2, c.seq // 2, tl) + v.shape[2:])
        return v.swapaxes(0, 1).reshape((toks,) + v.shape[4:])

    cosine, sine_table = rope_tables(by_tokens(positions))
    if pairs:
        gains4 = norm_gains.reshape(4, 2, hl, half_group, HD).transpose(3, 1, 0, 2, 4).reshape(size, 4, wide)
    else:
        gains4 = norm_gains.reshape(4, size, wide).transpose(1, 0, 2)
    gains_own = pick(gains4, c.g)

    mixed = dot_nn(x_full, full_qkv)
    query_pre, key_pre = mixed[:, :wide], mixed[:, wide : 2 * wide]
    squares = jnp.stack([jnp.sum(query_pre * query_pre, -1), jnp.sum(key_pre * key_pre, -1)])
    scales = lax.rsqrt(c.sum_tokens(squares) / d + eps)
    query_scale, key_scale = scales[0][:, None], scales[1][:, None]
    shape3 = (toks, hl, HD)
    query = rotate((query_pre * query_scale * gains_own[0]).reshape(shape3), cosine, sine_table, 1.0)
    key = rotate((key_pre * key_scale * gains_own[1]).reshape(shape3), cosine, sine_table, 1.0)
    query, key = by_rows(query.astype(BF)), by_rows(key.astype(BF))
    value = by_rows(mixed[:, 2 * wide :].reshape(shape3).astype(BF))
    score_scale = 1.0 / HD**0.5
    scores = jnp.einsum("rqhd,rkhd->rhqk", query, key, preferred_element_type=F32) * score_scale
    scores = jnp.where(allowed[:, None], scores, -1e30)
    row_max = jnp.max(scores, axis=-1, keepdims=True)
    exponent = jnp.exp(scores - row_max)
    probs = exponent / jnp.sum(exponent, axis=-1, keepdims=True)
    probs_low = probs.astype(BF)
    attended = jnp.einsum("rhqk,rkhd->rqhd", probs_low, value, preferred_element_type=F32).astype(BF)

    def to_out(v):
        if pairs:
            core = c.g % 2
            v = v.reshape(toks, hl, 2, HD // 2).transpose(2, 0, 1, 3).reshape(2, toks, wide // 2)
            own, got = pick(v, core), c.swap_tokens(pick(v, 1 - core), 1)
            first = jnp.where(core == 0, own, got)
            second = jnp.where(core == 0, got, own)
            return jnp.concatenate([first, second], axis=1)
        v = v.reshape(toks, wide // (size * n_out), size, n_out)
        v = c.exchange(v.transpose(2, 0, 1, 3).reshape(size, toks, wide // size), True)
        return v.transpose(1, 0, 2).reshape(toks, wide)

    def from_out(v):
        if pairs:
            core = c.g % 2
            v = v.reshape(toks, 2, wide // 2).transpose(1, 0, 2)
            own, got = pick(v, core), c.swap_tokens(pick(v, 1 - core), 1)
            first = jnp.where(core == 0, own, got).reshape(toks, hl, 1, HD // 2)
            second = jnp.where(core == 0, got, own).reshape(toks, hl, 1, HD // 2)
            return jnp.concatenate([first, second], axis=2).reshape(shape3)
        v = c.exchange(v.reshape(toks, size, wide // size).transpose(1, 0, 2), True)
        v = v.reshape(size, toks, wide // (size * n_out), n_out).transpose(1, 2, 0, 3)
        return v.reshape(shape3)

    attended = to_out(by_tokens(attended))
    branch = c.scatter_tokens(attended, lambda v: dot_nn(v, full_out))
    branch_scale = lax.rsqrt(jnp.mean(branch * branch, axis=-1, keepdims=True) + eps)
    hidden = flat_in.astype(F32) + branch * branch_scale * norm_gains[2]
    hidden_low = c.gather_tokens(hidden.astype(BF))

    gates, ups, inners = [], [], []
    for k in range(chunks):
        gate_up = dot_nn(hidden_low, full_gu[k])
        gate, up = gate_up[:, :ffc], gate_up[:, ffc:]
        gates.append(gate)
        ups.append(up)
        inners.append((gate * jax.nn.sigmoid(gate) * up).astype(BF))
    inner = jnp.concatenate(inners, axis=1)
    branch2 = c.scatter_tokens(inner, lambda v: dot_nn(v, full_down))
    branch2_scale = lax.rsqrt(jnp.mean(branch2 * branch2, axis=-1, keepdims=True) + eps)
    output = (hidden + branch2 * branch2_scale * norm_gains[3]).astype(BF)

    upstream = cotangent.reshape(tl, d).astype(F32)
    grad_branch2, gain_mlp = norm_back(branch2, branch2_scale, norm_gains[3], upstream)
    grad_branch2 = c.gather_tokens(grad_branch2.astype(BF))
    sums_down, sums_gu, grads_gu = [], [], []
    for k in range(chunks):
        g_down = dot_tn(inners[k], grad_branch2).astype(BF)
        sums_down.append(c.scatter(g_down.reshape(copies, piece, d)))
    for k in range(chunks):
        gate, up = gates[k], ups[k]
        sig = jax.nn.sigmoid(gate)
        grad_inner = dot_nt(grad_branch2, full_down[k * ffc : (k + 1) * ffc])
        grad_gate = grad_inner * up * sig * (1.0 + gate * (1.0 - sig))
        grad_gu = jnp.concatenate([grad_gate, grad_inner * (gate * sig)], axis=1).astype(BF)
        grads_gu.append(grad_gu)
        g_gu = dot_tn(hidden_low, grad_gu).astype(BF)
        sums_gu.append(c.scatter(g_gu.reshape(copies, size * n_in, 2 * ffc)))
    grad_gu = jnp.concatenate(grads_gu, axis=1)
    full_gu = jnp.concatenate(full_gu, axis=1)
    grad_hidden = upstream + c.scatter_tokens(grad_gu, lambda v: dot_nt(v, full_gu))
    grad_branch, gain_attn = norm_back(branch, branch_scale, norm_gains[2], grad_hidden)
    grad_branch = c.gather_tokens(grad_branch.astype(BF))
    g_out = dot_tn(attended, grad_branch).astype(BF)
    grad_out = c.scatter(g_out.reshape(copies, n_out, d))
    grad_att = by_rows(from_out(dot_nt(grad_branch, full_out).astype(BF)))
    grad_probs = jnp.einsum("rqhd,rkhd->rhqk", grad_att, value, preferred_element_type=F32)
    grad_value = jnp.einsum("rhqk,rqhd->rkhd", probs_low, grad_att, preferred_element_type=F32)
    row_sum = jnp.sum(probs * grad_probs, axis=-1, keepdims=True)
    grad_scores = (probs * (grad_probs - row_sum)).astype(BF)
    grad_query = jnp.einsum("rhqk,rkhd->rqhd", grad_scores, key, preferred_element_type=F32)
    grad_key = jnp.einsum("rhqk,rqhd->rkhd", grad_scores, query, preferred_element_type=F32)
    grad_query = by_tokens((grad_query * score_scale).astype(BF)).astype(F32)
    grad_key = by_tokens((grad_key * score_scale).astype(BF)).astype(F32)
    grad_value = by_tokens(grad_value.astype(BF)).reshape(toks, wide)
    e_query = rotate(grad_query, cosine, sine_table, -1.0).reshape(toks, wide)
    e_key = rotate(grad_key, cosine, sine_table, -1.0).reshape(toks, wide)
    scaled_q, scaled_k = e_query * gains_own[0], e_key * gains_own[1]
    means = c.sum_tokens(
        jnp.stack([jnp.sum(scaled_q * query_pre, -1), jnp.sum(scaled_k * key_pre, -1)])
    )
    means = means / d
    grad_qp = query_scale * scaled_q - query_pre * query_scale**3 * means[0][:, None]
    grad_kp = key_scale * scaled_k - key_pre * key_scale**3 * means[1][:, None]
    gain_query = jnp.sum(e_query * query_pre * query_scale, axis=0)
    gain_key = jnp.sum(e_key * key_pre * key_scale, axis=0)
    grad_mixed = jnp.concatenate([grad_qp.astype(BF), grad_kp.astype(BF), grad_value], axis=1)
    g_qkv = dot_tn(x_full, grad_mixed).astype(BF)
    sum_qkv = c.scatter(g_qkv.reshape(copies, size * n_in, 3 * wide))
    grad_input = grad_hidden + c.scatter_tokens(grad_mixed, lambda v: dot_nt(v, full_qkv))

    back_gu = jnp.stack([v.astype(BF).reshape(size, n_in, 2 * ffc) for v in sums_gu], axis=1)
    back_gu = c.exchange(back_gu).astype(F32)
    back_gu = back_gu.reshape(size, chunks, n_in, 2, copies, piece)
    grad_gate_up = back_gu.transpose(2, 3, 4, 0, 1, 5)
    back_qkv = c.exchange(sum_qkv.astype(BF).reshape(size, n_in, 3 * wide)).astype(F32)
    if pairs:
        grad_qkv = back_qkv.reshape(half_group, 2, n_in, 3, hl, HD).transpose(2, 3, 1, 4, 0, 5)
    else:
        grad_qkv = back_qkv.reshape(size, n_in, 3, wide).transpose(1, 2, 0, 3)

    own_terms = jnp.zeros((size, 2, wide), F32)
    own_terms = lax.dynamic_update_slice(own_terms, jnp.stack([gain_query, gain_key])[None], (c.g, 0, 0))
    if pairs:
        own_terms = own_terms.reshape(half_group, 2, 2, hl, HD).transpose(2, 1, 3, 0, 4)
    else:
        own_terms = own_terms.transpose(1, 0, 2)
    terms = jnp.concatenate([own_terms.reshape(2, d), jnp.stack([gain_attn, gain_mlp])])
    grad_gains = c.sum_all(terms)

    return (
        output.reshape(layer_input.shape),
        grad_input.reshape(layer_input.shape),
        grad_qkv.reshape(w_qkv.shape),
        grad_out,
        grad_gate_up.reshape(w_gate_up.shape),
        jnp.concatenate(sums_down, axis=0),
        grad_gains,
    )


def solution(mesh):
    both = P(("rows", "seq"), None)
    tokens = P("rows", "seq", None)
    return jax.shard_map(
        per_device,
        mesh=mesh,
        in_specs=(tokens, P("rows", None), both, both, both, both, P(), tokens),
        out_specs=(tokens, tokens, both, both, both, both, P()),
        check_vma=False,
    )
```

time: 1170 us -> 1220 us (1.043)
  local copies, waits for them, and re-layouts: 117 us -> 196 us
  waiting for transfers between devices: 663 us -> 590 us
  other arithmetic: 85.7 us -> 119 us
  matrix products: 195 us -> 216 us
    ppermute x114 -> x134, waiting for transfers between devices: 663 us -> 590 us  [send(): return lax.ppermute(v, ('rows', 'seq'), pairs)]
    unnamed x151 -> x230, local copies, waits for them, and re-layouts: 7.43 us -> 43.1 us
    convert_element_type x1 -> x10, local copies, waits for them, and re-layouts: 0.08 us -> 32.8 us  [the longest x4 15.5 us: per_device(): grad_query = by_tokens((grad_query * score_scale).astype(BF)).astype(F32)]
    cos x0 -> x2, other arithmetic: none -> 20.3 us  [rope_tables(): return (jnp.cos(angles)[:, None, :], jnp.sin(angles)[:, None, :])]
    convert_element_type x25, other arithmetic: 36.1 us -> 17.3 us  [the longest x12 11.3 us: scatter(): run.astype(BF)]
    dynamic_update_slice x48 -> x38, local copies, waits for them, and re-layouts: 30.3 us -> 13.2 us  [the longest x24 7.72 us: gather(): full = lax.dynamic_update_index_in_dim(full, block, self.near(j), 0)]
    squeeze x15 -> x8, local copies, waits for them, and re-layouts: 18.9 us -> 2.42 us  [pick(): return lax.dynamic_index_in_dim(array, index, 0, keepdims=False)]
    concatenate x1 -> x10, local copies, waits for them, and re-layouts: 0.07 us -> 14.2 us  [the longest x4 11.3 us: rotate(): jnp.concatenate([-tensor[..., half_width:], tensor[..., :half_width]], ax...]
  transfers between devices with their start and end apart: 114 -> 134, of which waited for: 49 -> 59; matrix products, arithmetic and copies ran while one was open for 25% -> 33% of each run, Pallas kernels for 0% -> 0%
where the time goes in v2:
time: 1220 us; the launch traced here: 1210 us
  waiting for transfers between devices  590 us (48%)
  matrix products  216 us (18%)
  local copies, waits for them, and re-layouts  196 us (16%)
  other arithmetic  119 us (10%)
  starting transfers between devices  83.4 us (7%)
    ppermute x134, waiting for transfers between devices, send(): return lax.ppermute(v, ('rows', 'seq'), pairs)  590 us
    ppermute x134, starting transfers between devices, send(): return lax.ppermute(v, ('rows', 'seq'), pairs)  83.4 us
    dot_general x7, matrix products, dot_nt(): lax.dot_general(a, b, (((1,), (1,)), ((), ())), preferred_element_type=F32)  57.9 us
    dot_general x6, matrix products, dot_tn(): lax.dot_general(a, b, (((0,), (0,)), ((), ())), preferred_element_type=F32)  56.1 us
    dot_general x7, matrix products, dot_nn(): lax.dot_general(a, b, (((1,), (0,)), ((), ())), preferred_element_type=F32)  54.8 us
    unnamed x230, local copies, waits for them, and re-layouts  43.1 us
  transfers between devices with their start and end apart: 134, of which 59 were waited for; matrix products, arithmetic and copies ran while one was open for 33% of the time, Pallas kernels for 0%

profile of v2, /device:TPU:0, one launch (start us, length us, event | category | flops | bytes accessed | tf_op | source)
XLA Modules:
  0.0 1208.4 jit_solution(108789151906826602)
XLA Ops:
  35.1 15.6 %fusion.111 = (f32[2,2,2,256,128]{3,2,1,0,4:T(2,128)}, f32[2,2,2,256,128]{3,2,1,0,4:T(2,128)}) fusion(f32[2,2,2,256,64]{3,2,1,0,4:T(2,128)S(1)} %broadcast_multiply_fusion.1), kind=kLoop, calls=%fused_computation.252 | loop fusion | flops 262144 | bytes 2621440 | tf_op jit(solution)/shard_map/cos | solution.py:19
  88.3 19.4 %collective-permute-done.20 = bf16[64,2048]{1,0:T(8,128)(2,1)S(1)} collective-permute-done((bf16[64,2048]{1,0:T(8,128)(2,1)}, bf16[64,2048]{1,0:T(8,128)(2,1)S(1)}, u32[]{:S(2)}, u32[]{:S(2)}) %collective-permute-start.20) | collective-permute-done | bytes 262176 | tf_op jit(solution)/shard_map/ppermute | solution.py:70
  111.5 23.7 %collective-permute-done.13 = bf16[512,768]{1,0:T(8,128)(2,1)S(1)} collective-permute-done((bf16[512,768]{1,0:T(8,128)(2,1)S(1)}, bf16[512,768]{1,0:T(8,128)(2,1)S(1)}, u32[]{:S(2)}, u32[]{:S(2)}) %collective-permute-start.13) | collective-permute-done | bytes 786464 | tf_op jit(solution)/shard_map/ppermute | solution.py:70
  242.8 19.5 %collective-permute-done.42 = bf16[1,4,2,64,1024]{4,3,2,1,0:T(8,128)(2,1)S(1)} collective-permute-done((bf16[1,4,2,64,1024]{4,3,2,1,0:T(8,128)(2,1)S(1)}, bf16[1,4,2,64,1024]{4,3,2,1,0:T(8,128)(2,1)S(1)}, u32[]{:S(2)}, u32[]{:S(2)}) %collective-permute-start.42) | collective-permute-done | bytes 1048608 | tf_op jit(solution)/shard_map/ppermute | solution.py:70
  267.8 21.5 %collective-permute-done.43 = bf16[512,1024]{1,0:T(8,128)(2,1)S(1)} collective-permute-done((bf16[512,1024]{1,0:T(8,128)(2,1)S(1)}, bf16[512,1024]{1,0:T(8,128)(2,1)S(1)}, u32[]{:S(2)}, u32[]{:S(2)}) %collective-permute-start.43) | collective-permute-done | bytes 1048608 | tf_op jit(solution)/shard_map/ppermute | solution.py:70
  330.2 14.5 %collective-permute-done.46 = bf16[512,1024]{1,0:T(8,128)(2,1)S(1)} collective-permute-done((bf16[512,1024]{1,0:T(8,128)(2,1)S(1)}, bf16[512,1024]{1,0:T(8,128)(2,1)S(1)}, u32[]{:S(2)}, u32[]{:S(2)}) %collective-permute-start.46) | collective-permute-done | bytes 1048608 | tf_op jit(solution)/shard_map/ppermute | solution.py:70
  344.7 19.1 %collective-permute-done.45 = bf16[512,1024]{1,0:T(8,128)(2,1)S(1)} collective-permute-done((bf16[512,1024]{1,0:T(8,128)(2,1)S(1)}, bf16[512,1024]{1,0:T(8,128)(2,1)S(1)}, u32[]{:S(2)}, u32[]{:S(2)}) %collective-permute-start.45) | collective-permute-done | bytes 1048608 | tf_op jit(solution)/shard_map/ppermute | solution.py:70
  366.5 21.0 %collective-permute-done.47 = bf16[512,1024]{1,0:T(8,128)(2,1)S(1)} collective-permute-done((bf16[512,1024]{1,0:T(8,128)(2,1)S(1)}, bf16[512,1024]{1,0:T(8,128)(2,1)S(1)}, u32[]{:S(2)}, u32[]{:S(2)}) %collective-permute-start.47) | collective-permute-done | bytes 1048608 | tf_op jit(solution)/shard_map/ppermute | solution.py:70
  388.6 15.7 %collective-permute-done.49 = bf16[128,2048]{1,0:T(8,128)(2,1)S(1)} collective-permute-done((bf16[128,2048]{1,0:T(8,128)(2,1)S(1)}, bf16[128,2048]{1,0:T(8,128)(2,1)S(1)}, u32[]{:S(2)}, u32[]{:S(2)}) %collective-permute-start.49) | collective-permute-done | bytes 524320 | tf_op jit(solution)/shard_map/ppermute | solution.py:70
  405.6 20.6 %collective-permute-done.48 = bf16[512,1024]{1,0:T(8,128)(2,1)S(1)} collective-permute-done((bf16[512,1024]{1,0:T(8,128)(2,1)S(1)}, bf16[512,1024]{1,0:T(8,128)(2,1)S(1)}, u32[]{:S(2)}, u32[]{:S(2)}) %collective-permute-start.48) | collective-permute-done | bytes 1048608 | tf_op jit(solution)/shard_map/ppermute | solution.py:70
  431.6 13.3 %fusion.165 = f32[2048,1024]{0,1:T(8,128)S(1)} fusion(bf16[2048,2048]{1,0:T(8,128)(2,1)} %copy-done.65, bf16[2048,1024]{1,0:T(8,128)(2,1)} %bitcast.444), kind=kOutput, calls=%fused_computation.423 | convolution fusion | flops 8589934592 | bytes 20971520 | tf_op jit(solution)/shard_map/dot_general | solution.py:29
  445.0 16.1 %fusion.164 = f32[2048,1024]{0,1:T(8,128)S(1)} fusion(bf16[2048,2048]{1,0:T(8,128)(2,1)} %copy-done.65, bf16[2048,1024]{1,0:T(8,128)(2,1)} %bitcast.441), kind=kOutput, calls=%fused_computation.422 | convolution fusion | flops 8589934592 | bytes 20971520 | tf_op jit(solution)/shard_map/dot_general | solution.py:29
  466.4 14.6 %collective-permute-done.52 = bf16[128,2048]{1,0:T(8,128)(2,1)S(1)} collective-permute-done((bf16[128,2048]{1,0:T(8,128)(2,1)S(1)}, bf16[128,2048]{1,0:T(8,128)(2,1)S(1)}, u32[]{:S(2)}, u32[]{:S(2)}) %collective-permute-start.52) | collective-permute-done | bytes 524320 | tf_op jit(solution)/shard_map/ppermute | solution.py:70
  492.6 13.2 %collective-permute-done.53 = bf16[128,2048]{1,0:T(8,128)(2,1)S(1)} collective-permute-done((bf16[128,2048]{1,0:T(8,128)(2,1)S(1)}, bf16[128,2048]{1,0:T(8,128)(2,1)S(1)}, u32[]{:S(2)}, u32[]{:S(2)}) %collective-permute-start.53) | collective-permute-done | bytes 524320 | tf_op jit(solution)/shard_map/ppermute | solution.py:70
  505.9 13.4 %collective-permute-done.54 = bf16[128,2048]{1,0:T(8,128)(2,1)S(1)} collective-permute-done((bf16[128,2048]{1,0:T(8,128)(2,1)S(1)}, bf16[128,2048]{1,0:T(8,128)(2,1)S(1)}, u32[]{:S(2)}, u32[]{:S(2)}) %collective-permute-start.54) | collective-permute-done | bytes 524320 | tf_op jit(solution)/shard_map/ppermute | solution.py:70
  579.7 18.2 %collective-permute-done.66 = bf16[256,2048]{1,0:T(8,128)(2,1)} collective-permute-done((bf16[256,2048]{1,0:T(8,128)(2,1)}, bf16[256,2048]{1,0:T(8,128)(2,1)}, u32[]{:S(2)}, u32[]{:S(2)}) %collective-permute-start.66) | collective-permute-done | bytes 1048608 | tf_op jit(solution)/shard_map/ppermute | solution.py:70
  647.2 12.2 %fusion.6 = f32[1024,2048]{1,0:T(8,128)S(1)} fusion(bf16[2048,1024]{1,0:T(8,128)(2,1)} %bitcast.445, bf16[2048,1024]{1,0:T(8,128)(2,1)S(1)} %bitcast.442, bf16[2048,2048]{0,1:T(8,128)(2,1)} %pad_maximum_fusion), kind=kOutput, calls=%fused_computation.14 | convolution fusion | flops 8606711808 | bytes 20971520 | tf_op jit(solution)/shard_map/dot_general | solution.py:33
  659.4 13.5 %fusion.29 = bf16[1024,2048]{1,0:T(8,128)(2,1)} fusion(bf16[2048,1024]{1,0:T(8,128)(2,1)} %bitcast.446, bf16[2048,1024]{1,0:T(8,128)(2,1)S(1)} %bitcast.443, bf16[2048,2048]{0,1:T(8,128)(2,1)} %pad_maximum_fusion), kind=kOutput, calls=%fused_computation.44 | convolution fusion | flops 8608808960 | bytes 16777216 | tf_op jit(solution)/shard_map/dot_general | solution.py:33
  673.0 12.4 %fusion.23 = bf16[2048,1024]{1,0:T(8,128)(2,1)S(1)} fusion(bf16[2048,2048]{1,0:T(8,128)(2,1)} %copy-done.65, bf16[2048,512]{0,1:T(8,128)(2,1)} %get-tuple-element.53, bf16[2048,512]{0,1:T(8,128)(2,1)S(1)} %copy-done.47), kind=kOutput, calls=%fused_computation.42 | convolution fusion | flops 8600420352 | bytes 16777216 | tf_op jit(solution)/shard_map/dot_general | solution.py:37
  685.4 14.3 %fusion.26 = bf16[2048,1024]{1,0:T(8,128)(2,1)S(1)} fusion(bf16[2048,2048]{1,0:T(8,128)(2,1)} %copy-done.65, bf16[2048,512]{0,1:T(8,128)(2,1)} %get-tuple-element.51, bf16[2048,512]{0,1:T(8,128)(2,1)} %copy-done.49), kind=kOutput, calls=%fused_computation.43 | convolution fusion | flops 8600420352 | bytes 16777216 | tf_op jit(solution)/shard_map/dot_general | solution.py:37
  752.2 54.5 %collective-permute-done.127 = bf16[128,2048]{1,0:T(8,128)(2,1)} collective-permute-done((bf16[128,2048]{1,0:T(8,128)(2,1)S(1)}, bf16[128,2048]{1,0:T(8,128)(2,1)}, u32[]{:S(2)}, u32[]{:S(2)}) %collective-permute-start.127) | collective-permute-done | bytes 524320 | tf_op jit(solution)/shard_map/ppermute | solution.py:70
  859.7 20.0 %collective-permute-done.115 = bf16[512,1024]{1,0:T(8,128)(2,1)S(1)} collective-permute-done((bf16[512,1024]{1,0:T(8,128)(2,1)S(1)}, bf16[512,1024]{1,0:T(8,128)(2,1)S(1)}, u32[]{:S(2)}, u32[]{:S(2)}) %collective-permute-start.115) | collective-permute-done | bytes 1048608 | tf_op jit(solution)/shard_map/ppermute | solution.py:70
  906.5 18.2 %collective-permute-done.119 = bf16[512,1024]{1,0:T(8,128)(2,1)S(1)} collective-permute-done((bf16[512,1024]{1,0:T(8,128)(2,1)S(1)}, bf16[512,1024]{1,0:T(8,128)(2,1)S(1)}, u32[]{:S(2)}, u32[]{:S(2)}) %collective-permute-start.119) | collective-permute-done | bytes 1048608 | tf_op jit(solution)/shard_map/ppermute | solution.py:70
  925.1 14.2 %collective-permute-done.116 = bf16[512,1024]{1,0:T(8,128)(2,1)S(1)} collective-permute-done((bf16[512,1024]{1,0:T(8,128)(2,1)S(1)}, bf16[512,1024]{1,0:T(8,128)(2,1)S(1)}, u32[]{:S(2)}, u32[]{:S(2)}) %collective-permute-start.116) | collective-permute-done | bytes 1048608 | tf_op jit(solution)/shard_map/ppermute | solution.py:70
  (759 shorter events, 765.6 us)
Async XLA Ops:
  0.6 56.1 %collective-permute-start = (bf16[256,2048]{1,0:T(8,128)(2,1)}, bf16[256,2048]{1,0:T(8,128)(2,1)}, u32[]{:S(2)}, u32[]{:S(2)}) collective-permute-start(bf16[256,2048]{1,0:T(8,128)(2,1)} %bitcast.420), channel_id=1, source_target_pairs={{0,2},{1,3},{2,0},{3,1},{4,6},{5,7},{6,4},{7,5},{8,10},{9,11},{10,... | collective-permute-start | bytes 3145736 | tf_op jit(solution)/shard_map/ppermute | solution.py:70
  3.7 50.4 %collective-permute-start.1 = (bf16[256,2048]{1,0:T(8,128)(2,1)}, bf16[256,2048]{1,0:T(8,128)(2,1)}, u32[]{:S(2)}, u32[]{:S(2)}) collective-permute-start(bf16[256,2048]{1,0:T(8,128)(2,1)} %bitcast.421), channel_id=1, source_target_pairs={{0,4},{1,5},{2,6},{3,7},{4,0},{5,1},{6,2},{7,3},{8,12},{9,13},{10,... | collective-permute-start | bytes 3145736 | tf_op jit(solution)/shard_map/ppermute | solution.py:70
  5.2 79.5 %collective-permute-start.4 = (bf16[256,2048]{1,0:T(8,128)(2,1)}, bf16[256,2048]{1,0:T(8,128)(2,1)}, u32[]{:S(2)}, u32[]{:S(2)}) collective-permute-start(bf16[256,2048]{1,0:T(8,128)(2,1)} %bitcast.422), channel_id=1, source_target_pairs={{0,1},{1,0},{2,3},{3,2},{4,5},{5,4},{6,7},{7,6},{8,9},{9,8},{10,11... | collective-permute-start | bytes 3145736 | tf_op jit(solution)/shard_map/ppermute | solution.py:70
  5.2 47.2 %collective-permute-start.19 = (bf16[64,2048]{1,0:T(8,128)(2,1)}, bf16[64,2048]{1,0:T(8,128)(2,1)}, u32[]{:S(2)}, u32[]{:S(2)}) collective-permute-start(bf16[64,2048]{1,0:T(8,128)(2,1)} %param.11), channel_id=1, source_target_pairs={{0,8},{1,9},{2,10},{3,11},{4,12},{5,13},{6,14},{7,15},{8,16},{9,17... | collective-permute-start | bytes 786440 | tf_op jit(solution)/shard_map/ppermute | solution.py:70
  58.4 49.3 %collective-permute-start.5 = (bf16[256,2048]{1,0:T(8,128)(2,1)}, bf16[256,2048]{1,0:T(8,128)(2,1)S(1)}, u32[]{:S(2)}, u32[]{:S(2)}) collective-permute-start(bf16[256,2048]{1,0:T(8,128)(2,1)} %collective-permute-done), channel_id=1, source_target_pairs={{0,1},{1,0},{2,3},{3,2},{4,5},{5,4},{6,7},{7,6},{8,9},{9,8},{10,11... | collective-permute-start | bytes 3145736 | tf_op jit(solution)/shard_map/ppermute | solution.py:70
  107.8 125.8 %collective-permute-start.21 = (bf16[64,2048]{1,0:T(8,128)(2,1)S(1)}, bf16[64,2048]{1,0:T(8,128)(2,1)}, u32[]{:S(2)}, u32[]{:S(2)}) collective-permute-start(bf16[64,2048]{1,0:T(8,128)(2,1)S(1)} %collective-permute-done.20), channel_id=1, source_target_pairs={{0,8},{1,9},{2,10},{3,11},{4,12},{5,13},{6,14},{7,15},{8,16},{9,17... | collective-permute-start | bytes 786440 | tf_op jit(solution)/shard_map/ppermute | solution.py:70
  153.9 81.4 %collective-permute-start.41 = (bf16[2,2,2,64,1024]{4,3,2,1,0:T(8,128)(2,1)}, bf16[2,2,2,64,1024]{4,3,2,1,0:T(8,128)(2,1)}, u32[]{:S(2)}, u32[]{:S(2)}) collective-permute-start(bf16[2,2,2,64,1024]{4,3,2,1,0:T(8,128)(2,1)} %dynamic-slice_bitcast_fusion.5), channel_id=1, source_target_pairs={{0,2},{1,3},{2,0},{3,1},{4,6},{5,7},{6,4},{7,5},{8,10},{9,11},{10,... | collective-permute-start | bytes 3145736 | tf_op jit(solution)/shard_map/ppermute | solution.py:70
  316.9 46.9 %collective-permute-start.45 = (bf16[512,1024]{1,0:T(8,128)(2,1)S(1)}, bf16[512,1024]{1,0:T(8,128)(2,1)S(1)}, u32[]{:S(2)}, u32[]{:S(2)}) collective-permute-start(bf16[512,1024]{1,0:T(8,128)(2,1)S(1)} %collective-permute-done.44), channel_id=1, source_target_pairs={{0,8},{1,9},{2,10},{3,11},{4,12},{5,13},{6,14},{7,15},{8,16},{9,17... | collective-permute-start | bytes 3145736 | tf_op jit(solution)/shard_map/ppermute | solution.py:70
  330.1 57.8 %collective-permute-start.36 = (bf16[256,2048]{1,0:T(8,128)(2,1)S(1)}, bf16[256,2048]{1,0:T(8,128)(2,1)S(1)}, u32[]{:S(2)}, u32[]{:S(2)}) collective-permute-start(bf16[256,2048]{1,0:T(8,128)(2,1)S(1)} %get-tuple-element.47), channel_id=1, source_target_pairs={{0,1},{1,0},{2,3},{3,2},{4,5},{5,4},{6,7},{7,6},{8,9},{9,8},{10,11... | collective-permute-start | bytes 3145736 | tf_op jit(solution)/shard_map/ppermute | solution.py:70
  734.0 95.4 %collective-permute-start.73 = (bf16[256,2048]{1,0:T(8,128)(2,1)}, bf16[256,2048]{1,0:T(8,128)(2,1)}, u32[]{:S(2)}, u32[]{:S(2)}) collective-permute-start(bf16[256,2048]{1,0:T(8,128)(2,1)} %get-tuple-element.74), channel_id=1, source_target_pairs={{0,1},{1,0},{2,3},{3,2},{4,5},{5,4},{6,7},{7,6},{8,9},{9,8},{10,11... | collective-permute-start | bytes 3145736 | tf_op jit(solution)/shard_map/ppermute | solution.py:70
  744.8 63.7 %collective-permute-start.117 = (bf16[512,1024]{1,0:T(8,128)(2,1)}, bf16[512,1024]{1,0:T(8,128)(2,1)}, u32[]{:S(2)}, u32[]{:S(2)}) collective-permute-start(bf16[512,1024]{1,0:T(8,128)(2,1)} %dynamic-slice_bitcast_fusion.2), channel_id=1, source_target_pairs={{0,8},{1,9},{2,10},{3,11},{4,12},{5,13},{6,14},{7,15},{8,16},{9,17... | collective-permute-start | bytes 3145736 | tf_op jit(solution)/shard_map/ppermute | solution.py:70
  745.7 78.4 %collective-permute-start.114 = (bf16[512,1024]{1,0:T(8,128)(2,1)}, bf16[512,1024]{1,0:T(8,128)(2,1)}, u32[]{:S(2)}, u32[]{:S(2)}) collective-permute-start(bf16[512,1024]{1,0:T(8,128)(2,1)} %dynamic-slice_bitcast_fusion.3), channel_id=1, source_target_pairs={{0,8},{1,9},{2,10},{3,11},{4,12},{5,13},{6,14},{7,15},{8,16},{9,17... | collective-permute-start | bytes 3145736 | tf_op jit(solution)/shard_map/ppermute | solution.py:70
  745.7 60.9 %collective-permute-start.127 = (bf16[128,2048]{1,0:T(8,128)(2,1)S(1)}, bf16[128,2048]{1,0:T(8,128)(2,1)}, u32[]{:S(2)}, u32[]{:S(2)}) collective-permute-start(bf16[128,2048]{1,0:T(8,128)(2,1)S(1)} %fusion.105), channel_id=1, source_target_pairs={{0,8},{1,9},{2,10},{3,11},{4,12},{5,13},{6,14},{7,15},{8,16},{9,17... | collective-permute-start | bytes 1572872 | tf_op jit(solution)/shard_map/ppermute | solution.py:70
  746.4 79.4 %collective-permute-start.124 = (bf16[128,2048]{1,0:T(8,128)(2,1)}, bf16[128,2048]{1,0:T(8,128)(2,1)}, u32[]{:S(2)}, u32[]{:S(2)}) collective-permute-start(bf16[128,2048]{1,0:T(8,128)(2,1)} %fusion.107), channel_id=1, source_target_pairs={{0,8},{1,9},{2,10},{3,11},{4,12},{5,13},{6,14},{7,15},{8,16},{9,17... | collective-permute-start | bytes 1572872 | tf_op jit(solution)/shard_map/ppermute | solution.py:70
  833.2 46.5 %collective-permute-start.115 = (bf16[512,1024]{1,0:T(8,128)(2,1)S(1)}, bf16[512,1024]{1,0:T(8,128)(2,1)S(1)}, u32[]{:S(2)}, u32[]{:S(2)}) collective-permute-start(bf16[512,1024]{1,0:T(8,128)(2,1)S(1)} %fusion.68), channel_id=1, source_target_pairs={{0,8},{1,9},{2,10},{3,11},{4,12},{5,13},{6,14},{7,15},{8,16},{9,17... | collective-permute-start | bytes 3145736 | tf_op jit(solution)/shard_map/ppermute | solution.py:70
  835.6 55.4 %collective-permute-start.128 = (bf16[128,2048]{1,0:T(8,128)(2,1)S(1)}, bf16[128,2048]{1,0:T(8,128)(2,1)S(1)}, u32[]{:S(2)}, u32[]{:S(2)}) collective-permute-start(bf16[128,2048]{1,0:T(8,128)(2,1)S(1)} %fusion.104), channel_id=1, source_target_pairs={{0,8},{1,9},{2,10},{3,11},{4,12},{5,13},{6,14},{7,15},{8,16},{9,17... | collective-permute-start | bytes 1572872 | tf_op jit(solution)/shard_map/ppermute | solution.py:70
  842.1 60.1 %collective-permute-start.125 = (bf16[128,2048]{1,0:T(8,128)(2,1)}, bf16[128,2048]{1,0:T(8,128)(2,1)S(1)}, u32[]{:S(2)}, u32[]{:S(2)}) collective-permute-start(bf16[128,2048]{1,0:T(8,128)(2,1)} %fusion.106), channel_id=1, source_target_pairs={{0,8},{1,9},{2,10},{3,11},{4,12},{5,13},{6,14},{7,15},{8,16},{9,17... | collective-permute-start | bytes 1572872 | tf_op jit(solution)/shard_map/ppermute | solution.py:70
  848.1 56.5 %collective-permute-start.83 = (bf16[256,2048]{1,0:T(8,128)(2,1)S(1)}, bf16[256,2048]{1,0:T(8,128)(2,1)S(1)}, u32[]{:S(2)}, u32[]{:S(2)}) collective-permute-start(bf16[256,2048]{1,0:T(8,128)(2,1)S(1)} %get-tuple-element.40), channel_id=1, source_target_pairs={{0,2},{1,3},{2,0},{3,1},{4,6},{5,7},{6,4},{7,5},{8,10},{9,11},{10,... | collective-permute-start | bytes 3145736 | tf_op jit(solution)/shard_map/ppermute | solution.py:70
  891.0 48.3 %collective-permute-start.116 = (bf16[512,1024]{1,0:T(8,128)(2,1)S(1)}, bf16[512,1024]{1,0:T(8,128)(2,1)S(1)}, u32[]{:S(2)}, u32[]{:S(2)}) collective-permute-start(bf16[512,1024]{1,0:T(8,128)(2,1)S(1)} %fusion.67), channel_id=1, source_target_pairs={{0,8},{1,9},{2,10},{3,11},{4,12},{5,13},{6,14},{7,15},{8,16},{9,17... | collective-permute-start | bytes 3145736 | tf_op jit(solution)/shard_map/ppermute | solution.py:70
  954.8 96.7 %collective-permute-start.121 = (bf16[2,2,2,64,1024]{4,3,2,1,0:T(8,128)(2,1)}, bf16[2,2,2,64,1024]{4,3,2,1,0:T(8,128)(2,1)}, u32[]{:S(2)}, u32[]{:S(2)}) collective-permute-start(bf16[2,2,2,64,1024]{4,3,2,1,0:T(8,128)(2,1)} %dynamic-slice_bitcast_fusion.1), channel_id=1, source_target_pairs={{0,2},{1,3},{2,0},{3,1},{4,6},{5,7},{6,4},{7,5},{8,10},{9,11},{10,... | collective-permute-start | bytes 3145736 | tf_op jit(solution)/shard_map/ppermute | solution.py:70
  963.6 86.0 %collective-permute-start.112 = (bf16[64,2048]{1,0:T(8,128)(2,1)S(1)}, bf16[64,2048]{1,0:T(8,128)(2,1)}, u32[]{:S(2)}, u32[]{:S(2)}) collective-permute-start(bf16[64,2048]{1,0:T(8,128)(2,1)S(1)} %fusion.118), channel_id=1, source_target_pairs={{0,8},{1,9},{2,10},{3,11},{4,12},{5,13},{6,14},{7,15},{8,16},{9,17... | collective-permute-start | bytes 786440 | tf_op jit(solution)/shard_map/ppermute | solution.py:70
  1112.1 49.0 %collective-permute-start.122 = (bf16[1,4,2,64,1024]{4,3,2,1,0:T(8,128)(2,1)}, bf16[1,4,2,64,1024]{4,3,2,1,0:T(8,128)(2,1)S(1)}, u32[]{:S(2)}, u32[]{:S(2)}) collective-permute-start(bf16[1,4,2,64,1024]{4,3,2,1,0:T(8,128)(2,1)} %dynamic-slice_bitcast_fusion), channel_id=1, source_target_pairs={{0,4},{1,5},{2,6},{3,7},{4,0},{5,1},{6,2},{7,3},{8,12},{9,13},{10,... | collective-permute-start | bytes 3145736 | tf_op jit(solution)/shard_map/ppermute | solution.py:70
  1113.3 80.9 %collective-permute-start.95 = (bf16[256,2048]{1,0:T(8,128)(2,1)}, bf16[256,2048]{1,0:T(8,128)(2,1)}, u32[]{:S(2)}, u32[]{:S(2)}) collective-permute-start(bf16[256,2048]{1,0:T(8,128)(2,1)} %get-tuple-element.73), channel_id=1, source_target_pairs={{0,1},{1,0},{2,3},{3,2},{4,5},{5,4},{6,7},{7,6},{8,9},{9,8},{10,11... | collective-permute-start | bytes 3145736 | tf_op jit(solution)/shard_map/ppermute | solution.py:70
  1134.6 60.4 %collective-permute-start.97 = (bf16[128,2048]{1,0:T(8,128)(2,1)}, bf16[128,2048]{1,0:T(8,128)(2,1)S(1)}, u32[]{:S(2)}, u32[]{:S(2)}) collective-permute-start(bf16[128,2048]{1,0:T(8,128)(2,1)} %slice.661), channel_id=1, source_target_pairs={{0,4},{1,5},{2,6},{3,7},{4,0},{5,1},{6,2},{7,3},{8,12},{9,13},{10,... | collective-permute-start | bytes 1572872 | tf_op jit(solution)/shard_map/ppermute | solution.py:70
  (203 other events, 3515.8 us)

commit v3 on v2

--- a/solution.py
+++ b/solution.py
@@ -64,6 +64,7 @@
         self.seq, self.t, self.s = seq, row % self.part, s
         bits = [1 << i for i in range(self.size.bit_length() - 1)]
         self.bits = bits
+        self.lines = [[i * self.size + g for i in range(self.copies)] for g in range(self.size)]
         self.order = list(range(0, self.size, 2)) + list(range(1, self.size, 2))
 
     def send(self, v, pairs):
@@ -72,29 +73,13 @@
     def swap(self, v, j):
         return self.send(v, [(i, i ^ j) for i in range(self.count)])
 
-    def ring(self, v):
-        return self.send(v, [(i, (i + self.size) % self.count) for i in range(self.count)])
-
-    def near(self, j):
-        return (self.d + (self.copies - j)) % self.copies
-
-    def gather(self, block, firsts=()):
-        full = jnp.zeros((self.copies,) + block.shape, block.dtype)
-        arrivals = []
-        for j in range(self.copies):
-            full = lax.dynamic_update_index_in_dim(full, block, self.near(j), 0)
-            if j < self.copies - 1:
-                if j < len(firsts):
-                    block = after(block, firsts[j])
-                block = self.ring(block)
-                arrivals.append(block)
-        return full, arrivals
+    def gather(self, block):
+        return lax.all_gather(block, ("rows", "seq"), axis=0, tiled=True, axis_index_groups=self.lines)
 
     def scatter(self, parts):
-        run = pick(parts, self.near(1))
-        for j in range(2, self.copies + 1):
-            run = self.ring(run.astype(BF)).astype(F32) + pick(parts, self.near(j)).astype(F32)
-        return run
+        return lax.psum_scatter(
+            parts, ("rows", "seq"), scatter_dimension=0, tiled=True, axis_index_groups=self.lines
+        )
 
     def exchange(self, parts, tokens=False):
         swap = self.swap_tokens if tokens else self.swap
@@ -172,34 +157,25 @@
     hl = heads // size
     wide = hl * HD
     n_in, n_out, n_ff = w_qkv.shape[0], w_out.shape[0], w_down.shape[0]
-    chunks = 2
-    piece = n_ff // chunks
-    ffc = piece * copies
+    ffl = n_ff * copies
     flat_in = layer_input.reshape(tl, d)
     pairs = 2 * n_out == HD and 2 * hl == copies
     half_group = size // 2
 
-    x_full = c.gather_tokens(flat_in)
     if pairs:
         send_qkv = w_qkv.reshape(n_in, 3, 2, hl, half_group, HD).transpose(4, 2, 0, 1, 3, 5)
     else:
         send_qkv = w_qkv.reshape(n_in, 3, size, wide).transpose(2, 0, 1, 3)
     slab_qkv = c.exchange(send_qkv.reshape(size, n_in, 3 * wide)).reshape(size * n_in, 3 * wide)
-    send_gu = w_gate_up.reshape(n_in, 2, copies, size, chunks, piece).transpose(3, 4, 0, 1, 2, 5)
-    slab_gu = c.exchange(send_gu.reshape(size, chunks, n_in, 2 * ffc))
-
-    full_out, _ = c.gather(w_out)
-    full_out = full_out.reshape(wide, d)
-    full_qkv, z_qkv = c.gather(slab_qkv)
-    full_qkv = full_qkv.reshape(d, 3 * wide)
-    full_gu, full_down, last = [], [], z_qkv
-    for k in range(chunks):
-        full, last = c.gather(slab_gu[:, k].reshape(size * n_in, 2 * ffc), last[-2:])
-        full_gu.append(full.reshape(d, 2 * ffc))
-    for k in range(chunks):
-        full, last = c.gather(w_down[k * piece : (k + 1) * piece], last[-2:])
-        full_down.append(full.reshape(ffc, d))
-    full_down = jnp.concatenate(full_down, axis=0)
+    x_full = c.gather_tokens(flat_in)
+    send_gu = w_gate_up.reshape(n_in, 2, copies, size, n_ff).transpose(3, 0, 1, 2, 4)
+    send_gu = after(send_gu.reshape(size, n_in, 2 * ffl), slab_qkv)
+    slab_gu = c.exchange(send_gu).reshape(size * n_in, 2 * ffl)
+
+    full_out = c.gather(w_out)
+    full_qkv = c.gather(slab_qkv)
+    full_gu = c.gather(after(slab_gu, full_qkv))
+    full_down = c.gather(after(w_down, full_qkv))
 
     lengths = doc_lengths.astype(jnp.int32)
     other = [lengths]
@@ -278,14 +254,10 @@
     hidden = flat_in.astype(F32) + branch * branch_scale * norm_gains[2]
     hidden_low = c.gather_tokens(hidden.astype(BF))
 
-    gates, ups, inners = [], [], []
-    for k in range(chunks):
-        gate_up = dot_nn(hidden_low, full_gu[k])
-        gate, up = gate_up[:, :ffc], gate_up[:, ffc:]
-        gates.append(gate)
-        ups.append(up)
-        inners.append((gate * jax.nn.sigmoid(gate) * up).astype(BF))
-    inner = jnp.concatenate(inners, axis=1)
+    gate_up = dot_nn(hidden_low, full_gu)
+    gate, up = gate_up[:, :ffl], gate_up[:, ffl:]
+    sig = jax.nn.sigmoid(gate)
+    inner = (gate * sig * up).astype(BF)
     branch2 = c.scatter_tokens(inner, lambda v: dot_nn(v, full_down))
     branch2_scale = lax.rsqrt(jnp.mean(branch2 * branch2, axis=-1, keepdims=True) + eps)
     output = (hidden + branch2 * branch2_scale * norm_gains[3]).astype(BF)
@@ -293,26 +265,18 @@
     upstream = cotangent.reshape(tl, d).astype(F32)
     grad_branch2, gain_mlp = norm_back(branch2, branch2_scale, norm_gains[3], upstream)
     grad_branch2 = c.gather_tokens(grad_branch2.astype(BF))
-    sums_down, sums_gu, grads_gu = [], [], []
-    for k in range(chunks):
-        g_down = dot_tn(inners[k], grad_branch2).astype(BF)
-        sums_down.append(c.scatter(g_down.reshape(copies, piece, d)))
-    for k in range(chunks):
-        gate, up = gates[k], ups[k]
-        sig = jax.nn.sigmoid(gate)
-        grad_inner = dot_nt(grad_branch2, full_down[k * ffc : (k + 1) * ffc])
-        grad_gate = grad_inner * up * sig * (1.0 + gate * (1.0 - sig))
-        grad_gu = jnp.concatenate([grad_gate, grad_inner * (gate * sig)], axis=1).astype(BF)
-        grads_gu.append(grad_gu)
-        g_gu = dot_tn(hidden_low, grad_gu).astype(BF)
-        sums_gu.append(c.scatter(g_gu.reshape(copies, size * n_in, 2 * ffc)))
-    grad_gu = jnp.concatenate(grads_gu, axis=1)
-    full_gu = jnp.concatenate(full_gu, axis=1)
+    g_down = dot_tn(inner, grad_branch2).astype(BF)
+    sum_down = c.scatter(g_down)
+    grad_inner = dot_nt(grad_branch2, full_down)
+    grad_gate = grad_inner * up * sig * (1.0 + gate * (1.0 - sig))
+    grad_gu = jnp.concatenate([grad_gate, grad_inner * (gate * sig)], axis=1).astype(BF)
+    g_gu = dot_tn(hidden_low, grad_gu).astype(BF)
+    sum_gu = c.scatter(g_gu)
     grad_hidden = upstream + c.scatter_tokens(grad_gu, lambda v: dot_nt(v, full_gu))
     grad_branch, gain_attn = norm_back(branch, branch_scale, norm_gains[2], grad_hidden)
     grad_branch = c.gather_tokens(grad_branch.astype(BF))
     g_out = dot_tn(attended, grad_branch).astype(BF)
-    grad_out = c.scatter(g_out.reshape(copies, n_out, d))
+    sum_out = c.scatter(g_out)
     grad_att = by_rows(from_out(dot_nt(grad_branch, full_out).astype(BF)))
     grad_probs = jnp.einsum("rqhd,rkhd->rhqk", grad_att, value, preferred_element_type=F32)
     grad_value = jnp.einsum("rhqk,rqhd->rkhd", probs_low, grad_att, preferred_element_type=F32)
@@ -335,15 +299,15 @@
     gain_query = jnp.sum(e_query * query_pre * query_scale, axis=0)
     gain_key = jnp.sum(e_key * key_pre * key_scale, axis=0)
     grad_mixed = jnp.concatenate([grad_qp.astype(BF), grad_kp.astype(BF), grad_value], axis=1)
+    grad_mixed = after(grad_mixed, sum_down, sum_gu)
     g_qkv = dot_tn(x_full, grad_mixed).astype(BF)
-    sum_qkv = c.scatter(g_qkv.reshape(copies, size * n_in, 3 * wide))
+    sum_qkv = c.scatter(g_qkv)
     grad_input = grad_hidden + c.scatter_tokens(grad_mixed, lambda v: dot_nt(v, full_qkv))
 
-    back_gu = jnp.stack([v.astype(BF).reshape(size, n_in, 2 * ffc) for v in sums_gu], axis=1)
-    back_gu = c.exchange(back_gu).astype(F32)
-    back_gu = back_gu.reshape(size, chunks, n_in, 2, copies, piece)
-    grad_gate_up = back_gu.transpose(2, 3, 4, 0, 1, 5)
-    back_qkv = c.exchange(sum_qkv.astype(BF).reshape(size, n_in, 3 * wide)).astype(F32)
+    back_gu = c.exchange(sum_gu.reshape(size, n_in, 2 * ffl)).astype(F32)
+    back_gu = back_gu.reshape(size, n_in, 2, copies, n_ff)
+    grad_gate_up = back_gu.transpose(1, 2, 3, 0, 4)
+    back_qkv = c.exchange(sum_qkv.reshape(size, n_in, 3 * wide)).astype(F32)
     if pairs:
         grad_qkv = back_qkv.reshape(half_group, 2, n_in, 3, hl, HD).transpose(2, 3, 1, 4, 0, 5)
     else:
@@ -362,9 +326,9 @@
         output.reshape(layer_input.shape),
         grad_input.reshape(layer_input.shape),
         grad_qkv.reshape(w_qkv.shape),
-        grad_out,
+        sum_out.astype(F32),
         grad_gate_up.reshape(w_gate_up.shape),
-        jnp.concatenate(sums_down, axis=0),
+        sum_down.astype(F32),
         grad_gains,
     )
 

time: 1220 us -> 919 us (0.75)
  waiting for transfers between devices: 590 us -> 344 us
  local copies, waits for them, and re-layouts: 196 us -> 155 us
  between operations: 3.94 us -> 16.6 us
    ppermute x134 -> x98, waiting for transfers between devices: 590 us -> 305 us  [send(): return lax.ppermute(v, ('rows', 'seq'), pairs)]
    all_gather x0 -> x4, waiting for transfers between devices: none -> 38.8 us  [gather(): lax.all_gather(block, ('rows', 'seq'), axis=0, tiled=True, axis_index_gro...]
    ppermute x134 -> x98, starting transfers between devices: 83.4 us -> 73.9 us  [send(): return lax.ppermute(v, ('rows', 'seq'), pairs)]
    dot_general x6 -> x4, matrix products: 56.1 us -> 49.8 us  [dot_tn(): lax.dot_general(a, b, (((0,), (0,)), ((), ())), preferred_element_type=F32)]
    unnamed x230 -> x180, local copies, waits for them, and re-layouts: 43.1 us -> 46.4 us
    dot_general x7 -> x6, matrix products: 54.8 us -> 51.6 us  [dot_nn(): lax.dot_general(a, b, (((1,), (0,)), ((), ())), preferred_element_type=F32)]
    dot_general x7 -> x6, matrix products: 57.9 us -> 59 us  [dot_nt(): lax.dot_general(a, b, (((1,), (1,)), ((), ())), preferred_element_type=F32)]
  transfers between devices with their start and end apart: 134 -> 106, of which waited for: 59 -> 46; matrix products, arithmetic and copies ran while one was open for 33% -> 46% of each run, Pallas kernels for 0% -> 0%
where the time goes in v3:
time: 919 us
  waiting for transfers between devices  344 us (37%)
  matrix products  209 us (23%)
  local copies, waits for them, and re-layouts  155 us (17%)
  other arithmetic  120 us (13%)
  starting transfers between devices  74.5 us (8%)
  between operations  16.6 us (2%)
    ppermute x98, waiting for transfers between devices, send(): return lax.ppermute(v, ('rows', 'seq'), pairs)  305 us
    ppermute x98, starting transfers between devices, send(): return lax.ppermute(v, ('rows', 'seq'), pairs)  73.9 us
    dot_general x6, matrix products, dot_nt(): lax.dot_general(a, b, (((1,), (1,)), ((), ())), preferred_element_type=F32)  59 us
    dot_general x6, matrix products, dot_nn(): lax.dot_general(a, b, (((1,), (0,)), ((), ())), preferred_element_type=F32)  51.6 us
    dot_general x4, matrix products, dot_tn(): lax.dot_general(a, b, (((0,), (0,)), ((), ())), preferred_element_type=F32)  49.8 us
    unnamed x180, local copies, waits for them, and re-layouts  46.4 us
    all_gather x4, waiting for transfers between devices, gather(): lax.all_gather(block, ('rows', 'seq'), axis=0, tiled=True, axis_index_gro...  38.8 us
    cos x2, other arithmetic, rope_tables(): return (jnp.cos(angles)[:, None, :], jnp.sin(angles)[:, None, :])  19.9 us
  transfers between devices with their start and end apart: 106, of which 46 were waited for; matrix products, arithmetic and copies ran while one was open for 46% of the time, Pallas kernels for 0%

profile of v3, /device:TPU:0, one launch (start us, length us, event | category | flops | bytes accessed | tf_op | source)
XLA Modules:
  0.0 918.9 jit_solution(7274593620476281369)
XLA Ops:
  50.6 11.1 %collective-permute-done.11 = s32[1,2]{1,0:T(1,128)S(1)} collective-permute-done((s32[1,2]{1,0:T(1,128)S(1)}, s32[1,2]{1,0:T(1,128)S(1)}, u32[]{:S(2)}, u32[]{:S(2)}) %collective-permute-start.11) | collective-permute-done | bytes 40 | tf_op jit(solution)/shard_map/ppermute | solution.py:71
  62.9 15.5 %fusion.84 = (f32[2,2,2,256,128]{3,2,1,0,4:T(2,128)S(1)}, f32[2,2,2,256,128]{3,2,1,0,4:T(2,128)}) fusion(f32[2,2,2,256,64]{3,2,1,0,4:T(2,128)S(1)} %broadcast_multiply_fusion.1), kind=kLoop, calls=%fused_computation.192 | loop fusion | flops 262144 | bytes 2621440 | tf_op jit(solution)/shard_map/cos | solution.py:19
  105.9 10.5 %fusion.129 = f32[2048,768]{0,1:T(8,128)S(1)} fusion(bf16[2048,2048]{1,0:T(8,128)(2,1)} %constant_dynamic-update-slice_fusion, bf16[2048,768]{1,0:T(8,128)(2,1)} %all-gather.5.cloned.1.call-done), kind=kOutput, calls=%fused_computation.333 | convolution fusion | flops 6442450944 | bytes 17825792 | tf_op jit(solution)/shard_map/dot_general | solution.py:29
  117.1 12.7 %collective-permute-done.35 = bf16[2,2,64,2048]{3,2,1,0:T(8,128)(2,1)} collective-permute-done((bf16[2,2,64,2048]{3,2,1,0:T(8,128)(2,1)}, bf16[2,2,64,2048]{3,2,1,0:T(8,128)(2,1)}, u32[]{:S(2)}, u32[]{:S(2)}) %collective-permute-start.35) | collective-permute-done | bytes 1048608 | tf_op jit(solution)/shard_map/ppermute | solution.py:71
  136.0 20.9 %collective-permute-done.36 = bf16[1,4,64,2048]{3,2,1,0:T(8,128)(2,1)S(1)} collective-permute-done((bf16[1,4,64,2048]{3,2,1,0:T(8,128)(2,1)S(1)}, bf16[1,4,64,2048]{3,2,1,0:T(8,128)(2,1)S(1)}, u32[]{:S(2)}, u32[]{:S(2)}) %collective-permute-start.36) | collective-permute-done | bytes 1048608 | tf_op jit(solution)/shard_map/ppermute | solution.py:71
  202.4 12.1 %fusion.128 = (f32[2,2,1024]{2,1,0:T(2,128)S(1)}, f32[2,2,1024,1024]{2,3,1,0:T(8,128)}) fusion(pred[2,1024,1024]{1,2,0:T(8,128)(4,1)} %compare_and_fusion, bf16[2,1024,2,128]{1,3,2,0:T(8,128)(2,1)S(1)} %reshape.441, bf16[2,1024,2,128]{1,3,2,0:T(8,128)(2,1)S(1)} %reshape.444), kind=kOutput, calls=%fused_computation.332 | convolution fusion | flops 1090520064 | bytes 20987904 | tf_op jit(solution)/shard_map/sub | solution.py:222
  241.8 10.5 %collective-permute-done.23 = bf16[128,2048]{1,0:T(8,128)(2,1)S(1)} collective-permute-done((bf16[128,2048]{1,0:T(8,128)(2,1)S(1)}, bf16[128,2048]{1,0:T(8,128)(2,1)S(1)}, u32[]{:S(2)}, u32[]{:S(2)}) %collective-permute-start.23) | collective-permute-done | bytes 524320 | tf_op jit(solution)/shard_map/ppermute | solution.py:71
  280.9 22.5 %collective-permute-done.27 = bf16[256,2048]{1,0:T(8,128)(2,1)S(1)} collective-permute-done((bf16[256,2048]{1,0:T(8,128)(2,1)S(1)}, bf16[256,2048]{1,0:T(8,128)(2,1)S(1)}, u32[]{:S(2)}, u32[]{:S(2)}) %collective-permute-start.27) | collective-permute-done | bytes 1048608 | tf_op jit(solution)/shard_map/ppermute | solution.py:71
  323.9 25.0 %fusion.130 = f32[2048,2048]{0,1:T(8,128)} fusion(bf16[2048,2048]{1,0:T(8,128)(2,1)} %constant_dynamic-update-slice_fusion.17, bf16[2048,2048]{1,0:T(8,128)(2,1)} %all-gather.9.cloned.1.call-done), kind=kOutput, calls=%fused_computation.334 | convolution fusion | flops 17179869184 | bytes 33554432 | tf_op jit(solution)/shard_map/dot_general | solution.py:29
  358.1 38.8 %all-gather.11.cloned.1.call-done = bf16[1024,2048]{1,0:T(8,128)(2,1)} async-done(((bf16[256,2048]{1,0:T(8,128)(2,1)}), bf16[1024,2048]{1,0:T(8,128)(2,1)}) %all-gather.11.cloned.1.call-update) | async-done | bytes 4194320 | tf_op jit(solution)/shard_map/all_gather | solution.py:77
  418.2 10.5 %collective-permute-done.44 = bf16[128,2048]{1,0:T(8,128)(2,1)S(1)} collective-permute-done((bf16[128,2048]{1,0:T(8,128)(2,1)S(1)}, bf16[128,2048]{1,0:T(8,128)(2,1)S(1)}, u32[]{:S(2)}, u32[]{:S(2)}) %collective-permute-start.44) | collective-permute-done | bytes 524320 | tf_op jit(solution)/shard_map/ppermute | solution.py:71
  451.8 12.3 %fusion.27 = (f32[2048]{0:T(1024)}, f32[256]{0:T(256)S(1)}) fusion(f32[256,2048]{1,0:T(8,128)S(1)} %get-tuple-element.37, bf16[1,256,2048]{2,1,0:T(8,128)(2,1)S(1)} %copy-done.11, f32[256]{0:T(256)S(1)} %get-tuple-element.134, f32[2048]{0:T(1024)S(1)} %bitcast.333), kind=kLoop, calls=%fused_computation.51 | loop fusion | flops 3667712 | bytes 3164160 | tf_op jit(solution)/shard_map/reduce_sum | solution.py:52
  466.7 21.6 %collective-permute-done.48 = bf16[256,2048]{1,0:T(8,128)(2,1)S(1)} collective-permute-done((bf16[256,2048]{1,0:T(8,128)(2,1)S(1)}, bf16[256,2048]{1,0:T(8,128)(2,1)S(1)}, u32[]{:S(2)}, u32[]{:S(2)}) %collective-permute-start.48) | collective-permute-done | bytes 1048608 | tf_op jit(solution)/shard_map/ppermute | solution.py:71
  507.5 10.5 %convolution_convert_fusion = bf16[1024,2048]{1,0:T(8,128)(2,1)} fusion(bf16[2048,1024]{0,1:T(8,128)(2,1)S(1)} %copy-done.22, bf16[2048,2048]{1,0:T(8,128)(2,1)S(1)} %constant_dynamic-update-slice_fusion.26), kind=kOutput, calls=%fused_computation.31 | convolution fusion | flops 8592031744 | bytes 16777216 | tf_op jit(solution)/shard_map/dot_general | solution.py:37
  518.1 20.9 %multiply_convert_fusion.1 = (bf16[2048,1024]{0,1:T(8,128)(2,1)S(1)}, bf16[2048,1024]{0,1:T(8,128)(2,1)}) fusion(f32[2048,2048]{0,1:T(8,128)} %fusion.130, bf16[2048,2048]{1,0:T(8,128)(2,1)} %copy-done.44, bf16[1024,2048]{1,0:T(8,128)(2,1)} %all-gather.11.cloned.1.call-done), kind=kOutput, calls=%fused_computation.12 | convolution fusion | flops 8617197568 | bytes 37748736 | tf_op jit(solution)/shard_map/dot_general | solution.py:33
  539.0 12.0 %fusion.18 = bf16[1024,2048]{1,0:T(8,128)(2,1)S(1)} fusion(bf16[2048,2048]{1,0:T(8,128)(2,1)} %all-gather.9.cloned.1.call-done, bf16[2048,1024]{0,1:T(8,128)(2,1)} %get-tuple-element.43, bf16[2048,1024]{0,1:T(8,128)(2,1)S(1)} %get-tuple-element.42), kind=kOutput, calls=%fused_computation.35 | convolution fusion | flops 8600420352 | bytes 20971520 | tf_op jit(solution)/shard_map/dot_general | solution.py:33
  553.0 12.4 %fusion.9 = f32[1024,2048]{1,0:T(8,128)S(1)} fusion(bf16[2048,2048]{1,0:T(8,128)(2,1)} %all-gather.9.cloned.1.call-done, bf16[2048,1024]{0,1:T(8,128)(2,1)} %get-tuple-element.43, bf16[2048,1024]{0,1:T(8,128)(2,1)S(1)} %get-tuple-element.42), kind=kOutput, calls=%fused_computation.24 | convolution fusion | flops 8598323200 | bytes 25165824 | tf_op jit(solution)/shard_map/dot_general | solution.py:33
  587.3 21.2 %fusion.7 = bf16[2048,2048]{1,0:T(8,128)(2,1)} fusion(bf16[2048,2048]{1,0:T(8,128)(2,1)} %constant_dynamic-update-slice_fusion.17, bf16[2048,1024]{0,1:T(8,128)(2,1)S(1)} %get-tuple-element.42, bf16[2048,1024]{0,1:T(8,128)(2,1)S(1)} %copy-done.64), kind=kOutput, calls=%fused_computation.22 | convolution fusion | flops 17200840704 | bytes 25165824 | tf_op jit(solution)/shard_map/dot_general | solution.py:37
  619.1 21.1 %collective-permute-done.66 = bf16[256,2048]{1,0:T(8,128)(2,1)S(1)} collective-permute-done((bf16[256,2048]{1,0:T(8,128)(2,1)S(1)}, bf16[256,2048]{1,0:T(8,128)(2,1)S(1)}, u32[]{:S(2)}, u32[]{:S(2)}) %collective-permute-start.66) | collective-permute-done | bytes 1048608 | tf_op jit(solution)/shard_map/ppermute | solution.py:71
  666.1 11.7 %multiply_reduce_fusion = (f32[2,2,1024]{2,1,0:T(2,128)S(1)}, f32[2,2,1024,1024]{2,3,1,0:T(8,128)}) fusion(f32[2,2,1024,1024]{2,3,1,0:T(8,128)} %get-tuple-element.136, f32[2,2,1024]{2,1,0:T(2,128)S(1)} %copy-done.52, bf16[2,1024,2,128]{3,1,2,0:T(8,128)(2,1)S(1)} %bitcast.317, bf16[2,1024,2,128]{1,3,2,0:T(8,128)(2,1)} %reshape.436), kind=kOutput, calls=%fused_computation.2 | convolution fusion | flops 1086320640 | bytes 35684352 | tf_op jit(solution)/shard_map/rqhd,rkhd->rhqk/dot_general | solution.py:281
  677.8 12.7 %multiply_convert_fusion = bf16[2,2,1024,1024]{2,3,1,0:T(8,128)(2,1)S(1)} fusion(f32[2,2,1024,1024]{2,3,1,0:T(8,128)} %get-tuple-element.138, f32[2,2,1024]{2,1,0:T(2,128)S(1)} %get-tuple-element.137, f32[2,2,1024,1024]{2,3,1,0:T(8,128)} %get-tuple-element.136, f32[2,2,1024]{2,1,0:T(2,128)S(1)} %copy-done.52), kind=kLoop, calls=%fused_computation.1 | loop fusion | flops 16777216 | bytes 41975808 | tf_op jit(solution)/shard_map/convert_element_type | solution.py:284
  765.3 11.4 %convolution_convert_fusion.4 = bf16[2048,768]{1,0:T(8,128)(2,1)} fusion(bf16[2048,2048]{1,0:T(8,128)(2,1)} %constant_dynamic-update-slice_fusion, bf16[2048,768]{0,1:T(8,128)(2,1)} %pad_maximum_fusion.4), kind=kOutput, calls=%fused_computation.36 | convolution fusion | flops 6444023808 | bytes 14680064 | tf_op jit(solution)/shard_map/dot_general | solution.py:37
  848.7 16.3 %collective-permute-done.91 = bf16[2,2,64,2048]{3,2,1,0:T(8,128)(2,1)} collective-permute-done((bf16[2,2,64,2048]{3,2,1,0:T(8,128)(2,1)}, bf16[2,2,64,2048]{3,2,1,0:T(8,128)(2,1)}, u32[]{:S(2)}, u32[]{:S(2)}) %collective-permute-start.91) | collective-permute-done | bytes 1048608 | tf_op jit(solution)/shard_map/ppermute | solution.py:71
  870.7 10.9 %collective-permute-done.85 = bf16[128,2048]{1,0:T(8,128)(2,1)S(1)} collective-permute-done((bf16[128,2048]{1,0:T(8,128)(2,1)}, bf16[128,2048]{1,0:T(8,128)(2,1)S(1)}, u32[]{:S(2)}, u32[]{:S(2)}) %collective-permute-start.85) | collective-permute-done | bytes 524320 | tf_op jit(solution)/shard_map/ppermute | solution.py:71
  (594 shorter events, 517.4 us)
Async XLA Ops:
  7.2 98.7 %all-gather.5.cloned.1.call-start = ((), (), s32[]{:S(2)}) async-start(), calls=%async_computation.4 | async-start | bytes 3932160 | tf_op jit(solution)/shard_map/all_gather | solution.py:77
  36.6 190.1 %all-gather.7.cloned.1.call-start = ((), (), s32[]{:S(2)}) async-start(), calls=%async_computation.5 | async-start | bytes 1310720 | tf_op jit(solution)/shard_map/all_gather | solution.py:77
  36.7 47.4 %collective-permute-start = (bf16[256,2048]{1,0:T(8,128)(2,1)}, bf16[256,2048]{1,0:T(8,128)(2,1)}, u32[]{:S(2)}, u32[]{:S(2)}) collective-permute-start(bf16[256,2048]{1,0:T(8,128)(2,1)} %bitcast), channel_id=1, source_target_pairs={{0,2},{1,3},{2,0},{3,1},{4,6},{5,7},{6,4},{7,5},{8,10},{9,11},{10,... | collective-permute-start | bytes 3145736 | tf_op jit(solution)/shard_map/ppermute | solution.py:71
  38.2 43.8 %collective-permute-start.1 = (bf16[256,2048]{1,0:T(8,128)(2,1)}, bf16[256,2048]{1,0:T(8,128)(2,1)}, u32[]{:S(2)}, u32[]{:S(2)}) collective-permute-start(bf16[256,2048]{1,0:T(8,128)(2,1)} %bitcast), channel_id=1, source_target_pairs={{0,4},{1,5},{2,6},{3,7},{4,0},{5,1},{6,2},{7,3},{8,12},{9,13},{10,... | collective-permute-start | bytes 3145736 | tf_op jit(solution)/shard_map/ppermute | solution.py:71
  39.7 58.5 %collective-permute-start.4 = (bf16[256,2048]{1,0:T(8,128)(2,1)}, bf16[256,2048]{1,0:T(8,128)(2,1)}, u32[]{:S(2)}, u32[]{:S(2)}) collective-permute-start(bf16[256,2048]{1,0:T(8,128)(2,1)} %bitcast), channel_id=1, source_target_pairs={{0,1},{1,0},{2,3},{3,2},{4,5},{5,4},{6,7},{7,6},{8,9},{9,8},{10,11... | collective-permute-start | bytes 3145736 | tf_op jit(solution)/shard_map/ppermute | solution.py:71
  40.3 283.6 %all-gather.9.cloned.1.call-start = ((), (), s32[]{:S(2)}) async-start(), calls=%async_computation.6 | async-start | bytes 10485760 | tf_op jit(solution)/shard_map/all_gather | solution.py:77
  103.9 25.9 %collective-permute-start.35 = (bf16[2,2,64,2048]{3,2,1,0:T(8,128)(2,1)}, bf16[2,2,64,2048]{3,2,1,0:T(8,128)(2,1)}, u32[]{:S(2)}, u32[]{:S(2)}) collective-permute-start(bf16[2,2,64,2048]{3,2,1,0:T(8,128)(2,1)} %dynamic-slice_bitcast_fusion.4), channel_id=1, source_target_pairs={{0,2},{1,3},{2,0},{3,1},{4,6},{5,7},{6,4},{7,5},{8,10},{9,11},{10,... | collective-permute-start | bytes 3145736 | tf_op jit(solution)/shard_map/ppermute | solution.py:71
  135.1 31.6 %collective-permute-start.14 = (f32[2,2048]{1,0:T(2,128)S(1)}, f32[2,2048]{1,0:T(2,128)S(1)}, u32[]{:S(2)}, u32[]{:S(2)}) collective-permute-start(f32[2,2048]{1,0:T(2,128)S(1)} %add.328), channel_id=1, source_target_pairs={{0,4},{1,5},{2,6},{3,7},{4,0},{5,1},{6,2},{7,3},{8,12},{9,13},{10,... | collective-permute-start | bytes 49160 | tf_op jit(solution)/shard_map/ppermute | solution.py:71
  166.4 230.4 %all-gather.11.cloned.1.call-start = ((), (), s32[]{:S(2)}) async-start(), calls=%async_computation.7 | async-start | bytes 5242880 | tf_op jit(solution)/shard_map/all_gather | solution.py:77
  239.6 25.4 %collective-permute-start.25 = (bf16[128,2048]{1,0:T(8,128)(2,1)S(1)}, bf16[128,2048]{1,0:T(8,128)(2,1)S(1)}, u32[]{:S(2)}, u32[]{:S(2)}) collective-permute-start(bf16[128,2048]{1,0:T(8,128)(2,1)S(1)} %slice.638), channel_id=1, source_target_pairs={{0,2},{1,3},{2,0},{3,1},{4,6},{5,7},{6,4},{7,5},{8,10},{9,11},{10,... | collective-permute-start | bytes 1572872 | tf_op jit(solution)/shard_map/ppermute | solution.py:71
  279.7 25.0 %collective-permute-start.26 = (bf16[256,2048]{1,0:T(8,128)(2,1)S(1)}, bf16[256,2048]{1,0:T(8,128)(2,1)S(1)}, u32[]{:S(2)}, u32[]{:S(2)}) collective-permute-start(bf16[256,2048]{1,0:T(8,128)(2,1)S(1)} %get-tuple-element.39), channel_id=1, source_target_pairs={{0,2},{1,3},{2,0},{3,1},{4,6},{5,7},{6,4},{7,5},{8,10},{9,11},{10,... | collective-permute-start | bytes 3145736 | tf_op jit(solution)/shard_map/ppermute | solution.py:71
  306.7 458.5 %reduce-scatter.5.cloned.1.call-start = ((), (), s32[]{:S(2)}) async-start(), calls=%async_computation.8 | async-start | bytes 5242880 | tf_op jit(solution)/shard_map/reduce_scatter | solution.py:80
  518.0 247.2 %reduce-scatter.7.cloned.1.call-start = ((), (), s32[]{:S(2)}) async-start(), calls=%async_computation.9 | async-start | bytes 10485760 | tf_op jit(solution)/shard_map/reduce_scatter | solution.py:80
  570.6 38.0 %collective-permute-start.55 = (bf16[256,2048]{1,0:T(8,128)(2,1)}, bf16[256,2048]{1,0:T(8,128)(2,1)}, u32[]{:S(2)}, u32[]{:S(2)}) collective-permute-start(bf16[256,2048]{1,0:T(8,128)(2,1)} %get-tuple-element.64), channel_id=1, source_target_pairs={{0,1},{1,0},{2,3},{3,2},{4,5},{5,4},{6,7},{7,6},{8,9},{9,8},{10,11... | collective-permute-start | bytes 3145736 | tf_op jit(solution)/shard_map/ppermute | solution.py:71
  571.5 37.1 %collective-permute-start.64 = (bf16[128,2048]{1,0:T(8,128)(2,1)}, bf16[128,2048]{1,0:T(8,128)(2,1)}, u32[]{:S(2)}, u32[]{:S(2)}) collective-permute-start(bf16[128,2048]{1,0:T(8,128)(2,1)} %slice.634), channel_id=1, source_target_pairs={{0,2},{1,3},{2,0},{3,1},{4,6},{5,7},{6,4},{7,5},{8,10},{9,11},{10,... | collective-permute-start | bytes 1572872 | tf_op jit(solution)/shard_map/ppermute | solution.py:71
  573.3 35.3 %collective-permute-start.57 = (bf16[128,2048]{1,0:T(8,128)(2,1)}, bf16[128,2048]{1,0:T(8,128)(2,1)}, u32[]{:S(2)}, u32[]{:S(2)}) collective-permute-start(bf16[128,2048]{1,0:T(8,128)(2,1)} %slice.635), channel_id=1, source_target_pairs={{0,4},{1,5},{2,6},{3,7},{4,0},{5,1},{6,2},{7,3},{8,12},{9,13},{10,... | collective-permute-start | bytes 1572872 | tf_op jit(solution)/shard_map/ppermute | solution.py:71
  608.5 193.3 %reduce-scatter.11.cloned.1.call-start = ((), (), s32[]{:S(2)}) async-start(), calls=%async_computation.11 | async-start | bytes 1310720 | tf_op jit(solution)/shard_map/reduce_scatter | solution.py:80
  742.2 105.3 %reduce-scatter.9.cloned.1.call-start = ((), (), s32[]{:S(2)}) async-start(), calls=%async_computation.10 | async-start | bytes 3932160 | tf_op jit(solution)/shard_map/reduce_scatter | solution.py:80
  806.6 61.7 %collective-permute-start.77 = (bf16[256,2048]{1,0:T(8,128)(2,1)}, bf16[256,2048]{1,0:T(8,128)(2,1)}, u32[]{:S(2)}, u32[]{:S(2)}) collective-permute-start(bf16[256,2048]{1,0:T(8,128)(2,1)} %get-tuple-element.63), channel_id=1, source_target_pairs={{0,1},{1,0},{2,3},{3,2},{4,5},{5,4},{6,7},{7,6},{8,9},{9,8},{10,11... | collective-permute-start | bytes 3145736 | tf_op jit(solution)/shard_map/ppermute | solution.py:71
  819.6 50.7 %collective-permute-start.79 = (bf16[128,2048]{1,0:T(8,128)(2,1)}, bf16[128,2048]{1,0:T(8,128)(2,1)S(1)}, u32[]{:S(2)}, u32[]{:S(2)}) collective-permute-start(bf16[128,2048]{1,0:T(8,128)(2,1)} %slice.633), channel_id=1, source_target_pairs={{0,4},{1,5},{2,6},{3,7},{4,0},{5,1},{6,2},{7,3},{8,12},{9,13},{10,... | collective-permute-start | bytes 1572872 | tf_op jit(solution)/shard_map/ppermute | solution.py:71
  822.4 48.4 %collective-permute-start.86 = (bf16[128,2048]{1,0:T(8,128)(2,1)}, bf16[128,2048]{1,0:T(8,128)(2,1)}, u32[]{:S(2)}, u32[]{:S(2)}) collective-permute-start(bf16[128,2048]{1,0:T(8,128)(2,1)} %slice.632), channel_id=1, source_target_pairs={{0,2},{1,3},{2,0},{3,1},{4,6},{5,7},{6,4},{7,5},{8,10},{9,11},{10,... | collective-permute-start | bytes 1572872 | tf_op jit(solution)/shard_map/ppermute | solution.py:71
  832.1 32.9 %collective-permute-start.91 = (bf16[2,2,64,2048]{3,2,1,0:T(8,128)(2,1)}, bf16[2,2,64,2048]{3,2,1,0:T(8,128)(2,1)}, u32[]{:S(2)}, u32[]{:S(2)}) collective-permute-start(bf16[2,2,64,2048]{3,2,1,0:T(8,128)(2,1)} %dynamic-slice_bitcast_fusion.1), channel_id=1, source_target_pairs={{0,2},{1,3},{2,0},{3,1},{4,6},{5,7},{6,4},{7,5},{8,10},{9,11},{10,... | collective-permute-start | bytes 3145736 | tf_op jit(solution)/shard_map/ppermute | solution.py:71
  844.8 25.9 %collective-permute-start.82 = (bf16[128,2048]{1,0:T(8,128)(2,1)}, bf16[128,2048]{1,0:T(8,128)(2,1)}, u32[]{:S(2)}, u32[]{:S(2)}) collective-permute-start(bf16[128,2048]{1,0:T(8,128)(2,1)} %fusion.71), channel_id=1, source_target_pairs={{0,4},{1,5},{2,6},{3,7},{4,0},{5,1},{6,2},{7,3},{8,12},{9,13},{10,... | collective-permute-start | bytes 1572872 | tf_op jit(solution)/shard_map/ppermute | solution.py:71
  868.3 26.1 %collective-permute-start.92 = (bf16[1,4,64,2048]{3,2,1,0:T(8,128)(2,1)S(1)}, bf16[1,4,64,2048]{3,2,1,0:T(8,128)(2,1)S(1)}, u32[]{:S(2)}, u32[]{:S(2)}) collective-permute-start(bf16[1,4,64,2048]{3,2,1,0:T(8,128)(2,1)S(1)} %dynamic-slice_bitcast_fusion), channel_id=1, source_target_pairs={{0,4},{1,5},{2,6},{3,7},{4,0},{5,1},{6,2},{7,3},{8,12},{9,13},{10,... | collective-permute-start | bytes 3145736 | tf_op jit(solution)/shard_map/ppermute | solution.py:71
  (149 other events, 1952.2 us)
Sparse Core Ops, SparseCore 0:
  36.8 64.6 all-gather.4
  103.0 26.6 all-gather.6
  166.5 149.8 all-gather.8
  317.9 78.9 all-gather.10
  518.2 74.7 reduce-scatter.4
  608.6 143.3 reduce-scatter.6
  754.3 27.8 reduce-scatter.10
  784.5 59.5 reduce-scatter.8

commit v4 on v3

--- a/solution.py
+++ b/solution.py
@@ -15,8 +15,10 @@
     half_width = HD // 2
     frequency = jnp.power(rope_base, -(jnp.arange(half_width, dtype=F32) * 2.0) / HD)
     angles = positions.astype(F32)[:, None] * frequency
-    angles = jnp.concatenate([angles, angles], axis=-1)
-    return jnp.cos(angles)[:, None, :], jnp.sin(angles)[:, None, :]
+    cosine, sine_table = lax.optimization_barrier((jnp.cos(angles), jnp.sin(angles)))
+    cosine = jnp.concatenate([cosine, cosine], axis=-1)
+    sine_table = jnp.concatenate([sine_table, sine_table], axis=-1)
+    return cosine[:, None, :], sine_table[:, None, :]
 
 
 def rotate(tensor, cosine, sine_table, turn_sign):
@@ -82,16 +84,16 @@
         )
 
     def exchange(self, parts, tokens=False):
-        swap = self.swap_tokens if tokens else self.swap
-        for bit in self.bits:
-            own = (self.g // bit) % 2
-            shape = parts.shape
-            parts = parts.reshape((self.size // (2 * bit), 2, bit) + shape[1:])
-            other = lax.dynamic_index_in_dim(parts, 1 - own, 1, keepdims=False)
-            axis = 2 if tokens else 0
-            moved = swap(other, bit, axis) if tokens else swap(other, bit)
-            parts = lax.dynamic_update_index_in_dim(parts, moved, 1 - own, 1).reshape(shape)
-        return parts
+        shape = parts.shape
+        swap = self.swap if not tokens else lambda v, j: self.swap_tokens(v, j, 1)
+        parts = parts.reshape((self.size // 2, 2) + shape[1:])
+        core, pair = self.g % 2, self.g // 2
+        other = swap(lax.dynamic_index_in_dim(parts, 1 - core, 1, keepdims=False), 1)
+        parts = lax.dynamic_update_index_in_dim(parts, other, 1 - core, 1)
+        moved = [swap(pick(parts, pair ^ j), 2 * j) for j in range(1, self.size // 2)]
+        for j, v in enumerate(moved):
+            parts = lax.dynamic_update_index_in_dim(parts, v, pair ^ (j + 1), 0)
+        return parts.reshape(shape)
 
     def swap_tokens(self, v, j, axis=0):
         pieces = jnp.split(self.swap(v, j), self.size, axis=axis)
@@ -162,26 +164,25 @@
     pairs = 2 * n_out == HD and 2 * hl == copies
     half_group = size // 2
 
+    lengths = doc_lengths.astype(jnp.int32)
+    lengths = [lengths] + [c.swap(lengths, j * c.seq) for j in range(1, part)]
+    lengths = jnp.concatenate(lengths, axis=0)
+
+    full_out = c.gather(w_out)
     if pairs:
         send_qkv = w_qkv.reshape(n_in, 3, 2, hl, half_group, HD).transpose(4, 2, 0, 1, 3, 5)
     else:
         send_qkv = w_qkv.reshape(n_in, 3, size, wide).transpose(2, 0, 1, 3)
     slab_qkv = c.exchange(send_qkv.reshape(size, n_in, 3 * wide)).reshape(size * n_in, 3 * wide)
-    x_full = c.gather_tokens(flat_in)
+    full_qkv = c.gather(after(slab_qkv, full_out))
+    x_full = c.gather_tokens(after(flat_in, lengths))
     send_gu = w_gate_up.reshape(n_in, 2, copies, size, n_ff).transpose(3, 0, 1, 2, 4)
-    send_gu = after(send_gu.reshape(size, n_in, 2 * ffl), slab_qkv)
+    send_gu = after(send_gu.reshape(size, n_in, 2 * ffl), x_full)
     slab_gu = c.exchange(send_gu).reshape(size * n_in, 2 * ffl)
-
-    full_out = c.gather(w_out)
-    full_qkv = c.gather(slab_qkv)
     full_gu = c.gather(after(slab_gu, full_qkv))
     full_down = c.gather(after(w_down, full_qkv))
 
-    lengths = doc_lengths.astype(jnp.int32)
-    other = [lengths]
-    for j in range(1, part):
-        other.append(c.swap(lengths, j * c.seq))
-    lengths = jnp.concatenate(other, axis=0)
+    lengths = after(lengths, x_full)
     doc_ends = jnp.cumsum(lengths, axis=1)
     near = [k % c.seq for k in c.order if k < c.seq]
     places = jnp.concatenate([(c.s ^ k) * tl + jnp.arange(tl, dtype=jnp.int32) for k in near])
@@ -205,7 +206,7 @@
         gains4 = norm_gains.reshape(4, size, wide).transpose(1, 0, 2)
     gains_own = pick(gains4, c.g)
 
-    mixed = dot_nn(x_full, full_qkv)
+    mixed = dot_nn(after(x_full, slab_gu), full_qkv)
     query_pre, key_pre = mixed[:, :wide], mixed[:, wide : 2 * wide]
     squares = jnp.stack([jnp.sum(query_pre * query_pre, -1), jnp.sum(key_pre * key_pre, -1)])
     scales = lax.rsqrt(c.sum_tokens(squares) / d + eps)
@@ -302,11 +303,12 @@
     grad_mixed = after(grad_mixed, sum_down, sum_gu)
     g_qkv = dot_tn(x_full, grad_mixed).astype(BF)
     sum_qkv = c.scatter(g_qkv)
-    grad_input = grad_hidden + c.scatter_tokens(grad_mixed, lambda v: dot_nt(v, full_qkv))
-
     back_gu = c.exchange(sum_gu.reshape(size, n_in, 2 * ffl)).astype(F32)
     back_gu = back_gu.reshape(size, n_in, 2, copies, n_ff)
     grad_gate_up = back_gu.transpose(1, 2, 3, 0, 4)
+    grad_mixed = after(grad_mixed, g_qkv, back_gu)
+    grad_input = grad_hidden + c.scatter_tokens(grad_mixed, lambda v: dot_nt(v, full_qkv))
+
     back_qkv = c.exchange(sum_qkv.reshape(size, n_in, 3 * wide)).astype(F32)
     if pairs:
         grad_qkv = back_qkv.reshape(half_group, 2, n_in, 3, hl, HD).transpose(2, 3, 1, 4, 0, 5)

time: 919 us -> 977 us (1.063)
  waiting for transfers between devices: 344 us -> 381 us
  other arithmetic: 120 us -> 92.5 us
  local copies, waits for them, and re-layouts: 155 us -> 178 us
  starting transfers between devices: 74.5 us -> 84.9 us
    reduce_scatter x4, waiting for transfers between devices: 0.01 us -> 28.9 us  [scatter(): lax.psum_scatter(parts, ('rows', 'seq'), scatter_dimension=0, tiled=True,...]
    cos x2 -> x0, other arithmetic: 19.9 us -> none  [rope_tables(): return (jnp.cos(angles)[:, None, :], jnp.sin(angles)[:, None, :])]
    reduce_sum x2, other arithmetic: 17.8 us -> 5.57 us  [norm_back(): gain_term = jnp.sum(upstream * tensor * inv_scale, axis=0)]
    ppermute x98 -> x102, starting transfers between devices: 73.9 us -> 84.6 us  [send(): return lax.ppermute(v, ('rows', 'seq'), pairs)]
    ppermute x98 -> x102, waiting for transfers between devices: 305 us -> 315 us  [send(): return lax.ppermute(v, ('rows', 'seq'), pairs)]
    unnamed x180 -> x192, local copies, waits for them, and re-layouts: 46.4 us -> 55.3 us
  transfers between devices with their start and end apart: 106 -> 110, of which waited for: 46 -> 47; matrix products, arithmetic and copies ran while one was open for 46% -> 39% of each run, Pallas kernels for 0% -> 0%
where the time goes in v4:
time: 977 us; the launch traced here: 969 us
  waiting for transfers between devices  381 us (39%)
  matrix products  215 us (22%)
  local copies, waits for them, and re-layouts  178 us (18%)
  other arithmetic  92.5 us (9%)
  starting transfers between devices  84.9 us (9%)
  between operations  16.5 us (2%)
    ppermute x102, waiting for transfers between devices, send(): return lax.ppermute(v, ('rows', 'seq'), pairs)  315 us
    ppermute x102, starting transfers between devices, send(): return lax.ppermute(v, ('rows', 'seq'), pairs)  84.6 us
    dot_general x6, matrix products, dot_nt(): lax.dot_general(a, b, (((1,), (1,)), ((), ())), preferred_element_type=F32)  63.4 us
    unnamed x192, local copies, waits for them, and re-layouts  55.3 us
    dot_general x4, matrix products, dot_tn(): lax.dot_general(a, b, (((0,), (0,)), ((), ())), preferred_element_type=F32)  52.5 us
    dot_general x6, matrix products, dot_nn(): lax.dot_general(a, b, (((1,), (0,)), ((), ())), preferred_element_type=F32)  49.5 us
    all_gather x4, waiting for transfers between devices, gather(): lax.all_gather(block, ('rows', 'seq'), axis=0, tiled=True, axis_index_gro...  37.6 us
    reduce_scatter x4, waiting for transfers between devices, scatter(): lax.psum_scatter(parts, ('rows', 'seq'), scatter_dimension=0, tiled=True,...  28.9 us
  transfers between devices with their start and end apart: 110, of which 47 were waited for; matrix products, arithmetic and copies ran while one was open for 39% of the time, Pallas kernels for 0%

profile of v4, /device:TPU:0, one launch (start us, length us, event | category | flops | bytes accessed | tf_op | source)
XLA Modules:
  0.0 969.0 jit_solution(3989697605339017773)
XLA Ops:
  27.4 16.9 %collective-permute-done.14 = bf16[2,64,768]{2,1,0:T(8,128)(2,1)S(1)} collective-permute-done((bf16[2,64,768]{2,1,0:T(8,128)(2,1)S(1)}, bf16[2,64,768]{2,1,0:T(8,128)(2,1)S(1)}, u32[]{:S(2)}, u32[]{:S(2)}) %collective-permute-start.14) | collective-permute-done | bytes 196640 | tf_op jit(solution)/shard_map/ppermute | solution.py:73
  91.7 10.8 %collective-permute-done.10 = bf16[2,64,2048]{2,1,0:T(8,128)(2,1)S(1)} collective-permute-done((bf16[2,64,2048]{2,1,0:T(8,128)(2,1)S(1)}, bf16[2,64,2048]{2,1,0:T(8,128)(2,1)S(1)}, u32[]{:S(2)}, u32[]{:S(2)}) %collective-permute-start.10) | collective-permute-done | bytes 524320 | tf_op jit(solution)/shard_map/ppermute | solution.py:73
  130.1 10.4 %fusion.124 = f32[2048,768]{0,1:T(8,128)S(1)} fusion(bf16[2048,2048]{1,0:T(8,128)(2,1)} %constant_dynamic-update-slice_fusion, bf16[2048,768]{1,0:T(8,128)(2,1)} %all-gather.7.cloned.1.call-done), kind=kOutput, calls=%fused_computation.340 | convolution fusion | flops 6442450944 | bytes 17825792 | tf_op jit(solution)/shard_map/dot_general | solution.py:31
  197.8 12.2 %fusion.123 = (f32[2,2,1024]{2,1,0:T(2,128)S(1)}, f32[2,2,1024,1024]{2,3,1,0:T(8,128)}) fusion(pred[2,1024,1024]{1,2,0:T(8,128)(4,1)} %compare_and_fusion, bf16[2,1024,2,128]{1,3,2,0:T(8,128)(2,1)} %reshape.375, bf16[2,1024,2,128]{1,3,2,0:T(8,128)(2,1)S(1)} %reshape.378), kind=kOutput, calls=%fused_computation.339 | convolution fusion | flops 1090520064 | bytes 20987904 | tf_op jit(solution)/shard_map/sub | solution.py:223
  239.9 10.5 %collective-permute-done.28 = bf16[128,2048]{1,0:T(8,128)(2,1)S(1)} collective-permute-done((bf16[128,2048]{1,0:T(8,128)(2,1)S(1)}, bf16[128,2048]{1,0:T(8,128)(2,1)S(1)}, u32[]{:S(2)}, u32[]{:S(2)}) %collective-permute-start.28) | collective-permute-done | bytes 524320 | tf_op jit(solution)/shard_map/ppermute | solution.py:73
  278.0 21.2 %collective-permute-done.32 = bf16[256,2048]{1,0:T(8,128)(2,1)S(1)} collective-permute-done((bf16[256,2048]{1,0:T(8,128)(2,1)S(1)}, bf16[256,2048]{1,0:T(8,128)(2,1)S(1)}, u32[]{:S(2)}, u32[]{:S(2)}) %collective-permute-start.32) | collective-permute-done | bytes 1048608 | tf_op jit(solution)/shard_map/ppermute | solution.py:73
  320.7 24.6 %fusion.125 = f32[2048,2048]{0,1:T(8,128)} fusion(bf16[2048,2048]{1,0:T(8,128)(2,1)} %constant_dynamic-update-slice_fusion.21, bf16[2048,2048]{1,0:T(8,128)(2,1)} %all-gather.9.cloned.1.call-done), kind=kOutput, calls=%fused_computation.341 | convolution fusion | flops 17179869184 | bytes 33554432 | tf_op jit(solution)/shard_map/dot_general | solution.py:31
  354.6 35.0 %all-gather.11.cloned.1.call-done = bf16[1024,2048]{1,0:T(8,128)(2,1)} async-done(((bf16[256,2048]{1,0:T(8,128)(2,1)}), bf16[1024,2048]{1,0:T(8,128)(2,1)}) %all-gather.11.cloned.1.call-update) | async-done | bytes 4194320 | tf_op jit(solution)/shard_map/all_gather | solution.py:79
  410.9 10.5 %collective-permute-done.46 = bf16[128,2048]{1,0:T(8,128)(2,1)S(1)} collective-permute-done((bf16[128,2048]{1,0:T(8,128)(2,1)S(1)}, bf16[128,2048]{1,0:T(8,128)(2,1)S(1)}, u32[]{:S(2)}, u32[]{:S(2)}) %collective-permute-start.46) | collective-permute-done | bytes 524320 | tf_op jit(solution)/shard_map/ppermute | solution.py:73
  448.6 21.6 %collective-permute-done.50 = bf16[256,2048]{1,0:T(8,128)(2,1)S(1)} collective-permute-done((bf16[256,2048]{1,0:T(8,128)(2,1)S(1)}, bf16[256,2048]{1,0:T(8,128)(2,1)S(1)}, u32[]{:S(2)}, u32[]{:S(2)}) %collective-permute-start.50) | collective-permute-done | bytes 1048608 | tf_op jit(solution)/shard_map/ppermute | solution.py:73
  489.3 10.5 %convolution_convert_fusion = bf16[1024,2048]{1,0:T(8,128)(2,1)} fusion(bf16[2048,1024]{0,1:T(8,128)(2,1)S(1)} %copy-done.30, bf16[2048,2048]{1,0:T(8,128)(2,1)S(1)} %constant_dynamic-update-slice_fusion.30), kind=kOutput, calls=%fused_computation.31 | convolution fusion | flops 8592031744 | bytes 16777216 | tf_op jit(solution)/shard_map/dot_general | solution.py:39
  499.8 20.1 %multiply_convert_fusion.1 = (bf16[2048,1024]{0,1:T(8,128)(2,1)S(1)}, bf16[2048,1024]{0,1:T(8,128)(2,1)}) fusion(f32[2048,2048]{0,1:T(8,128)} %fusion.125, bf16[2048,2048]{1,0:T(8,128)(2,1)} %copy-done.52, bf16[1024,2048]{1,0:T(8,128)(2,1)} %all-gather.11.cloned.1.call-done), kind=kOutput, calls=%fused_computation.12 | convolution fusion | flops 8617197568 | bytes 37748736 | tf_op jit(solution)/shard_map/dot_general | solution.py:35
  519.9 13.5 %fusion.18 = bf16[1024,2048]{1,0:T(8,128)(2,1)S(1)} fusion(bf16[2048,2048]{1,0:T(8,128)(2,1)} %all-gather.9.cloned.1.call-done, bf16[2048,1024]{0,1:T(8,128)(2,1)} %get-tuple-element.57, bf16[2048,1024]{0,1:T(8,128)(2,1)S(1)} %get-tuple-element.56), kind=kOutput, calls=%fused_computation.35 | convolution fusion | flops 8600420352 | bytes 20971520 | tf_op jit(solution)/shard_map/dot_general | solution.py:35
  536.2 12.6 %fusion.9 = f32[1024,2048]{1,0:T(8,128)S(1)} fusion(bf16[2048,2048]{1,0:T(8,128)(2,1)} %all-gather.9.cloned.1.call-done, bf16[2048,1024]{0,1:T(8,128)(2,1)} %get-tuple-element.57, bf16[2048,1024]{0,1:T(8,128)(2,1)} %copy-done.67), kind=kOutput, calls=%fused_computation.24 | convolution fusion | flops 8598323200 | bytes 25165824 | tf_op jit(solution)/shard_map/dot_general | solution.py:35
  556.6 10.4 %collective-permute-done.64 = bf16[128,2048]{1,0:T(8,128)(2,1)S(1)} collective-permute-done((bf16[128,2048]{1,0:T(8,128)(2,1)S(1)}, bf16[128,2048]{1,0:T(8,128)(2,1)S(1)}, u32[]{:S(2)}, u32[]{:S(2)}) %collective-permute-start.64) | collective-permute-done | bytes 524320 | tf_op jit(solution)/shard_map/ppermute | solution.py:73
  597.0 22.4 %collective-permute-done.68 = bf16[256,2048]{1,0:T(8,128)(2,1)S(1)} collective-permute-done((bf16[256,2048]{1,0:T(8,128)(2,1)S(1)}, bf16[256,2048]{1,0:T(8,128)(2,1)S(1)}, u32[]{:S(2)}, u32[]{:S(2)}) %collective-permute-start.68) | collective-permute-done | bytes 1048608 | tf_op jit(solution)/shard_map/ppermute | solution.py:73
  623.1 23.5 %fusion.7 = bf16[2048,2048]{1,0:T(8,128)(2,1)} fusion(bf16[2048,2048]{1,0:T(8,128)(2,1)S(1)} %bitcast.336, bf16[2048,1024]{0,1:T(8,128)(2,1)} %copy-done.67, bf16[2048,1024]{0,1:T(8,128)(2,1)} %get-tuple-element.57), kind=kOutput, calls=%fused_computation.22 | convolution fusion | flops 17200840704 | bytes 25165824 | tf_op jit(solution)/shard_map/dot_general | solution.py:39
  666.8 11.8 %multiply_reduce_fusion = (f32[2,2,1024]{2,1,0:T(2,128)S(1)}, f32[2,2,1024,1024]{2,3,1,0:T(8,128)}) fusion(f32[2,2,1024,1024]{2,3,1,0:T(8,128)} %get-tuple-element.160, f32[2,2,1024]{2,1,0:T(2,128)S(1)} %copy-done.57, bf16[2,1024,2,128]{3,1,2,0:T(8,128)(2,1)S(1)} %bitcast.315, bf16[2,1024,2,128]{1,3,2,0:T(8,128)(2,1)} %reshape.370), kind=kOutput, calls=%fused_computation.2 | convolution fusion | flops 1086320640 | bytes 35684352 | tf_op jit(solution)/shard_map/rqhd,rkhd->rhqk/dot_general | solution.py:282
  678.6 12.3 %multiply_convert_fusion = bf16[2,2,1024,1024]{2,3,1,0:T(8,128)(2,1)S(1)} fusion(f32[2,2,1024,1024]{2,3,1,0:T(8,128)} %get-tuple-element.162, f32[2,2,1024]{2,1,0:T(2,128)S(1)} %get-tuple-element.161, f32[2,2,1024,1024]{2,3,1,0:T(8,128)} %get-tuple-element.160, f32[2,2,1024]{2,1,0:T(2,128)S(1)} %copy-done.57), kind=kLoop, calls=%fused_computation.1 | loop fusion | flops 16777216 | bytes 41975808 | tf_op jit(solution)/shard_map/convert_element_type | solution.py:285
  760.9 28.9 %reduce-scatter.7.cloned.1.call-done = bf16[512,2048]{1,0:T(8,128)(2,1)} async-done(((bf16[2048,2048]{1,0:T(8,128)(2,1)}), bf16[512,2048]{1,0:T(8,128)(2,1)}) %reduce-scatter.7.cloned.1.call-update) | async-done | bytes 2097168 | tf_op jit(solution)/shard_map/reduce_scatter | solution.py:82
  789.8 11.8 %convolution_convert_fusion.4 = bf16[2048,768]{1,0:T(8,128)(2,1)} fusion(bf16[2048,2048]{1,0:T(8,128)(2,1)} %constant_dynamic-update-slice_fusion, bf16[2048,768]{0,1:T(8,128)(2,1)} %pad_maximum_fusion.4), kind=kOutput, calls=%fused_computation.36 | convolution fusion | flops 6444023808 | bytes 14680064 | tf_op jit(solution)/shard_map/dot_general | solution.py:39
  807.7 12.5 %collective-permute-done.80 = bf16[2,64,2048]{2,1,0:T(8,128)(2,1)S(1)} collective-permute-done((bf16[2,64,2048]{2,1,0:T(8,128)(2,1)S(1)}, bf16[2,64,2048]{2,1,0:T(8,128)(2,1)S(1)}, u32[]{:S(2)}, u32[]{:S(2)}) %collective-permute-start.80) | collective-permute-done | bytes 524320 | tf_op jit(solution)/shard_map/ppermute | solution.py:73
  875.2 12.7 %collective-permute-done.98 = f32[4,2048]{1,0:T(4,128)S(1)} collective-permute-done((f32[4,2048]{1,0:T(4,128)S(1)}, f32[4,2048]{1,0:T(4,128)S(1)}, u32[]{:S(2)}, u32[]{:S(2)}) %collective-permute-start.98) | collective-permute-done | bytes 32800 | tf_op jit(solution)/shard_map/ppermute | solution.py:73
  908.5 17.2 %collective-permute-done.90 = bf16[128,2048]{1,0:T(8,128)(2,1)} collective-permute-done((bf16[128,2048]{1,0:T(8,128)(2,1)}, bf16[128,2048]{1,0:T(8,128)(2,1)}, u32[]{:S(2)}, u32[]{:S(2)}) %collective-permute-start.90) | collective-permute-done | bytes 524320 | tf_op jit(solution)/shard_map/ppermute | solution.py:73
  (617 shorter events, 558.6 us)
Async XLA Ops:
  7.2 59.8 %all-gather.5.cloned.1.call-start = ((), (), s32[]{:S(2)}) async-start(), calls=%async_computation.4 | async-start | bytes 1310720 | tf_op jit(solution)/shard_map/all_gather | solution.py:79
  15.4 42.5 %collective-permute-start.1 = (bf16[256,2048]{1,0:T(8,128)(2,1)S(1)}, bf16[256,2048]{1,0:T(8,128)(2,1)}, u32[]{:S(2)}, u32[]{:S(2)}) collective-permute-start(bf16[256,2048]{1,0:T(8,128)(2,1)S(1)} %bitcast.294), channel_id=1, source_target_pairs={{0,2},{1,3},{2,0},{3,1},{4,6},{5,7},{6,4},{7,5},{8,10},{9,11},{10,... | collective-permute-start | bytes 3145736 | tf_op jit(solution)/shard_map/ppermute | solution.py:73
  17.5 36.1 %collective-permute-start.2 = (bf16[256,2048]{1,0:T(8,128)(2,1)S(1)}, bf16[256,2048]{1,0:T(8,128)(2,1)}, u32[]{:S(2)}, u32[]{:S(2)}) collective-permute-start(bf16[256,2048]{1,0:T(8,128)(2,1)S(1)} %bitcast.295), channel_id=1, source_target_pairs={{0,4},{1,5},{2,6},{3,7},{4,0},{5,1},{6,2},{7,3},{8,12},{9,13},{10,... | collective-permute-start | bytes 3145736 | tf_op jit(solution)/shard_map/ppermute | solution.py:73
  19.1 25.2 %collective-permute-start.14 = (bf16[2,64,768]{2,1,0:T(8,128)(2,1)S(1)}, bf16[2,64,768]{2,1,0:T(8,128)(2,1)S(1)}, u32[]{:S(2)}, u32[]{:S(2)}) collective-permute-start(bf16[2,64,768]{2,1,0:T(8,128)(2,1)S(1)} %dynamic-slice_bitcast_fusion.17), channel_id=1, source_target_pairs={{0,2},{1,3},{2,0},{3,1},{4,6},{5,7},{6,4},{7,5},{8,10},{9,11},{10,... | collective-permute-start | bytes 589832 | tf_op jit(solution)/shard_map/ppermute | solution.py:73
  19.7 110.4 %all-gather.7.cloned.1.call-start = ((), (), s32[]{:S(2)}) async-start(), calls=%async_computation.5 | async-start | bytes 3932160 | tf_op jit(solution)/shard_map/all_gather | solution.py:79
  27.3 47.3 %collective-permute-start.5 = (bf16[256,2048]{1,0:T(8,128)(2,1)S(1)}, bf16[256,2048]{1,0:T(8,128)(2,1)}, u32[]{:S(2)}, u32[]{:S(2)}) collective-permute-start(bf16[256,2048]{1,0:T(8,128)(2,1)S(1)} %bitcast.296), channel_id=1, source_target_pairs={{0,1},{1,0},{2,3},{3,2},{4,5},{5,4},{6,7},{7,6},{8,9},{9,8},{10,11... | collective-permute-start | bytes 3145736 | tf_op jit(solution)/shard_map/ppermute | solution.py:73
  67.0 253.7 %all-gather.9.cloned.1.call-start = ((), (), s32[]{:S(2)}) async-start(), calls=%async_computation.6 | async-start | bytes 10485760 | tf_op jit(solution)/shard_map/all_gather | solution.py:79
  160.9 228.6 %all-gather.11.cloned.1.call-start = ((), (), s32[]{:S(2)}) async-start(), calls=%async_computation.7 | async-start | bytes 5242880 | tf_op jit(solution)/shard_map/all_gather | solution.py:79
  276.4 25.1 %collective-permute-start.31 = (bf16[256,2048]{1,0:T(8,128)(2,1)S(1)}, bf16[256,2048]{1,0:T(8,128)(2,1)S(1)}, u32[]{:S(2)}, u32[]{:S(2)}) collective-permute-start(bf16[256,2048]{1,0:T(8,128)(2,1)S(1)} %get-tuple-element.53), channel_id=1, source_target_pairs={{0,2},{1,3},{2,0},{3,1},{4,6},{5,7},{6,4},{7,5},{8,10},{9,11},{10,... | collective-permute-start | bytes 3145736 | tf_op jit(solution)/shard_map/ppermute | solution.py:73
  303.8 457.0 %reduce-scatter.5.cloned.1.call-start = ((), (), s32[]{:S(2)}) async-start(), calls=%async_computation.8 | async-start | bytes 5242880 | tf_op jit(solution)/shard_map/reduce_scatter | solution.py:82
  409.6 24.5 %collective-permute-start.48 = (bf16[128,2048]{1,0:T(8,128)(2,1)S(1)}, bf16[128,2048]{1,0:T(8,128)(2,1)S(1)}, u32[]{:S(2)}, u32[]{:S(2)}) collective-permute-start(bf16[128,2048]{1,0:T(8,128)(2,1)S(1)} %slice.636), channel_id=1, source_target_pairs={{0,2},{1,3},{2,0},{3,1},{4,6},{5,7},{6,4},{7,5},{8,10},{9,11},{10,... | collective-permute-start | bytes 1572872 | tf_op jit(solution)/shard_map/ppermute | solution.py:73
  447.1 24.7 %collective-permute-start.49 = (bf16[256,2048]{1,0:T(8,128)(2,1)S(1)}, bf16[256,2048]{1,0:T(8,128)(2,1)S(1)}, u32[]{:S(2)}, u32[]{:S(2)}) collective-permute-start(bf16[256,2048]{1,0:T(8,128)(2,1)S(1)} %get-tuple-element.49), channel_id=1, source_target_pairs={{0,2},{1,3},{2,0},{3,1},{4,6},{5,7},{6,4},{7,5},{8,10},{9,11},{10,... | collective-permute-start | bytes 3145736 | tf_op jit(solution)/shard_map/ppermute | solution.py:73
  536.1 253.6 %reduce-scatter.7.cloned.1.call-start = ((), (), s32[]{:S(2)}) async-start(), calls=%async_computation.9 | async-start | bytes 10485760 | tf_op jit(solution)/shard_map/reduce_scatter | solution.py:82
  553.9 24.9 %collective-permute-start.66 = (bf16[128,2048]{1,0:T(8,128)(2,1)S(1)}, bf16[128,2048]{1,0:T(8,128)(2,1)S(1)}, u32[]{:S(2)}, u32[]{:S(2)}) collective-permute-start(bf16[128,2048]{1,0:T(8,128)(2,1)S(1)} %slice.634), channel_id=1, source_target_pairs={{0,2},{1,3},{2,0},{3,1},{4,6},{5,7},{6,4},{7,5},{8,10},{9,11},{10,... | collective-permute-start | bytes 1572872 | tf_op jit(solution)/shard_map/ppermute | solution.py:73
  596.4 25.0 %collective-permute-start.67 = (bf16[256,2048]{1,0:T(8,128)(2,1)S(1)}, bf16[256,2048]{1,0:T(8,128)(2,1)S(1)}, u32[]{:S(2)}, u32[]{:S(2)}) collective-permute-start(bf16[256,2048]{1,0:T(8,128)(2,1)S(1)} %get-tuple-element.46), channel_id=1, source_target_pairs={{0,2},{1,3},{2,0},{3,1},{4,6},{5,7},{6,4},{7,5},{8,10},{9,11},{10,... | collective-permute-start | bytes 3145736 | tf_op jit(solution)/shard_map/ppermute | solution.py:73
  620.3 29.2 %collective-permute-start.69 = (bf16[128,2048]{1,0:T(8,128)(2,1)}, bf16[128,2048]{1,0:T(8,128)(2,1)S(1)}, u32[]{:S(2)}, u32[]{:S(2)}) collective-permute-start(bf16[128,2048]{1,0:T(8,128)(2,1)} %slice.464), channel_id=1, source_target_pairs={{0,2},{1,3},{2,0},{3,1},{4,6},{5,7},{6,4},{7,5},{8,10},{9,11},{10,... | collective-permute-start | bytes 1572872 | tf_op jit(solution)/shard_map/ppermute | solution.py:73
  622.2 27.3 %collective-permute-start.70 = (bf16[128,2048]{1,0:T(8,128)(2,1)}, bf16[128,2048]{1,0:T(8,128)(2,1)S(1)}, u32[]{:S(2)}, u32[]{:S(2)}) collective-permute-start(bf16[128,2048]{1,0:T(8,128)(2,1)} %slice.465), channel_id=1, source_target_pairs={{0,4},{1,5},{2,6},{3,7},{4,0},{5,1},{6,2},{7,3},{8,12},{9,13},{10,... | collective-permute-start | bytes 1572872 | tf_op jit(solution)/shard_map/ppermute | solution.py:73
  646.6 256.1 %reduce-scatter.9.cloned.1.call-start = ((), (), s32[]{:S(2)}) async-start(), calls=%async_computation.10 | async-start | bytes 3932160 | tf_op jit(solution)/shard_map/reduce_scatter | solution.py:82
  801.6 131.7 %reduce-scatter.11.cloned.1.call-start = ((), (), s32[]{:S(2)}) async-start(), calls=%async_computation.11 | async-start | bytes 1310720 | tf_op jit(solution)/shard_map/reduce_scatter | solution.py:82
  873.0 30.7 %collective-permute-start.87 = (bf16[128,2048]{1,0:T(8,128)(2,1)}, bf16[128,2048]{1,0:T(8,128)(2,1)}, u32[]{:S(2)}, u32[]{:S(2)}) collective-permute-start(bf16[128,2048]{1,0:T(8,128)(2,1)} %get-tuple-element.110), channel_id=1, source_target_pairs={{0,2},{1,3},{2,0},{3,1},{4,6},{5,7},{6,4},{7,5},{8,10},{9,11},{10,... | collective-permute-start | bytes 1572872 | tf_op jit(solution)/shard_map/ppermute | solution.py:73
  895.8 32.3 %collective-permute-start.101 = (f32[4,2048]{1,0:T(4,128)S(1)}, f32[4,2048]{1,0:T(4,128)S(1)}, u32[]{:S(2)}, u32[]{:S(2)}) collective-permute-start(f32[4,2048]{1,0:T(4,128)S(1)} %add.372), channel_id=1, source_target_pairs={{0,16},{1,17},{2,18},{3,19},{4,20},{5,21},{6,22},{7,23},{8,24},{9,... | collective-permute-start | bytes 98312 | tf_op jit(solution)/shard_map/ppermute | solution.py:73
  898.9 46.8 %collective-permute-start.83 = (bf16[256,2048]{1,0:T(8,128)(2,1)}, bf16[256,2048]{1,0:T(8,128)(2,1)}, u32[]{:S(2)}, u32[]{:S(2)}) collective-permute-start(bf16[256,2048]{1,0:T(8,128)(2,1)} %get-tuple-element.77), channel_id=1, source_target_pairs={{0,1},{1,0},{2,3},{3,2},{4,5},{5,4},{6,7},{7,6},{8,9},{9,8},{10,11... | collective-permute-start | bytes 3145736 | tf_op jit(solution)/shard_map/ppermute | solution.py:73
  899.8 47.5 %collective-permute-start.85 = (bf16[128,2048]{1,0:T(8,128)(2,1)}, bf16[128,2048]{1,0:T(8,128)(2,1)}, u32[]{:S(2)}, u32[]{:S(2)}) collective-permute-start(bf16[128,2048]{1,0:T(8,128)(2,1)} %slice.633), channel_id=1, source_target_pairs={{0,4},{1,5},{2,6},{3,7},{4,0},{5,1},{6,2},{7,3},{8,12},{9,13},{10,... | collective-permute-start | bytes 1572872 | tf_op jit(solution)/shard_map/ppermute | solution.py:73
  906.2 41.1 %collective-permute-start.92 = (bf16[128,2048]{1,0:T(8,128)(2,1)}, bf16[128,2048]{1,0:T(8,128)(2,1)}, u32[]{:S(2)}, u32[]{:S(2)}) collective-permute-start(bf16[128,2048]{1,0:T(8,128)(2,1)} %slice.632), channel_id=1, source_target_pairs={{0,2},{1,3},{2,0},{3,1},{4,6},{5,7},{6,4},{7,5},{8,10},{9,11},{10,... | collective-permute-start | bytes 1572872 | tf_op jit(solution)/shard_map/ppermute | solution.py:73
  (158 other events, 2013.0 us)
Sparse Core Ops, SparseCore 0:
  19.8 28.1 all-gather.4
  67.1 62.9 all-gather.6
  161.0 148.0 all-gather.8
  310.6 78.9 all-gather.10
  536.3 74.7 reduce-scatter.4
  646.8 142.9 reduce-scatter.6
  801.7 61.0 reduce-scatter.8
  865.0 27.1 reduce-scatter.10

commit v5 on v4

--- a/solution.py
+++ b/solution.py
@@ -168,18 +168,19 @@
     lengths = [lengths] + [c.swap(lengths, j * c.seq) for j in range(1, part)]
     lengths = jnp.concatenate(lengths, axis=0)
 
-    full_out = c.gather(w_out)
     if pairs:
         send_qkv = w_qkv.reshape(n_in, 3, 2, hl, half_group, HD).transpose(4, 2, 0, 1, 3, 5)
     else:
         send_qkv = w_qkv.reshape(n_in, 3, size, wide).transpose(2, 0, 1, 3)
     slab_qkv = c.exchange(send_qkv.reshape(size, n_in, 3 * wide)).reshape(size * n_in, 3 * wide)
-    full_qkv = c.gather(after(slab_qkv, full_out))
-    x_full = c.gather_tokens(after(flat_in, lengths))
+    full_qkv = c.gather(slab_qkv)
+    full_out = c.gather(w_out)
+    x_full = c.gather_tokens(after(flat_in, slab_qkv, lengths))
     send_gu = w_gate_up.reshape(n_in, 2, copies, size, n_ff).transpose(3, 0, 1, 2, 4)
     send_gu = after(send_gu.reshape(size, n_in, 2 * ffl), x_full)
     slab_gu = c.exchange(send_gu).reshape(size * n_in, 2 * ffl)
-    full_gu = c.gather(after(slab_gu, full_qkv))
+    x_full, slab_gu = lax.optimization_barrier((x_full, slab_gu))
+    full_gu = c.gather(slab_gu)
     full_down = c.gather(after(w_down, full_qkv))
 
     lengths = after(lengths, x_full)
@@ -206,7 +207,7 @@
         gains4 = norm_gains.reshape(4, size, wide).transpose(1, 0, 2)
     gains_own = pick(gains4, c.g)
 
-    mixed = dot_nn(after(x_full, slab_gu), full_qkv)
+    mixed = dot_nn(x_full, full_qkv)
     query_pre, key_pre = mixed[:, :wide], mixed[:, wide : 2 * wide]
     squares = jnp.stack([jnp.sum(query_pre * query_pre, -1), jnp.sum(key_pre * key_pre, -1)])
     scales = lax.rsqrt(c.sum_tokens(squares) / d + eps)
@@ -271,11 +272,12 @@
     grad_inner = dot_nt(grad_branch2, full_down)
     grad_gate = grad_inner * up * sig * (1.0 + gate * (1.0 - sig))
     grad_gu = jnp.concatenate([grad_gate, grad_inner * (gate * sig)], axis=1).astype(BF)
+    grad_hidden = upstream + c.scatter_tokens(grad_gu, lambda v: dot_nt(v, full_gu))
     g_gu = dot_tn(hidden_low, grad_gu).astype(BF)
     sum_gu = c.scatter(g_gu)
-    grad_hidden = upstream + c.scatter_tokens(grad_gu, lambda v: dot_nt(v, full_gu))
     grad_branch, gain_attn = norm_back(branch, branch_scale, norm_gains[2], grad_hidden)
     grad_branch = c.gather_tokens(grad_branch.astype(BF))
+    grad_branch = after(grad_branch, sum_down)
     g_out = dot_tn(attended, grad_branch).astype(BF)
     sum_out = c.scatter(g_out)
     grad_att = by_rows(from_out(dot_nt(grad_branch, full_out).astype(BF)))
@@ -303,12 +305,11 @@
     grad_mixed = after(grad_mixed, sum_down, sum_gu)
     g_qkv = dot_tn(x_full, grad_mixed).astype(BF)
     sum_qkv = c.scatter(g_qkv)
+    grad_input = grad_hidden + c.scatter_tokens(grad_mixed, lambda v: dot_nt(v, full_qkv))
+
     back_gu = c.exchange(sum_gu.reshape(size, n_in, 2 * ffl)).astype(F32)
     back_gu = back_gu.reshape(size, n_in, 2, copies, n_ff)
     grad_gate_up = back_gu.transpose(1, 2, 3, 0, 4)
-    grad_mixed = after(grad_mixed, g_qkv, back_gu)
-    grad_input = grad_hidden + c.scatter_tokens(grad_mixed, lambda v: dot_nt(v, full_qkv))
-
     back_qkv = c.exchange(sum_qkv.reshape(size, n_in, 3 * wide)).astype(F32)
     if pairs:
         grad_qkv = back_qkv.reshape(half_group, 2, n_in, 3, hl, HD).transpose(2, 3, 1, 4, 0, 5)

time: 977 us -> 926 us (0.948)
  waiting for transfers between devices: 381 us -> 355 us
  local copies, waits for them, and re-layouts: 178 us -> 159 us
    reduce_scatter x4, waiting for transfers between devices: 28.9 us -> 0.01 us  [scatter(): lax.psum_scatter(parts, ('rows', 'seq'), scatter_dimension=0, tiled=True,...]
    unnamed x192 -> x178, local copies, waits for them, and re-layouts: 55.3 us -> 40.4 us
    reshape x0 -> x2, local copies, waits for them, and re-layouts: none -> 10.8 us  [per_device(): grad_gate_up.reshape(w_gate_up.shape)]
    reduce_sum x2, other arithmetic: 5.57 us -> 16.1 us  [norm_back(): gain_term = jnp.sum(upstream * tensor * inv_scale, axis=0)]
  transfers between devices with their start and end apart: 110 -> 110, of which waited for: 47 -> 49; matrix products, arithmetic and copies ran while one was open for 39% -> 45% of each run, Pallas kernels for 0% -> 0%
where the time goes in v5:
time: 926 us; the launch traced here: 925 us
  waiting for transfers between devices  355 us (38%)
  matrix products  213 us (23%)
  local copies, waits for them, and re-layouts  159 us (17%)
  other arithmetic  98.9 us (11%)
  starting transfers between devices  82.5 us (9%)
  between operations  16.5 us (2%)
    ppermute x102, waiting for transfers between devices, send(): return lax.ppermute(v, ('rows', 'seq'), pairs)  323 us
    ppermute x102, starting transfers between devices, send(): return lax.ppermute(v, ('rows', 'seq'), pairs)  81.7 us
    dot_general x6, matrix products, dot_nt(): lax.dot_general(a, b, (((1,), (1,)), ((), ())), preferred_element_type=F32)  63.5 us
    dot_general x4, matrix products, dot_tn(): lax.dot_general(a, b, (((0,), (0,)), ((), ())), preferred_element_type=F32)  51.4 us
    dot_general x6, matrix products, dot_nn(): lax.dot_general(a, b, (((1,), (0,)), ((), ())), preferred_element_type=F32)  51.2 us
    unnamed x178, local copies, waits for them, and re-layouts  40.4 us
    all_gather x4, waiting for transfers between devices, gather(): lax.all_gather(block, ('rows', 'seq'), axis=0, tiled=True, axis_index_gro...  32.3 us
  transfers between devices with their start and end apart: 110, of which 49 were waited for; matrix products, arithmetic and copies ran while one was open for 45% of the time, Pallas kernels for 0%

profile of v5, /device:TPU:0, one launch (start us, length us, event | category | flops | bytes accessed | tf_op | source)
XLA Modules:
  0.0 924.9 jit_solution(6277627055708861745)
XLA Ops:
  44.8 11.9 %collective-permute-done.6 = bf16[256,2048]{1,0:T(8,128)(2,1)} collective-permute-done((bf16[256,2048]{1,0:T(8,128)(2,1)S(1)}, bf16[256,2048]{1,0:T(8,128)(2,1)}, u32[]{:S(2)}, u32[]{:S(2)}) %collective-permute-start.6) | collective-permute-done | bytes 1048608 | tf_op jit(solution)/shard_map/ppermute | solution.py:73
  78.8 12.7 %collective-permute-done.14 = bf16[2,64,2048]{2,1,0:T(8,128)(2,1)} collective-permute-done((bf16[2,64,2048]{2,1,0:T(8,128)(2,1)}, bf16[2,64,2048]{2,1,0:T(8,128)(2,1)}, u32[]{:S(2)}, u32[]{:S(2)}) %collective-permute-start.14) | collective-permute-done | bytes 524320 | tf_op jit(solution)/shard_map/ppermute | solution.py:73
  97.9 10.8 %collective-permute-done.15 = bf16[2,64,2048]{2,1,0:T(8,128)(2,1)} collective-permute-done((bf16[2,64,2048]{2,1,0:T(8,128)(2,1)}, bf16[2,64,2048]{2,1,0:T(8,128)(2,1)}, u32[]{:S(2)}, u32[]{:S(2)}) %collective-permute-start.15) | collective-permute-done | bytes 524320 | tf_op jit(solution)/shard_map/ppermute | solution.py:73
  128.3 10.4 %fusion.124 = f32[2048,768]{0,1:T(8,128)S(1)} fusion(bf16[2048,2048]{1,0:T(8,128)(2,1)} %copy-done.47, bf16[2048,768]{1,0:T(8,128)(2,1)} %all-gather.5.cloned.1.call-done), kind=kOutput, calls=%fused_computation.340 | convolution fusion | flops 6442450944 | bytes 17825792 | tf_op jit(solution)/shard_map/dot_general | solution.py:31
  194.5 12.0 %fusion.123 = (f32[2,2,1024]{2,1,0:T(2,128)S(1)}, f32[2,2,1024,1024]{2,3,1,0:T(8,128)}) fusion(pred[2,1024,1024]{1,2,0:T(8,128)(4,1)} %compare_and_fusion, bf16[2,1024,2,128]{1,3,2,0:T(8,128)(2,1)} %reshape.378, bf16[2,1024,2,128]{1,3,2,0:T(8,128)(2,1)S(1)} %reshape.381), kind=kOutput, calls=%fused_computation.339 | convolution fusion | flops 1090520064 | bytes 20987904 | tf_op jit(solution)/shard_map/sub | solution.py:224
  235.7 10.5 %collective-permute-done.28 = bf16[128,2048]{1,0:T(8,128)(2,1)S(1)} collective-permute-done((bf16[128,2048]{1,0:T(8,128)(2,1)S(1)}, bf16[128,2048]{1,0:T(8,128)(2,1)S(1)}, u32[]{:S(2)}, u32[]{:S(2)}) %collective-permute-start.28) | collective-permute-done | bytes 524320 | tf_op jit(solution)/shard_map/ppermute | solution.py:73
  273.0 22.0 %collective-permute-done.32 = bf16[256,2048]{1,0:T(8,128)(2,1)S(1)} collective-permute-done((bf16[256,2048]{1,0:T(8,128)(2,1)S(1)}, bf16[256,2048]{1,0:T(8,128)(2,1)S(1)}, u32[]{:S(2)}, u32[]{:S(2)}) %collective-permute-start.32) | collective-permute-done | bytes 1048608 | tf_op jit(solution)/shard_map/ppermute | solution.py:73
  315.7 24.6 %fusion.125 = f32[2048,2048]{0,1:T(8,128)} fusion(bf16[2048,2048]{1,0:T(8,128)(2,1)} %constant_dynamic-update-slice_fusion.21, bf16[2048,2048]{1,0:T(8,128)(2,1)} %all-gather.9.cloned.1.call-done), kind=kOutput, calls=%fused_computation.341 | convolution fusion | flops 17179869184 | bytes 33554432 | tf_op jit(solution)/shard_map/dot_general | solution.py:31
  349.6 32.3 %all-gather.11.cloned.1.call-done = bf16[1024,2048]{1,0:T(8,128)(2,1)} async-done(((bf16[256,2048]{1,0:T(8,128)(2,1)}), bf16[1024,2048]{1,0:T(8,128)(2,1)}) %all-gather.11.cloned.1.call-update) | async-done | bytes 4194320 | tf_op jit(solution)/shard_map/all_gather | solution.py:79
  403.3 10.5 %collective-permute-done.46 = bf16[128,2048]{1,0:T(8,128)(2,1)S(1)} collective-permute-done((bf16[128,2048]{1,0:T(8,128)(2,1)S(1)}, bf16[128,2048]{1,0:T(8,128)(2,1)S(1)}, u32[]{:S(2)}, u32[]{:S(2)}) %collective-permute-start.46) | collective-permute-done | bytes 524320 | tf_op jit(solution)/shard_map/ppermute | solution.py:73
  436.9 12.1 %fusion.27 = (f32[2048]{0:T(1024)}, f32[256]{0:T(256)S(1)}) fusion(f32[256,2048]{1,0:T(8,128)S(1)} %get-tuple-element.49, bf16[1,256,2048]{2,1,0:T(8,128)(2,1)S(1)} %copy-done.9, f32[256]{0:T(256)S(1)} %get-tuple-element.156, f32[2048]{0:T(1024)S(1)} %bitcast.329), kind=kLoop, calls=%fused_computation.51 | loop fusion | flops 3667712 | bytes 3164160 | tf_op jit(solution)/shard_map/reduce_sum | solution.py:54
  451.6 21.6 %collective-permute-done.50 = bf16[256,2048]{1,0:T(8,128)(2,1)S(1)} collective-permute-done((bf16[256,2048]{1,0:T(8,128)(2,1)S(1)}, bf16[256,2048]{1,0:T(8,128)(2,1)S(1)}, u32[]{:S(2)}, u32[]{:S(2)}) %collective-permute-start.50) | collective-permute-done | bytes 1048608 | tf_op jit(solution)/shard_map/ppermute | solution.py:73
  492.4 10.5 %convolution_convert_fusion = bf16[1024,2048]{1,0:T(8,128)(2,1)} fusion(bf16[2048,1024]{0,1:T(8,128)(2,1)S(1)} %copy-done.27, bf16[2048,2048]{1,0:T(8,128)(2,1)S(1)} %constant_dynamic-update-slice_fusion.30), kind=kOutput, calls=%fused_computation.31 | convolution fusion | flops 8592031744 | bytes 16777216 | tf_op jit(solution)/shard_map/dot_general | solution.py:39
  503.0 20.9 %multiply_convert_fusion.1 = (bf16[2048,1024]{0,1:T(8,128)(2,1)S(1)}, bf16[2048,1024]{0,1:T(8,128)(2,1)}) fusion(f32[2048,2048]{0,1:T(8,128)} %fusion.125, bf16[2048,2048]{1,0:T(8,128)(2,1)} %copy-done.48, bf16[1024,2048]{1,0:T(8,128)(2,1)} %all-gather.11.cloned.1.call-done), kind=kOutput, calls=%fused_computation.12 | convolution fusion | flops 8617197568 | bytes 37748736 | tf_op jit(solution)/shard_map/dot_general | solution.py:35
  525.9 22.8 %fusion.7 = bf16[2048,2048]{1,0:T(8,128)(2,1)} fusion(bf16[2048,2048]{1,0:T(8,128)(2,1)} %constant_dynamic-update-slice_fusion.21, bf16[2048,1024]{0,1:T(8,128)(2,1)S(1)} %get-tuple-element.54, bf16[2048,1024]{0,1:T(8,128)(2,1)} %get-tuple-element.55), kind=kOutput, calls=%fused_computation.22 | convolution fusion | flops 17200840704 | bytes 25165824 | tf_op jit(solution)/shard_map/dot_general | solution.py:39
  548.8 12.9 %fusion.18 = bf16[1024,2048]{1,0:T(8,128)(2,1)S(1)} fusion(bf16[2048,2048]{1,0:T(8,128)(2,1)} %all-gather.9.cloned.1.call-done, bf16[2048,1024]{0,1:T(8,128)(2,1)} %get-tuple-element.55, bf16[2048,1024]{0,1:T(8,128)(2,1)} %copy-done.62), kind=kOutput, calls=%fused_computation.35 | convolution fusion | flops 8600420352 | bytes 20971520 | tf_op jit(solution)/shard_map/dot_general | solution.py:35
  562.8 12.6 %fusion.9 = f32[1024,2048]{1,0:T(8,128)S(1)} fusion(bf16[2048,2048]{1,0:T(8,128)(2,1)} %all-gather.9.cloned.1.call-done, bf16[2048,1024]{0,1:T(8,128)(2,1)} %get-tuple-element.55, bf16[2048,1024]{0,1:T(8,128)(2,1)} %copy-done.62), kind=kOutput, calls=%fused_computation.24 | convolution fusion | flops 8598323200 | bytes 25165824 | tf_op jit(solution)/shard_map/dot_general | solution.py:35
  581.0 10.4 %collective-permute-done.64 = bf16[128,2048]{1,0:T(8,128)(2,1)S(1)} collective-permute-done((bf16[128,2048]{1,0:T(8,128)(2,1)S(1)}, bf16[128,2048]{1,0:T(8,128)(2,1)S(1)}, u32[]{:S(2)}, u32[]{:S(2)}) %collective-permute-start.64) | collective-permute-done | bytes 524320 | tf_op jit(solution)/shard_map/ppermute | solution.py:73
  603.3 10.3 %collective-permute-done.65 = bf16[128,2048]{1,0:T(8,128)(2,1)S(1)} collective-permute-done((bf16[128,2048]{1,0:T(8,128)(2,1)S(1)}, bf16[128,2048]{1,0:T(8,128)(2,1)S(1)}, u32[]{:S(2)}, u32[]{:S(2)}) %collective-permute-start.65) | collective-permute-done | bytes 524320 | tf_op jit(solution)/shard_map/ppermute | solution.py:73
  621.3 22.4 %collective-permute-done.68 = bf16[256,2048]{1,0:T(8,128)(2,1)S(1)} collective-permute-done((bf16[256,2048]{1,0:T(8,128)(2,1)S(1)}, bf16[256,2048]{1,0:T(8,128)(2,1)S(1)}, u32[]{:S(2)}, u32[]{:S(2)}) %collective-permute-start.68) | collective-permute-done | bytes 1048608 | tf_op jit(solution)/shard_map/ppermute | solution.py:73
  680.0 11.7 %multiply_reduce_fusion = (f32[2,2,1024]{2,1,0:T(2,128)S(1)}, f32[2,2,1024,1024]{2,3,1,0:T(8,128)}) fusion(f32[2,2,1024,1024]{2,3,1,0:T(8,128)} %get-tuple-element.158, f32[2,2,1024]{2,1,0:T(2,128)S(1)} %copy-done.52, bf16[2,1024,2,128]{3,1,2,0:T(8,128)(2,1)S(1)} %bitcast.313, bf16[2,1024,2,128]{1,3,2,0:T(8,128)(2,1)} %reshape.373), kind=kOutput, calls=%fused_computation.2 | convolution fusion | flops 1086320640 | bytes 35684352 | tf_op jit(solution)/shard_map/rqhd,rkhd->rhqk/dot_general | solution.py:284
  691.7 12.3 %multiply_convert_fusion = bf16[2,2,1024,1024]{2,3,1,0:T(8,128)(2,1)S(1)} fusion(f32[2,2,1024,1024]{2,3,1,0:T(8,128)} %get-tuple-element.160, f32[2,2,1024]{2,1,0:T(2,128)S(1)} %get-tuple-element.159, f32[2,2,1024,1024]{2,3,1,0:T(8,128)} %get-tuple-element.158, f32[2,2,1024]{2,1,0:T(2,128)S(1)} %copy-done.52), kind=kLoop, calls=%fused_computation.1 | loop fusion | flops 16777216 | bytes 41975808 | tf_op jit(solution)/shard_map/convert_element_type | solution.py:287
  768.4 11.4 %convolution_convert_fusion.4 = bf16[2048,768]{1,0:T(8,128)(2,1)} fusion(bf16[2048,2048]{1,0:T(8,128)(2,1)} %copy-done.47, bf16[2048,768]{0,1:T(8,128)(2,1)} %pad_maximum_fusion.4), kind=kOutput, calls=%fused_computation.36 | convolution fusion | flops 6444023808 | bytes 14680064 | tf_op jit(solution)/shard_map/dot_general | solution.py:39
  878.1 12.0 %collective-permute-done.90 = bf16[2,64,768]{2,1,0:T(8,128)(2,1)S(1)} collective-permute-done((bf16[2,64,768]{2,1,0:T(8,128)(2,1)S(1)}, bf16[2,64,768]{2,1,0:T(8,128)(2,1)S(1)}, u32[]{:S(2)}, u32[]{:S(2)}) %collective-permute-start.90) | collective-permute-done | bytes 196640 | tf_op jit(solution)/shard_map/ppermute | solution.py:73
  (602 shorter events, 546.8 us)
Async XLA Ops:
  7.2 121.2 %all-gather.5.cloned.1.call-start = ((), (), s32[]{:S(2)}) async-start(), calls=%async_computation.4 | async-start | bytes 3932160 | tf_op jit(solution)/shard_map/all_gather | solution.py:79
  44.7 175.9 %all-gather.7.cloned.1.call-start = ((), (), s32[]{:S(2)}) async-start(), calls=%async_computation.5 | async-start | bytes 1310720 | tf_op jit(solution)/shard_map/all_gather | solution.py:79
  78.4 237.3 %all-gather.9.cloned.1.call-start = ((), (), s32[]{:S(2)}) async-start(), calls=%async_computation.6 | async-start | bytes 10485760 | tf_op jit(solution)/shard_map/all_gather | solution.py:79
  152.0 229.9 %all-gather.11.cloned.1.call-start = ((), (), s32[]{:S(2)}) async-start(), calls=%async_computation.7 | async-start | bytes 5242880 | tf_op jit(solution)/shard_map/all_gather | solution.py:79
  232.7 25.1 %collective-permute-start.30 = (bf16[128,2048]{1,0:T(8,128)(2,1)S(1)}, bf16[128,2048]{1,0:T(8,128)(2,1)S(1)}, u32[]{:S(2)}, u32[]{:S(2)}) collective-permute-start(bf16[128,2048]{1,0:T(8,128)(2,1)S(1)} %slice.638), channel_id=1, source_target_pairs={{0,2},{1,3},{2,0},{3,1},{4,6},{5,7},{6,4},{7,5},{8,10},{9,11},{10,... | collective-permute-start | bytes 1572872 | tf_op jit(solution)/shard_map/ppermute | solution.py:73
  234.1 23.8 %collective-permute-start.23 = (bf16[128,2048]{1,0:T(8,128)(2,1)S(1)}, bf16[128,2048]{1,0:T(8,128)(2,1)S(1)}, u32[]{:S(2)}, u32[]{:S(2)}) collective-permute-start(bf16[128,2048]{1,0:T(8,128)(2,1)S(1)} %slice.639), channel_id=1, source_target_pairs={{0,4},{1,5},{2,6},{3,7},{4,0},{5,1},{6,2},{7,3},{8,12},{9,13},{10,... | collective-permute-start | bytes 1572872 | tf_op jit(solution)/shard_map/ppermute | solution.py:73
  270.7 24.3 %collective-permute-start.32 = (bf16[256,2048]{1,0:T(8,128)(2,1)S(1)}, bf16[256,2048]{1,0:T(8,128)(2,1)S(1)}, u32[]{:S(2)}, u32[]{:S(2)}) collective-permute-start(bf16[256,2048]{1,0:T(8,128)(2,1)S(1)} %get-tuple-element.51), channel_id=1, source_target_pairs={{0,4},{1,5},{2,6},{3,7},{4,0},{5,1},{6,2},{7,3},{8,12},{9,13},{10,... | collective-permute-start | bytes 3145736 | tf_op jit(solution)/shard_map/ppermute | solution.py:73
  272.3 24.3 %collective-permute-start.31 = (bf16[256,2048]{1,0:T(8,128)(2,1)S(1)}, bf16[256,2048]{1,0:T(8,128)(2,1)S(1)}, u32[]{:S(2)}, u32[]{:S(2)}) collective-permute-start(bf16[256,2048]{1,0:T(8,128)(2,1)S(1)} %get-tuple-element.51), channel_id=1, source_target_pairs={{0,2},{1,3},{2,0},{3,1},{4,6},{5,7},{6,4},{7,5},{8,10},{9,11},{10,... | collective-permute-start | bytes 3145736 | tf_op jit(solution)/shard_map/ppermute | solution.py:73
  298.9 364.5 %reduce-scatter.5.cloned.1.call-start = ((), (), s32[]{:S(2)}) async-start(), calls=%async_computation.8 | async-start | bytes 5242880 | tf_op jit(solution)/shard_map/reduce_scatter | solution.py:82
  402.0 24.5 %collective-permute-start.48 = (bf16[128,2048]{1,0:T(8,128)(2,1)S(1)}, bf16[128,2048]{1,0:T(8,128)(2,1)S(1)}, u32[]{:S(2)}, u32[]{:S(2)}) collective-permute-start(bf16[128,2048]{1,0:T(8,128)(2,1)S(1)} %slice.636), channel_id=1, source_target_pairs={{0,2},{1,3},{2,0},{3,1},{4,6},{5,7},{6,4},{7,5},{8,10},{9,11},{10,... | collective-permute-start | bytes 1572872 | tf_op jit(solution)/shard_map/ppermute | solution.py:73
  402.7 23.8 %collective-permute-start.41 = (bf16[128,2048]{1,0:T(8,128)(2,1)S(1)}, bf16[128,2048]{1,0:T(8,128)(2,1)S(1)}, u32[]{:S(2)}, u32[]{:S(2)}) collective-permute-start(bf16[128,2048]{1,0:T(8,128)(2,1)S(1)} %slice.637), channel_id=1, source_target_pairs={{0,4},{1,5},{2,6},{3,7},{4,0},{5,1},{6,2},{7,3},{8,12},{9,13},{10,... | collective-permute-start | bytes 1572872 | tf_op jit(solution)/shard_map/ppermute | solution.py:73
  449.5 23.7 %collective-permute-start.50 = (bf16[256,2048]{1,0:T(8,128)(2,1)S(1)}, bf16[256,2048]{1,0:T(8,128)(2,1)S(1)}, u32[]{:S(2)}, u32[]{:S(2)}) collective-permute-start(bf16[256,2048]{1,0:T(8,128)(2,1)S(1)} %get-tuple-element.47), channel_id=1, source_target_pairs={{0,4},{1,5},{2,6},{3,7},{4,0},{5,1},{6,2},{7,3},{8,12},{9,13},{10,... | collective-permute-start | bytes 3145736 | tf_op jit(solution)/shard_map/ppermute | solution.py:73
  450.1 24.7 %collective-permute-start.49 = (bf16[256,2048]{1,0:T(8,128)(2,1)S(1)}, bf16[256,2048]{1,0:T(8,128)(2,1)S(1)}, u32[]{:S(2)}, u32[]{:S(2)}) collective-permute-start(bf16[256,2048]{1,0:T(8,128)(2,1)S(1)} %get-tuple-element.47), channel_id=1, source_target_pairs={{0,2},{1,3},{2,0},{3,1},{4,6},{5,7},{6,4},{7,5},{8,10},{9,11},{10,... | collective-permute-start | bytes 3145736 | tf_op jit(solution)/shard_map/ppermute | solution.py:73
  502.9 265.5 %reduce-scatter.7.cloned.1.call-start = ((), (), s32[]{:S(2)}) async-start(), calls=%async_computation.9 | async-start | bytes 10485760 | tf_op jit(solution)/shard_map/reduce_scatter | solution.py:82
  548.8 256.9 %reduce-scatter.11.cloned.1.call-start = ((), (), s32[]{:S(2)}) async-start(), calls=%async_computation.11 | async-start | bytes 1310720 | tf_op jit(solution)/shard_map/reduce_scatter | solution.py:82
  578.3 24.9 %collective-permute-start.66 = (bf16[128,2048]{1,0:T(8,128)(2,1)S(1)}, bf16[128,2048]{1,0:T(8,128)(2,1)S(1)}, u32[]{:S(2)}, u32[]{:S(2)}) collective-permute-start(bf16[128,2048]{1,0:T(8,128)(2,1)S(1)} %slice.634), channel_id=1, source_target_pairs={{0,2},{1,3},{2,0},{3,1},{4,6},{5,7},{6,4},{7,5},{8,10},{9,11},{10,... | collective-permute-start | bytes 1572872 | tf_op jit(solution)/shard_map/ppermute | solution.py:73
  579.5 23.8 %collective-permute-start.59 = (bf16[128,2048]{1,0:T(8,128)(2,1)S(1)}, bf16[128,2048]{1,0:T(8,128)(2,1)S(1)}, u32[]{:S(2)}, u32[]{:S(2)}) collective-permute-start(bf16[128,2048]{1,0:T(8,128)(2,1)S(1)} %slice.635), channel_id=1, source_target_pairs={{0,4},{1,5},{2,6},{3,7},{4,0},{5,1},{6,2},{7,3},{8,12},{9,13},{10,... | collective-permute-start | bytes 1572872 | tf_op jit(solution)/shard_map/ppermute | solution.py:73
  619.2 24.5 %collective-permute-start.68 = (bf16[256,2048]{1,0:T(8,128)(2,1)S(1)}, bf16[256,2048]{1,0:T(8,128)(2,1)S(1)}, u32[]{:S(2)}, u32[]{:S(2)}) collective-permute-start(bf16[256,2048]{1,0:T(8,128)(2,1)S(1)} %get-tuple-element.44), channel_id=1, source_target_pairs={{0,4},{1,5},{2,6},{3,7},{4,0},{5,1},{6,2},{7,3},{8,12},{9,13},{10,... | collective-permute-start | bytes 3145736 | tf_op jit(solution)/shard_map/ppermute | solution.py:73
  620.7 24.1 %collective-permute-start.67 = (bf16[256,2048]{1,0:T(8,128)(2,1)S(1)}, bf16[256,2048]{1,0:T(8,128)(2,1)S(1)}, u32[]{:S(2)}, u32[]{:S(2)}) collective-permute-start(bf16[256,2048]{1,0:T(8,128)(2,1)S(1)} %get-tuple-element.44), channel_id=1, source_target_pairs={{0,2},{1,3},{2,0},{3,1},{4,6},{5,7},{6,4},{7,5},{8,10},{9,11},{10,... | collective-permute-start | bytes 3145736 | tf_op jit(solution)/shard_map/ppermute | solution.py:73
  677.4 183.8 %reduce-scatter.9.cloned.1.call-start = ((), (), s32[]{:S(2)}) async-start(), calls=%async_computation.10 | async-start | bytes 3932160 | tf_op jit(solution)/shard_map/reduce_scatter | solution.py:82
  807.4 54.7 %collective-permute-start.79 = (bf16[256,2048]{1,0:T(8,128)(2,1)}, bf16[256,2048]{1,0:T(8,128)(2,1)}, u32[]{:S(2)}, u32[]{:S(2)}) collective-permute-start(bf16[256,2048]{1,0:T(8,128)(2,1)} %get-tuple-element.75), channel_id=1, source_target_pairs={{0,1},{1,0},{2,3},{3,2},{4,5},{5,4},{6,7},{7,6},{8,9},{9,8},{10,11... | collective-permute-start | bytes 3145736 | tf_op jit(solution)/shard_map/ppermute | solution.py:73
  823.2 39.0 %collective-permute-start.81 = (bf16[128,2048]{1,0:T(8,128)(2,1)}, bf16[128,2048]{1,0:T(8,128)(2,1)S(1)}, u32[]{:S(2)}, u32[]{:S(2)}) collective-permute-start(bf16[128,2048]{1,0:T(8,128)(2,1)} %slice.633), channel_id=1, source_target_pairs={{0,4},{1,5},{2,6},{3,7},{4,0},{5,1},{6,2},{7,3},{8,12},{9,13},{10,... | collective-permute-start | bytes 1572872 | tf_op jit(solution)/shard_map/ppermute | solution.py:73
  824.1 39.9 %collective-permute-start.88 = (bf16[128,2048]{1,0:T(8,128)(2,1)}, bf16[128,2048]{1,0:T(8,128)(2,1)}, u32[]{:S(2)}, u32[]{:S(2)}) collective-permute-start(bf16[128,2048]{1,0:T(8,128)(2,1)} %slice.632), channel_id=1, source_target_pairs={{0,2},{1,3},{2,0},{3,1},{4,6},{5,7},{6,4},{7,5},{8,10},{9,11},{10,... | collective-permute-start | bytes 1572872 | tf_op jit(solution)/shard_map/ppermute | solution.py:73
  862.2 29.0 %collective-permute-start.96 = (bf16[2,64,2048]{2,1,0:T(8,128)(2,1)}, bf16[2,64,2048]{2,1,0:T(8,128)(2,1)S(1)}, u32[]{:S(2)}, u32[]{:S(2)}) collective-permute-start(bf16[2,64,2048]{2,1,0:T(8,128)(2,1)} %get-tuple-element.89), channel_id=1, source_target_pairs={{0,6},{1,7},{2,4},{3,5},{4,2},{5,3},{6,0},{7,1},{8,14},{9,15},{10,... | collective-permute-start | bytes 1572872 | tf_op jit(solution)/shard_map/ppermute | solution.py:73
  (151 other events, 1822.3 us)
Sparse Core Ops, SparseCore 0:
  44.9 62.7 all-gather.4
  109.3 26.6 all-gather.6
  152.1 149.3 all-gather.8
  302.9 78.9 all-gather.10
  503.0 74.7 reduce-scatter.4
  580.1 145.1 reduce-scatter.6
  727.5 27.8 reduce-scatter.10
  779.9 60.3 reduce-scatter.8

commit v6 on v5

--- a/solution.py
+++ b/solution.py
@@ -84,16 +84,22 @@
         )
 
     def exchange(self, parts, tokens=False):
-        shape = parts.shape
         swap = self.swap if not tokens else lambda v, j: self.swap_tokens(v, j, 1)
-        parts = parts.reshape((self.size // 2, 2) + shape[1:])
-        core, pair = self.g % 2, self.g // 2
+        return self.exchange_chips(self.exchange_pair(parts, swap), swap)
+
+    def exchange_pair(self, parts, swap):
+        parts = parts.reshape((self.size // 2, 2) + parts.shape[1:])
+        core = self.g % 2
         other = swap(lax.dynamic_index_in_dim(parts, 1 - core, 1, keepdims=False), 1)
-        parts = lax.dynamic_update_index_in_dim(parts, other, 1 - core, 1)
-        moved = [swap(pick(parts, pair ^ j), 2 * j) for j in range(1, self.size // 2)]
+        return lax.dynamic_update_index_in_dim(parts, other, 1 - core, 1)
+
+    def exchange_chips(self, parts, swap):
+        pair = self.g // 2
+        picks = lax.optimization_barrier([pick(parts, pair ^ j) for j in range(1, self.size // 2)])
+        moved = lax.optimization_barrier([swap(v, 2 * (j + 1)) for j, v in enumerate(picks)])
         for j, v in enumerate(moved):
             parts = lax.dynamic_update_index_in_dim(parts, v, pair ^ (j + 1), 0)
-        return parts.reshape(shape)
+        return parts.reshape((self.size,) + parts.shape[2:])
 
     def swap_tokens(self, v, j, axis=0):
         pieces = jnp.split(self.swap(v, j), self.size, axis=axis)
@@ -193,14 +199,26 @@
     allowed = (places[:, None] >= places[None, :])[None] & (segment[:, :, None] == segment[:, None, :])
 
     def by_rows(v):
-        v = v.reshape((2, part, c.seq // 2, tl) + v.shape[1:])
-        return v.swapaxes(0, 1).reshape((part, row_len) + v.shape[4:])
+        v = jnp.stack([v[:, k * HD : (k + 1) * HD] for k in range(v.shape[1] // HD)])
+        v = v.reshape(-1, 2, part, c.seq // 2, tl, HD).transpose(2, 0, 1, 3, 4, 5)
+        return v.reshape(part, -1, row_len, HD)
 
     def by_tokens(v):
-        v = v.reshape((part, 2, c.seq // 2, tl) + v.shape[2:])
-        return v.swapaxes(0, 1).reshape((toks,) + v.shape[4:])
-
-    cosine, sine_table = rope_tables(by_tokens(positions))
+        v = jnp.concatenate([v[:, k] for k in range(v.shape[1])], axis=-1)
+        v = v.reshape(part, 2, c.seq // 2, tl, v.shape[-1]).swapaxes(0, 1)
+        return v.reshape(toks, v.shape[-1])
+
+    def stat_rows(v):
+        v = v.reshape(-1, 2, part, c.seq // 2, tl).swapaxes(1, 2)
+        return v.reshape(-1, part, 1, row_len, 1)
+
+    def stat_tokens(v):
+        v = v.reshape(-1, part, 2, c.seq // 2, tl).swapaxes(1, 2)
+        return v.reshape(-1, toks)
+
+    cosine, sine_table = rope_tables(positions.reshape(-1))
+    cosine = cosine.reshape(part, 1, row_len, HD)
+    sine_table = sine_table.reshape(part, 1, row_len, HD)
     if pairs:
         gains4 = norm_gains.reshape(4, 2, hl, half_group, HD).transpose(3, 1, 0, 2, 4).reshape(size, 4, wide)
     else:
@@ -211,25 +229,29 @@
     query_pre, key_pre = mixed[:, :wide], mixed[:, wide : 2 * wide]
     squares = jnp.stack([jnp.sum(query_pre * query_pre, -1), jnp.sum(key_pre * key_pre, -1)])
     scales = lax.rsqrt(c.sum_tokens(squares) / d + eps)
-    query_scale, key_scale = scales[0][:, None], scales[1][:, None]
-    shape3 = (toks, hl, HD)
-    query = rotate((query_pre * query_scale * gains_own[0]).reshape(shape3), cosine, sine_table, 1.0)
-    key = rotate((key_pre * key_scale * gains_own[1]).reshape(shape3), cosine, sine_table, 1.0)
-    query, key = by_rows(query.astype(BF)), by_rows(key.astype(BF))
-    value = by_rows(mixed[:, 2 * wide :].reshape(shape3).astype(BF))
+    query_scale, key_scale = stat_rows(scales)
+    query_pre, key_pre = by_rows(query_pre), by_rows(key_pre)
+    gain_q = gains_own[0].reshape(1, hl, 1, HD)
+    gain_k = gains_own[1].reshape(1, hl, 1, HD)
+    query = rotate(query_pre * query_scale * gain_q, cosine, sine_table, 1.0).astype(BF)
+    key = rotate(key_pre * key_scale * gain_k, cosine, sine_table, 1.0).astype(BF)
+    value = by_rows(mixed[:, 2 * wide :].astype(BF))
     score_scale = 1.0 / HD**0.5
-    scores = jnp.einsum("rqhd,rkhd->rhqk", query, key, preferred_element_type=F32) * score_scale
+    scores = jnp.einsum("rhqd,rhkd->rhqk", query, key, preferred_element_type=F32) * score_scale
     scores = jnp.where(allowed[:, None], scores, -1e30)
     row_max = jnp.max(scores, axis=-1, keepdims=True)
     exponent = jnp.exp(scores - row_max)
     probs = exponent / jnp.sum(exponent, axis=-1, keepdims=True)
     probs_low = probs.astype(BF)
-    attended = jnp.einsum("rhqk,rkhd->rqhd", probs_low, value, preferred_element_type=F32).astype(BF)
+    attended = jnp.einsum("rhqk,rhkd->rhqd", probs_low, value, preferred_element_type=F32).astype(BF)
+
+    part_of = HD // 2
 
     def to_out(v):
         if pairs:
             core = c.g % 2
-            v = v.reshape(toks, hl, 2, HD // 2).transpose(2, 0, 1, 3).reshape(2, toks, wide // 2)
+            cuts = [v[:, k * part_of : (k + 1) * part_of] for k in range(2 * hl)]
+            v = jnp.stack([jnp.concatenate(cuts[0::2], axis=1), jnp.concatenate(cuts[1::2], axis=1)])
             own, got = pick(v, core), c.swap_tokens(pick(v, 1 - core), 1)
             first = jnp.where(core == 0, own, got)
             second = jnp.where(core == 0, got, own)
@@ -241,14 +263,14 @@
     def from_out(v):
         if pairs:
             core = c.g % 2
-            v = v.reshape(toks, 2, wide // 2).transpose(1, 0, 2)
+            v = jnp.stack([v[:, : wide // 2], v[:, wide // 2 :]])
             own, got = pick(v, core), c.swap_tokens(pick(v, 1 - core), 1)
-            first = jnp.where(core == 0, own, got).reshape(toks, hl, 1, HD // 2)
-            second = jnp.where(core == 0, got, own).reshape(toks, hl, 1, HD // 2)
-            return jnp.concatenate([first, second], axis=2).reshape(shape3)
+            halves = [jnp.where(core == 0, own, got), jnp.where(core == 0, got, own)]
+            cuts = [u[:, k * part_of : (k + 1) * part_of] for k in range(hl) for u in halves]
+            return jnp.concatenate(cuts, axis=1)
         v = c.exchange(v.reshape(toks, size, wide // size).transpose(1, 0, 2), True)
         v = v.reshape(size, toks, wide // (size * n_out), n_out).transpose(1, 2, 0, 3)
-        return v.reshape(shape3)
+        return v.reshape(toks, wide)
 
     attended = to_out(by_tokens(attended))
     branch = c.scatter_tokens(attended, lambda v: dot_nn(v, full_out))
@@ -269,7 +291,7 @@
     grad_branch2 = c.gather_tokens(grad_branch2.astype(BF))
     g_down = dot_tn(inner, grad_branch2).astype(BF)
     sum_down = c.scatter(g_down)
-    grad_inner = dot_nt(grad_branch2, full_down)
+    grad_inner = dot_nt(after(grad_branch2, g_down), full_down)
     grad_gate = grad_inner * up * sig * (1.0 + gate * (1.0 - sig))
     grad_gu = jnp.concatenate([grad_gate, grad_inner * (gate * sig)], axis=1).astype(BF)
     grad_hidden = upstream + c.scatter_tokens(grad_gu, lambda v: dot_nt(v, full_gu))
@@ -281,34 +303,36 @@
     g_out = dot_tn(attended, grad_branch).astype(BF)
     sum_out = c.scatter(g_out)
     grad_att = by_rows(from_out(dot_nt(grad_branch, full_out).astype(BF)))
-    grad_probs = jnp.einsum("rqhd,rkhd->rhqk", grad_att, value, preferred_element_type=F32)
-    grad_value = jnp.einsum("rhqk,rqhd->rkhd", probs_low, grad_att, preferred_element_type=F32)
+    grad_probs = jnp.einsum("rhqd,rhkd->rhqk", grad_att, value, preferred_element_type=F32)
+    grad_value = jnp.einsum("rhqk,rhqd->rhkd", probs_low, grad_att, preferred_element_type=F32)
     row_sum = jnp.sum(probs * grad_probs, axis=-1, keepdims=True)
     grad_scores = (probs * (grad_probs - row_sum)).astype(BF)
-    grad_query = jnp.einsum("rhqk,rkhd->rqhd", grad_scores, key, preferred_element_type=F32)
-    grad_key = jnp.einsum("rhqk,rqhd->rkhd", grad_scores, query, preferred_element_type=F32)
-    grad_query = by_tokens((grad_query * score_scale).astype(BF)).astype(F32)
-    grad_key = by_tokens((grad_key * score_scale).astype(BF)).astype(F32)
-    grad_value = by_tokens(grad_value.astype(BF)).reshape(toks, wide)
-    e_query = rotate(grad_query, cosine, sine_table, -1.0).reshape(toks, wide)
-    e_key = rotate(grad_key, cosine, sine_table, -1.0).reshape(toks, wide)
-    scaled_q, scaled_k = e_query * gains_own[0], e_key * gains_own[1]
-    means = c.sum_tokens(
-        jnp.stack([jnp.sum(scaled_q * query_pre, -1), jnp.sum(scaled_k * key_pre, -1)])
+    grad_query = jnp.einsum("rhqk,rhkd->rhqd", grad_scores, key, preferred_element_type=F32)
+    grad_key = jnp.einsum("rhqk,rhqd->rhkd", grad_scores, query, preferred_element_type=F32)
+    grad_query = (grad_query * score_scale).astype(BF).astype(F32)
+    grad_key = (grad_key * score_scale).astype(BF).astype(F32)
+    e_query = rotate(grad_query, cosine, sine_table, -1.0)
+    e_key = rotate(grad_key, cosine, sine_table, -1.0)
+    scaled_q, scaled_k = e_query * gain_q, e_key * gain_k
+    sums = jnp.stack(
+        [jnp.sum(scaled_q * query_pre, axis=(1, 3)), jnp.sum(scaled_k * key_pre, axis=(1, 3))]
     )
-    means = means / d
-    grad_qp = query_scale * scaled_q - query_pre * query_scale**3 * means[0][:, None]
-    grad_kp = key_scale * scaled_k - key_pre * key_scale**3 * means[1][:, None]
-    gain_query = jnp.sum(e_query * query_pre * query_scale, axis=0)
-    gain_key = jnp.sum(e_key * key_pre * key_scale, axis=0)
-    grad_mixed = jnp.concatenate([grad_qp.astype(BF), grad_kp.astype(BF), grad_value], axis=1)
-    grad_mixed = after(grad_mixed, sum_down, sum_gu)
+    mean_q, mean_k = stat_rows(c.sum_tokens(stat_tokens(sums)) / d)
+    grad_qp = query_scale * scaled_q - query_pre * query_scale**3 * mean_q
+    grad_kp = key_scale * scaled_k - key_pre * key_scale**3 * mean_k
+    gain_query = jnp.sum(e_query * query_pre * query_scale, axis=(0, 2)).reshape(wide)
+    gain_key = jnp.sum(e_key * key_pre * key_scale, axis=(0, 2)).reshape(wide)
+    grad_mixed = by_tokens(
+        jnp.concatenate([grad_qp.astype(BF), grad_kp.astype(BF), grad_value.astype(BF)], axis=1)
+    )
+    back_gu = c.exchange_pair(sum_gu.reshape(size, n_in, 2 * ffl), c.swap)
+    grad_mixed = after(grad_mixed, back_gu)
     g_qkv = dot_tn(x_full, grad_mixed).astype(BF)
     sum_qkv = c.scatter(g_qkv)
+    back_gu = c.exchange_chips(back_gu, c.swap)
+    grad_mixed = after(grad_mixed, g_qkv, back_gu)
     grad_input = grad_hidden + c.scatter_tokens(grad_mixed, lambda v: dot_nt(v, full_qkv))
-
-    back_gu = c.exchange(sum_gu.reshape(size, n_in, 2 * ffl)).astype(F32)
-    back_gu = back_gu.reshape(size, n_in, 2, copies, n_ff)
+    back_gu = back_gu.astype(F32).reshape(size, n_in, 2, copies, n_ff)
     grad_gate_up = back_gu.transpose(1, 2, 3, 0, 4)
     back_qkv = c.exchange(sum_qkv.reshape(size, n_in, 3 * wide)).astype(F32)
     if pairs:

time: 926 us -> 864 us (0.933)
  local copies, waits for them, and re-layouts: 159 us -> 109 us
    ppermute x102, waiting for transfers between devices: 323 us -> 289 us  [send(): return lax.ppermute(v, ('rows', 'seq'), pairs)]
    convert_element_type x10 -> x0, local copies, waits for them, and re-layouts: 23.1 us -> none  [the longest x4 11.9 us: per_device(): grad_key = by_tokens((grad_key * score_scale).astype(BF)).astype(F32)]
    all_gather x4, waiting for transfers between devices: 32.3 us -> 50 us  [gather(): lax.all_gather(block, ('rows', 'seq'), axis=0, tiled=True, axis_index_gro...]
    reshape x9 -> x1, local copies, waits for them, and re-layouts: 17.6 us -> 0.02 us  [stat_tokens(): return v.reshape(-1, toks)]
    reduce_scatter x4, waiting for transfers between devices: 0.01 us -> 14.5 us  [scatter(): lax.psum_scatter(parts, ('rows', 'seq'), scatter_dimension=0, tiled=True,...]
    unnamed x178 -> x193, local copies, waits for them, and re-layouts: 40.4 us -> 52.6 us
    concatenate x6 -> x3, local copies, waits for them, and re-layouts: 12.6 us -> 0.4 us  [by_tokens(): v = jnp.concatenate([v[:, k] for k in range(v.shape[1])], axis=-1)]
  transfers between devices with their start and end apart: 110 -> 110, of which waited for: 49 -> 51; matrix products, arithmetic and copies ran while one was open for 45% -> 41% of each run, Pallas kernels for 0% -> 0%
where the time goes in v6:
time: 864 us; the launch traced here: 858 us
  waiting for transfers between devices  354 us (41%)
  matrix products  207 us (24%)
  local copies, waits for them, and re-layouts  109 us (13%)
  other arithmetic  90 us (10%)
  starting transfers between devices  81.3 us (9%)
  between operations  16.7 us (2%)
    ppermute x102, waiting for transfers between devices, send(): return lax.ppermute(v, ('rows', 'seq'), pairs)  289 us
    ppermute x102, starting transfers between devices, send(): return lax.ppermute(v, ('rows', 'seq'), pairs)  80.4 us
    dot_general x6, matrix products, dot_nt(): lax.dot_general(a, b, (((1,), (1,)), ((), ())), preferred_element_type=F32)  62.5 us
    unnamed x193, local copies, waits for them, and re-layouts  52.6 us
    dot_general x6, matrix products, dot_nn(): lax.dot_general(a, b, (((1,), (0,)), ((), ())), preferred_element_type=F32)  50.4 us
    all_gather x4, waiting for transfers between devices, gather(): lax.all_gather(block, ('rows', 'seq'), axis=0, tiled=True, axis_index_gro...  50 us
    dot_general x4, matrix products, dot_tn(): lax.dot_general(a, b, (((0,), (0,)), ((), ())), preferred_element_type=F32)  48.8 us
  transfers between devices with their start and end apart: 110, of which 51 were waited for; matrix products, arithmetic and copies ran while one was open for 41% of the time, Pallas kernels for 0%

profile of v6, /device:TPU:0, one launch (start us, length us, event | category | flops | bytes accessed | tf_op | source)
XLA Modules:
  0.0 858.3 jit_solution(13637828282726497700)
XLA Ops:
  41.8 12.5 %collective-permute-done.6 = bf16[256,2048]{1,0:T(8,128)(2,1)} collective-permute-done((bf16[256,2048]{1,0:T(8,128)(2,1)S(1)}, bf16[256,2048]{1,0:T(8,128)(2,1)}, u32[]{:S(2)}, u32[]{:S(2)}) %collective-permute-start.6) | collective-permute-done | bytes 1048608 | tf_op jit(solution)/shard_map/ppermute | solution.py:73
  95.6 10.7 %collective-permute-done.16 = bf16[2,64,2048]{2,1,0:T(8,128)(2,1)} collective-permute-done((bf16[2,64,2048]{2,1,0:T(8,128)(2,1)S(1)}, bf16[2,64,2048]{2,1,0:T(8,128)(2,1)}, u32[]{:S(2)}, u32[]{:S(2)}) %collective-permute-start.16) | collective-permute-done | bytes 524320 | tf_op jit(solution)/shard_map/ppermute | solution.py:73
  118.2 10.0 %fusion.151 = (bf16[2048,768]{1,0:T(8,128)(2,1)S(1)}, f32[2048,768]{1,0:T(8,128)S(1)}) fusion(bf16[2048,2048]{1,0:T(8,128)(2,1)} %copy-done.55, bf16[2048,768]{1,0:T(8,128)(2,1)} %all-gather.5.cloned.1.call-done), kind=kOutput, calls=%fused_computation.385 | convolution fusion | flops 6444023808 | bytes 20971520 | tf_op jit(solution)/shard_map/dot_general | solution.py:31
  148.2 11.8 %fusion.152 = (f32[2,2,1024]{2,1,0:T(2,128)S(1)}, f32[2,2,1024,1024]{2,3,1,0:T(8,128)}) fusion(pred[2,1024,1024]{1,2,0:T(8,128)(4,1)} %compare_and_fusion, bf16[2,2,1024,128]{3,2,1,0:T(8,128)(2,1)} %get-tuple-element.152, bf16[2,2,1024,128]{3,2,1,0:T(8,128)(2,1)} %get-tuple-element.151), kind=kOutput, calls=%fused_computation.386 | convolution fusion | flops 1090520064 | bytes 20987904 | tf_op jit(solution)/shard_map/sub | solution.py:243
  187.9 10.5 %collective-permute-done.28 = bf16[128,2048]{1,0:T(8,128)(2,1)S(1)} collective-permute-done((bf16[128,2048]{1,0:T(8,128)(2,1)S(1)}, bf16[128,2048]{1,0:T(8,128)(2,1)S(1)}, u32[]{:S(2)}, u32[]{:S(2)}) %collective-permute-start.28) | collective-permute-done | bytes 524320 | tf_op jit(solution)/shard_map/ppermute | solution.py:73
  210.2 10.1 %collective-permute-done.29 = bf16[128,2048]{1,0:T(8,128)(2,1)S(1)} collective-permute-done((bf16[128,2048]{1,0:T(8,128)(2,1)S(1)}, bf16[128,2048]{1,0:T(8,128)(2,1)S(1)}, u32[]{:S(2)}, u32[]{:S(2)}) %collective-permute-start.29) | collective-permute-done | bytes 524320 | tf_op jit(solution)/shard_map/ppermute | solution.py:73
  225.0 22.2 %collective-permute-done.32 = bf16[256,2048]{1,0:T(8,128)(2,1)S(1)} collective-permute-done((bf16[256,2048]{1,0:T(8,128)(2,1)S(1)}, bf16[256,2048]{1,0:T(8,128)(2,1)S(1)}, u32[]{:S(2)}, u32[]{:S(2)}) %collective-permute-start.32) | collective-permute-done | bytes 1048608 | tf_op jit(solution)/shard_map/ppermute | solution.py:73
  271.0 24.3 %fusion.153 = f32[2048,2048]{0,1:T(8,128)} fusion(bf16[2048,2048]{1,0:T(8,128)(2,1)} %constant_dynamic-update-slice_fusion.17, bf16[2048,2048]{1,0:T(8,128)(2,1)} %all-gather.9.cloned.1.call-done), kind=kOutput, calls=%fused_computation.387 | convolution fusion | flops 17179869184 | bytes 33554432 | tf_op jit(solution)/shard_map/dot_general | solution.py:31
  304.4 47.0 %all-gather.11.cloned.1.call-done = bf16[1024,2048]{1,0:T(8,128)(2,1)} async-done(((bf16[256,2048]{1,0:T(8,128)(2,1)}), bf16[1024,2048]{1,0:T(8,128)(2,1)}) %all-gather.11.cloned.1.call-update) | async-done | bytes 4194320 | tf_op jit(solution)/shard_map/all_gather | solution.py:79
  372.8 10.5 %collective-permute-done.46 = bf16[128,2048]{1,0:T(8,128)(2,1)S(1)} collective-permute-done((bf16[128,2048]{1,0:T(8,128)(2,1)S(1)}, bf16[128,2048]{1,0:T(8,128)(2,1)S(1)}, u32[]{:S(2)}, u32[]{:S(2)}) %collective-permute-start.46) | collective-permute-done | bytes 524320 | tf_op jit(solution)/shard_map/ppermute | solution.py:73
  410.8 21.6 %collective-permute-done.50 = bf16[256,2048]{1,0:T(8,128)(2,1)S(1)} collective-permute-done((bf16[256,2048]{1,0:T(8,128)(2,1)S(1)}, bf16[256,2048]{1,0:T(8,128)(2,1)S(1)}, u32[]{:S(2)}, u32[]{:S(2)}) %collective-permute-start.50) | collective-permute-done | bytes 1048608 | tf_op jit(solution)/shard_map/ppermute | solution.py:73
  451.5 10.4 %convolution_convert_fusion = bf16[1024,2048]{1,0:T(8,128)(2,1)} fusion(bf16[2048,1024]{0,1:T(8,128)(2,1)S(1)} %copy-done.31, bf16[2048,2048]{1,0:T(8,128)(2,1)S(1)} %constant_dynamic-update-slice_fusion.26), kind=kOutput, calls=%fused_computation.31 | convolution fusion | flops 8592031744 | bytes 16777216 | tf_op jit(solution)/shard_map/dot_general | solution.py:39
  462.0 20.9 %multiply_convert_fusion.1 = (bf16[2048,1024]{0,1:T(8,128)(2,1)S(1)}, bf16[2048,1024]{0,1:T(8,128)(2,1)}) fusion(f32[2048,2048]{0,1:T(8,128)} %fusion.153, bf16[2048,2048]{1,0:T(8,128)(2,1)} %copy-done.56, bf16[1024,2048]{1,0:T(8,128)(2,1)} %all-gather.11.cloned.1.call-done), kind=kOutput, calls=%fused_computation.12 | convolution fusion | flops 8617197568 | bytes 37748736 | tf_op jit(solution)/shard_map/dot_general | solution.py:35
  482.9 12.0 %fusion.18 = bf16[1024,2048]{1,0:T(8,128)(2,1)S(1)} fusion(bf16[2048,2048]{1,0:T(8,128)(2,1)} %all-gather.9.cloned.1.call-done, bf16[2048,1024]{0,1:T(8,128)(2,1)} %get-tuple-element.105, bf16[2048,1024]{0,1:T(8,128)(2,1)S(1)} %get-tuple-element.104), kind=kOutput, calls=%fused_computation.35 | convolution fusion | flops 8600420352 | bytes 20971520 | tf_op jit(solution)/shard_map/dot_general | solution.py:35
  496.9 12.2 %fusion.9 = f32[1024,2048]{1,0:T(8,128)S(1)} fusion(bf16[2048,2048]{1,0:T(8,128)(2,1)} %all-gather.9.cloned.1.call-done, bf16[2048,1024]{0,1:T(8,128)(2,1)} %get-tuple-element.105, bf16[2048,1024]{0,1:T(8,128)(2,1)S(1)} %get-tuple-element.104), kind=kOutput, calls=%fused_computation.24 | convolution fusion | flops 8598323200 | bytes 25165824 | tf_op jit(solution)/shard_map/dot_general | solution.py:35
  530.8 21.2 %fusion.7 = bf16[2048,2048]{1,0:T(8,128)(2,1)} fusion(bf16[2048,2048]{1,0:T(8,128)(2,1)} %constant_dynamic-update-slice_fusion.17, bf16[2048,1024]{0,1:T(8,128)(2,1)S(1)} %get-tuple-element.104, bf16[2048,1024]{0,1:T(8,128)(2,1)S(1)} %copy-done.70), kind=kOutput, calls=%fused_computation.22 | convolution fusion | flops 17200840704 | bytes 25165824 | tf_op jit(solution)/shard_map/dot_general | solution.py:39
  563.2 21.1 %collective-permute-done.68 = bf16[256,2048]{1,0:T(8,128)(2,1)S(1)} collective-permute-done((bf16[256,2048]{1,0:T(8,128)(2,1)S(1)}, bf16[256,2048]{1,0:T(8,128)(2,1)S(1)}, u32[]{:S(2)}, u32[]{:S(2)}) %collective-permute-start.68) | collective-permute-done | bytes 1048608 | tf_op jit(solution)/shard_map/ppermute | solution.py:73
  614.4 11.0 %multiply_reduce_fusion = (f32[2,2,1024]{2,1,0:T(2,128)S(1)}, f32[2,2,1024,1024]{2,3,1,0:T(8,128)}) fusion(f32[2,2,1024,1024]{2,3,1,0:T(8,128)} %get-tuple-element.231, f32[2,2,1024]{2,1,0:T(2,128)S(1)} %copy-done.64, bf16[2,2,1024,128]{3,2,1,0:T(8,128)(2,1)S(1)} %bitcast.311, bf16[2,2,1024,128]{3,2,1,0:T(8,128)(2,1)S(1)} %bitcast.310), kind=kOutput, calls=%fused_computation.2 | convolution fusion | flops 1086320640 | bytes 35684352 | tf_op jit(solution)/shard_map/rhqd,rhkd->rhqk/dot_general | solution.py:306
  625.4 13.0 %multiply_convert_fusion = bf16[2,2,1024,1024]{2,3,1,0:T(8,128)(2,1)S(1)} fusion(f32[2,2,1024,1024]{2,3,1,0:T(8,128)} %get-tuple-element.233, f32[2,2,1024]{2,1,0:T(2,128)S(1)} %get-tuple-element.232, f32[2,2,1024,1024]{2,3,1,0:T(8,128)} %get-tuple-element.231, f32[2,2,1024]{2,1,0:T(2,128)S(1)} %copy-done.64), kind=kLoop, calls=%fused_computation.1 | loop fusion | flops 16777216 | bytes 41975808 | tf_op jit(solution)/shard_map/convert_element_type | solution.py:309
  681.1 14.5 %reduce-scatter.7.cloned.1.call-done = bf16[512,2048]{1,0:T(8,128)(2,1)} async-done(((bf16[2048,2048]{1,0:T(8,128)(2,1)}), bf16[512,2048]{1,0:T(8,128)(2,1)}) %reduce-scatter.7.cloned.1.call-update) | async-done | bytes 2097168 | tf_op jit(solution)/shard_map/reduce_scatter | solution.py:82
  702.6 10.5 %convolution_convert_fusion.4 = bf16[2048,768]{1,0:T(8,128)(2,1)} fusion(bf16[2048,2048]{1,0:T(8,128)(2,1)} %copy-done.55, bf16[2048,768]{1,0:T(8,128)(2,1)S(1)} %bitcast.292), kind=kOutput, calls=%fused_computation.36 | convolution fusion | flops 6444023808 | bytes 14680064 | tf_op jit(solution)/shard_map/dot_general | solution.py:39
  726.2 12.7 %collective-permute-done.98 = f32[4,2048]{1,0:T(4,128)S(1)} collective-permute-done((f32[4,2048]{1,0:T(4,128)S(1)}, f32[4,2048]{1,0:T(4,128)S(1)}, u32[]{:S(2)}, u32[]{:S(2)}) %collective-permute-start.98) | collective-permute-done | bytes 32800 | tf_op jit(solution)/shard_map/ppermute | solution.py:73
  771.9 11.0 %collective-permute-done.96 = bf16[2,64,2048]{2,1,0:T(8,128)(2,1)S(1)} collective-permute-done((bf16[2,64,2048]{2,1,0:T(8,128)(2,1)}, bf16[2,64,2048]{2,1,0:T(8,128)(2,1)S(1)}, u32[]{:S(2)}, u32[]{:S(2)}) %collective-permute-start.96) | collective-permute-done | bytes 524320 | tf_op jit(solution)/shard_map/ppermute | solution.py:73
  805.9 10.7 %collective-permute-done.87 = bf16[128,2048]{1,0:T(8,128)(2,1)} collective-permute-done((bf16[128,2048]{1,0:T(8,128)(2,1)}, bf16[128,2048]{1,0:T(8,128)(2,1)}, u32[]{:S(2)}, u32[]{:S(2)}) %collective-permute-start.87) | collective-permute-done | bytes 524320 | tf_op jit(solution)/shard_map/ppermute | solution.py:73
  (630 shorter events, 469.1 us)
Async XLA Ops:
  7.2 111.0 %all-gather.5.cloned.1.call-start = ((), (), s32[]{:S(2)}) async-start(), calls=%async_computation.4 | async-start | bytes 3932160 | tf_op jit(solution)/shard_map/all_gather | solution.py:79
  27.2 145.6 %all-gather.7.cloned.1.call-start = ((), (), s32[]{:S(2)}) async-start(), calls=%async_computation.5 | async-start | bytes 1310720 | tf_op jit(solution)/shard_map/all_gather | solution.py:79
  75.9 195.1 %all-gather.9.cloned.1.call-start = ((), (), s32[]{:S(2)}) async-start(), calls=%async_computation.6 | async-start | bytes 10485760 | tf_op jit(solution)/shard_map/all_gather | solution.py:79
  81.7 24.5 %collective-permute-start.16 = (bf16[2,64,2048]{2,1,0:T(8,128)(2,1)S(1)}, bf16[2,64,2048]{2,1,0:T(8,128)(2,1)}, u32[]{:S(2)}, u32[]{:S(2)}) collective-permute-start(bf16[2,64,2048]{2,1,0:T(8,128)(2,1)S(1)} %get-tuple-element.53), channel_id=1, source_target_pairs={{0,6},{1,7},{2,4},{3,5},{4,2},{5,3},{6,0},{7,1},{8,14},{9,15},{10,... | collective-permute-start | bytes 1572872 | tf_op jit(solution)/shard_map/ppermute | solution.py:73
  117.9 233.5 %all-gather.11.cloned.1.call-start = ((), (), s32[]{:S(2)}) async-start(), calls=%async_computation.7 | async-start | bytes 5242880 | tf_op jit(solution)/shard_map/all_gather | solution.py:79
  185.1 25.1 %collective-permute-start.30 = (bf16[128,2048]{1,0:T(8,128)(2,1)S(1)}, bf16[128,2048]{1,0:T(8,128)(2,1)S(1)}, u32[]{:S(2)}, u32[]{:S(2)}) collective-permute-start(bf16[128,2048]{1,0:T(8,128)(2,1)S(1)} %slice.742), channel_id=1, source_target_pairs={{0,2},{1,3},{2,0},{3,1},{4,6},{5,7},{6,4},{7,5},{8,10},{9,11},{10,... | collective-permute-start | bytes 1572872 | tf_op jit(solution)/shard_map/ppermute | solution.py:73
  250.9 352.2 %reduce-scatter.5.cloned.1.call-start = ((), (), s32[]{:S(2)}) async-start(), calls=%async_computation.8 | async-start | bytes 5242880 | tf_op jit(solution)/shard_map/reduce_scatter | solution.py:82
  371.5 24.5 %collective-permute-start.48 = (bf16[128,2048]{1,0:T(8,128)(2,1)S(1)}, bf16[128,2048]{1,0:T(8,128)(2,1)S(1)}, u32[]{:S(2)}, u32[]{:S(2)}) collective-permute-start(bf16[128,2048]{1,0:T(8,128)(2,1)S(1)} %slice.740), channel_id=1, source_target_pairs={{0,2},{1,3},{2,0},{3,1},{4,6},{5,7},{6,4},{7,5},{8,10},{9,11},{10,... | collective-permute-start | bytes 1572872 | tf_op jit(solution)/shard_map/ppermute | solution.py:73
  409.3 24.7 %collective-permute-start.49 = (bf16[256,2048]{1,0:T(8,128)(2,1)S(1)}, bf16[256,2048]{1,0:T(8,128)(2,1)S(1)}, u32[]{:S(2)}, u32[]{:S(2)}) collective-permute-start(bf16[256,2048]{1,0:T(8,128)(2,1)S(1)} %get-tuple-element.97), channel_id=1, source_target_pairs={{0,2},{1,3},{2,0},{3,1},{4,6},{5,7},{6,4},{7,5},{8,10},{9,11},{10,... | collective-permute-start | bytes 3145736 | tf_op jit(solution)/shard_map/ppermute | solution.py:73
  461.9 233.7 %reduce-scatter.7.cloned.1.call-start = ((), (), s32[]{:S(2)}) async-start(), calls=%async_computation.9 | async-start | bytes 10485760 | tf_op jit(solution)/shard_map/reduce_scatter | solution.py:82
  514.2 37.9 %collective-permute-start.57 = (bf16[256,2048]{1,0:T(8,128)(2,1)}, bf16[256,2048]{1,0:T(8,128)(2,1)}, u32[]{:S(2)}, u32[]{:S(2)}) collective-permute-start(bf16[256,2048]{1,0:T(8,128)(2,1)} %get-tuple-element.126), channel_id=1, source_target_pairs={{0,1},{1,0},{2,3},{3,2},{4,5},{5,4},{6,7},{7,6},{8,9},{9,8},{10,11... | collective-permute-start | bytes 3145736 | tf_op jit(solution)/shard_map/ppermute | solution.py:73
  515.1 37.1 %collective-permute-start.66 = (bf16[128,2048]{1,0:T(8,128)(2,1)}, bf16[128,2048]{1,0:T(8,128)(2,1)}, u32[]{:S(2)}, u32[]{:S(2)}) collective-permute-start(bf16[128,2048]{1,0:T(8,128)(2,1)} %slice.738), channel_id=1, source_target_pairs={{0,2},{1,3},{2,0},{3,1},{4,6},{5,7},{6,4},{7,5},{8,10},{9,11},{10,... | collective-permute-start | bytes 1572872 | tf_op jit(solution)/shard_map/ppermute | solution.py:73
  516.9 35.2 %collective-permute-start.59 = (bf16[128,2048]{1,0:T(8,128)(2,1)}, bf16[128,2048]{1,0:T(8,128)(2,1)}, u32[]{:S(2)}, u32[]{:S(2)}) collective-permute-start(bf16[128,2048]{1,0:T(8,128)(2,1)} %slice.739), channel_id=1, source_target_pairs={{0,4},{1,5},{2,6},{3,7},{4,0},{5,1},{6,2},{7,3},{8,12},{9,13},{10,... | collective-permute-start | bytes 1572872 | tf_op jit(solution)/shard_map/ppermute | solution.py:73
  552.1 203.0 %reduce-scatter.11.cloned.1.call-start = ((), (), s32[]{:S(2)}) async-start(), calls=%async_computation.11 | async-start | bytes 1310720 | tf_op jit(solution)/shard_map/reduce_scatter | solution.py:82
  660.8 144.1 %reduce-scatter.9.cloned.1.call-start = ((), (), s32[]{:S(2)}) async-start(), calls=%async_computation.10 | async-start | bytes 3932160 | tf_op jit(solution)/shard_map/reduce_scatter | solution.py:82
  723.1 59.8 %collective-permute-start.86 = (bf16[256,2048]{1,0:T(8,128)(2,1)}, bf16[256,2048]{1,0:T(8,128)(2,1)S(1)}, u32[]{:S(2)}, u32[]{:S(2)}) collective-permute-start(bf16[256,2048]{1,0:T(8,128)(2,1)} %get-tuple-element.122), channel_id=1, source_target_pairs={{0,1},{1,0},{2,3},{3,2},{4,5},{5,4},{6,7},{7,6},{8,9},{9,8},{10,11... | collective-permute-start | bytes 3145736 | tf_op jit(solution)/shard_map/ppermute | solution.py:73
  723.6 59.4 %collective-permute-start.83 = (bf16[256,2048]{1,0:T(8,128)(2,1)}, bf16[256,2048]{1,0:T(8,128)(2,1)}, u32[]{:S(2)}, u32[]{:S(2)}) collective-permute-start(bf16[256,2048]{1,0:T(8,128)(2,1)} %get-tuple-element.123), channel_id=1, source_target_pairs={{0,1},{1,0},{2,3},{3,2},{4,5},{5,4},{6,7},{7,6},{8,9},{9,8},{10,11... | collective-permute-start | bytes 3145736 | tf_op jit(solution)/shard_map/ppermute | solution.py:73
  723.6 60.1 %collective-permute-start.81 = (bf16[256,2048]{1,0:T(8,128)(2,1)}, bf16[256,2048]{1,0:T(8,128)(2,1)}, u32[]{:S(2)}, u32[]{:S(2)}) collective-permute-start(bf16[256,2048]{1,0:T(8,128)(2,1)} %get-tuple-element.124), channel_id=1, source_target_pairs={{0,1},{1,0},{2,3},{3,2},{4,5},{5,4},{6,7},{7,6},{8,9},{9,8},{10,11... | collective-permute-start | bytes 3145736 | tf_op jit(solution)/shard_map/ppermute | solution.py:73
  724.1 34.3 %collective-permute-start.94 = (bf16[2,64,2048]{2,1,0:T(8,128)(2,1)}, bf16[2,64,2048]{2,1,0:T(8,128)(2,1)}, u32[]{:S(2)}, u32[]{:S(2)}) collective-permute-start(bf16[2,64,2048]{2,1,0:T(8,128)(2,1)} %get-tuple-element.73), channel_id=1, source_target_pairs={{0,2},{1,3},{2,0},{3,1},{4,6},{5,7},{6,4},{7,5},{8,10},{9,11},{10,... | collective-permute-start | bytes 1572872 | tf_op jit(solution)/shard_map/ppermute | solution.py:73
  758.4 24.6 %collective-permute-start.96 = (bf16[2,64,2048]{2,1,0:T(8,128)(2,1)}, bf16[2,64,2048]{2,1,0:T(8,128)(2,1)S(1)}, u32[]{:S(2)}, u32[]{:S(2)}) collective-permute-start(bf16[2,64,2048]{2,1,0:T(8,128)(2,1)} %get-tuple-element.75), channel_id=1, source_target_pairs={{0,6},{1,7},{2,4},{3,5},{4,2},{5,3},{6,0},{7,1},{8,14},{9,15},{10,... | collective-permute-start | bytes 1572872 | tf_op jit(solution)/shard_map/ppermute | solution.py:73
  771.9 63.1 %collective-permute-start.80 = (bf16[256,2048]{1,0:T(8,128)(2,1)}, bf16[256,2048]{1,0:T(8,128)(2,1)}, u32[]{:S(2)}, u32[]{:S(2)}) collective-permute-start(bf16[256,2048]{1,0:T(8,128)(2,1)} %get-tuple-element.125), channel_id=1, source_target_pairs={{0,1},{1,0},{2,3},{3,2},{4,5},{5,4},{6,7},{7,6},{8,9},{9,8},{10,11... | collective-permute-start | bytes 3145736 | tf_op jit(solution)/shard_map/ppermute | solution.py:73
  790.3 45.3 %collective-permute-start.82 = (bf16[128,2048]{1,0:T(8,128)(2,1)}, bf16[128,2048]{1,0:T(8,128)(2,1)S(1)}, u32[]{:S(2)}, u32[]{:S(2)}) collective-permute-start(bf16[128,2048]{1,0:T(8,128)(2,1)} %slice.737), channel_id=1, source_target_pairs={{0,4},{1,5},{2,6},{3,7},{4,0},{5,1},{6,2},{7,3},{8,12},{9,13},{10,... | collective-permute-start | bytes 1572872 | tf_op jit(solution)/shard_map/ppermute | solution.py:73
  792.6 44.5 %collective-permute-start.89 = (bf16[128,2048]{1,0:T(8,128)(2,1)}, bf16[128,2048]{1,0:T(8,128)(2,1)S(1)}, u32[]{:S(2)}, u32[]{:S(2)}) collective-permute-start(bf16[128,2048]{1,0:T(8,128)(2,1)} %slice.736), channel_id=1, source_target_pairs={{0,2},{1,3},{2,0},{3,1},{4,6},{5,7},{6,4},{7,5},{8,10},{9,11},{10,... | collective-permute-start | bytes 1572872 | tf_op jit(solution)/shard_map/ppermute | solution.py:73
  803.4 35.2 %collective-permute-start.85 = (bf16[128,2048]{1,0:T(8,128)(2,1)}, bf16[128,2048]{1,0:T(8,128)(2,1)}, u32[]{:S(2)}, u32[]{:S(2)}) collective-permute-start(bf16[128,2048]{1,0:T(8,128)(2,1)} %fusion.83), channel_id=1, source_target_pairs={{0,4},{1,5},{2,6},{3,7},{4,0},{5,1},{6,2},{7,3},{8,12},{9,13},{10,... | collective-permute-start | bytes 1572872 | tf_op jit(solution)/shard_map/ppermute | solution.py:73
  (157 other events, 1584.5 us)
Sparse Core Ops, SparseCore 0:
  27.3 64.8 all-gather.4
  93.8 26.6 all-gather.6
  122.0 148.9 all-gather.8
  272.5 78.9 all-gather.10
  462.0 74.7 reduce-scatter.4
  552.2 143.3 reduce-scatter.6
  697.9 27.8 reduce-scatter.10
  728.1 60.3 reduce-scatter.8

commit v7 on v6

--- a/solution.py
+++ b/solution.py
@@ -322,11 +322,19 @@
     grad_kp = key_scale * scaled_k - key_pre * key_scale**3 * mean_k
     gain_query = jnp.sum(e_query * query_pre * query_scale, axis=(0, 2)).reshape(wide)
     gain_key = jnp.sum(e_key * key_pre * key_scale, axis=(0, 2)).reshape(wide)
+    own_terms = jnp.zeros((size, 2, wide), F32)
+    own_terms = lax.dynamic_update_slice(own_terms, jnp.stack([gain_query, gain_key])[None], (c.g, 0, 0))
+    if pairs:
+        own_terms = own_terms.reshape(half_group, 2, 2, hl, HD).transpose(2, 1, 3, 0, 4)
+    else:
+        own_terms = own_terms.transpose(1, 0, 2)
+    terms = jnp.concatenate([own_terms.reshape(2, d), jnp.stack([gain_attn, gain_mlp])])
+    grad_gains = c.sum_all(terms)
     grad_mixed = by_tokens(
         jnp.concatenate([grad_qp.astype(BF), grad_kp.astype(BF), grad_value.astype(BF)], axis=1)
     )
     back_gu = c.exchange_pair(sum_gu.reshape(size, n_in, 2 * ffl), c.swap)
-    grad_mixed = after(grad_mixed, back_gu)
+    grad_mixed = after(grad_mixed, back_gu, grad_gains)
     g_qkv = dot_tn(x_full, grad_mixed).astype(BF)
     sum_qkv = c.scatter(g_qkv)
     back_gu = c.exchange_chips(back_gu, c.swap)
@@ -340,15 +348,6 @@
     else:
         grad_qkv = back_qkv.reshape(size, n_in, 3, wide).transpose(1, 2, 0, 3)
 
-    own_terms = jnp.zeros((size, 2, wide), F32)
-    own_terms = lax.dynamic_update_slice(own_terms, jnp.stack([gain_query, gain_key])[None], (c.g, 0, 0))
-    if pairs:
-        own_terms = own_terms.reshape(half_group, 2, 2, hl, HD).transpose(2, 1, 3, 0, 4)
-    else:
-        own_terms = own_terms.transpose(1, 0, 2)
-    terms = jnp.concatenate([own_terms.reshape(2, d), jnp.stack([gain_attn, gain_mlp])])
-    grad_gains = c.sum_all(terms)
-
     return (
         output.reshape(layer_input.shape),
         grad_input.reshape(layer_input.shape),

time: 864 us -> 854 us (0.988)
    reduce_scatter x4, waiting for transfers between devices: 14.5 us -> 0.01 us  [scatter(): lax.psum_scatter(parts, ('rows', 'seq'), scatter_dimension=0, tiled=True,...]
    ppermute x102, waiting for transfers between devices: 289 us -> 304 us  [send(): return lax.ppermute(v, ('rows', 'seq'), pairs)]
    unnamed x193 -> x185, local copies, waits for them, and re-layouts: 52.6 us -> 47.1 us
where the time goes in v7:
time: 854 us; the launch traced here: 848 us
  waiting for transfers between devices  354 us (41%)
  matrix products  211 us (25%)
  local copies, waits for them, and re-layouts  105 us (12%)
  other arithmetic  83.6 us (10%)
  starting transfers between devices  77.6 us (9%)
  between operations  16.7 us (2%)
    ppermute x102, waiting for transfers between devices, send(): return lax.ppermute(v, ('rows', 'seq'), pairs)  304 us
    ppermute x102, starting transfers between devices, send(): return lax.ppermute(v, ('rows', 'seq'), pairs)  76.7 us
    dot_general x6, matrix products, dot_nt(): lax.dot_general(a, b, (((1,), (1,)), ((), ())), preferred_element_type=F32)  63.6 us
    dot_general x4, matrix products, dot_tn(): lax.dot_general(a, b, (((0,), (0,)), ((), ())), preferred_element_type=F32)  50.5 us
    dot_general x6, matrix products, dot_nn(): lax.dot_general(a, b, (((1,), (0,)), ((), ())), preferred_element_type=F32)  50.4 us
    all_gather x4, waiting for transfers between devices, gather(): lax.all_gather(block, ('rows', 'seq'), axis=0, tiled=True, axis_index_gro...  49.8 us
    unnamed x185, local copies, waits for them, and re-layouts  47.1 us
  transfers between devices with their start and end apart: 110, of which 51 were waited for; matrix products, arithmetic and copies ran while one was open for 41% of the time, Pallas kernels for 0%

profile of v7, /device:TPU:0, one launch (start us, length us, event | category | flops | bytes accessed | tf_op | source)
XLA Modules:
  0.0 847.5 jit_solution(17932883584614805790)
XLA Ops:
  41.8 12.5 %collective-permute-done.6 = bf16[256,2048]{1,0:T(8,128)(2,1)} collective-permute-done((bf16[256,2048]{1,0:T(8,128)(2,1)S(1)}, bf16[256,2048]{1,0:T(8,128)(2,1)}, u32[]{:S(2)}, u32[]{:S(2)}) %collective-permute-start.6) | collective-permute-done | bytes 1048608 | tf_op jit(solution)/shard_map/ppermute | solution.py:73
  95.6 10.7 %collective-permute-done.16 = bf16[2,64,2048]{2,1,0:T(8,128)(2,1)} collective-permute-done((bf16[2,64,2048]{2,1,0:T(8,128)(2,1)S(1)}, bf16[2,64,2048]{2,1,0:T(8,128)(2,1)}, u32[]{:S(2)}, u32[]{:S(2)}) %collective-permute-start.16) | collective-permute-done | bytes 524320 | tf_op jit(solution)/shard_map/ppermute | solution.py:73
  118.2 10.0 %fusion.151 = (bf16[2048,768]{1,0:T(8,128)(2,1)S(1)}, f32[2048,768]{1,0:T(8,128)S(1)}) fusion(bf16[2048,2048]{1,0:T(8,128)(2,1)} %copy-done.51, bf16[2048,768]{1,0:T(8,128)(2,1)} %all-gather.5.cloned.1.call-done), kind=kOutput, calls=%fused_computation.385 | convolution fusion | flops 6444023808 | bytes 20971520 | tf_op jit(solution)/shard_map/dot_general | solution.py:31
  148.3 11.8 %fusion.152 = (f32[2,2,1024]{2,1,0:T(2,128)S(1)}, f32[2,2,1024,1024]{2,3,1,0:T(8,128)}) fusion(pred[2,1024,1024]{1,2,0:T(8,128)(4,1)} %compare_and_fusion, bf16[2,2,1024,128]{3,2,1,0:T(8,128)(2,1)} %get-tuple-element.152, bf16[2,2,1024,128]{3,2,1,0:T(8,128)(2,1)} %get-tuple-element.151), kind=kOutput, calls=%fused_computation.386 | convolution fusion | flops 1090520064 | bytes 20987904 | tf_op jit(solution)/shard_map/sub | solution.py:243
  188.0 10.5 %collective-permute-done.28 = bf16[128,2048]{1,0:T(8,128)(2,1)S(1)} collective-permute-done((bf16[128,2048]{1,0:T(8,128)(2,1)S(1)}, bf16[128,2048]{1,0:T(8,128)(2,1)S(1)}, u32[]{:S(2)}, u32[]{:S(2)}) %collective-permute-start.28) | collective-permute-done | bytes 524320 | tf_op jit(solution)/shard_map/ppermute | solution.py:73
  210.3 10.1 %collective-permute-done.29 = bf16[128,2048]{1,0:T(8,128)(2,1)S(1)} collective-permute-done((bf16[128,2048]{1,0:T(8,128)(2,1)S(1)}, bf16[128,2048]{1,0:T(8,128)(2,1)S(1)}, u32[]{:S(2)}, u32[]{:S(2)}) %collective-permute-start.29) | collective-permute-done | bytes 524320 | tf_op jit(solution)/shard_map/ppermute | solution.py:73
  225.1 22.2 %collective-permute-done.32 = bf16[256,2048]{1,0:T(8,128)(2,1)S(1)} collective-permute-done((bf16[256,2048]{1,0:T(8,128)(2,1)S(1)}, bf16[256,2048]{1,0:T(8,128)(2,1)S(1)}, u32[]{:S(2)}, u32[]{:S(2)}) %collective-permute-start.32) | collective-permute-done | bytes 1048608 | tf_op jit(solution)/shard_map/ppermute | solution.py:73
  271.0 24.4 %fusion.153 = f32[2048,2048]{0,1:T(8,128)} fusion(bf16[2048,2048]{1,0:T(8,128)(2,1)} %constant_dynamic-update-slice_fusion.17, bf16[2048,2048]{1,0:T(8,128)(2,1)} %all-gather.9.cloned.1.call-done), kind=kOutput, calls=%fused_computation.387 | convolution fusion | flops 17179869184 | bytes 33554432 | tf_op jit(solution)/shard_map/dot_general | solution.py:31
  304.5 47.0 %all-gather.11.cloned.1.call-done = bf16[1024,2048]{1,0:T(8,128)(2,1)} async-done(((bf16[256,2048]{1,0:T(8,128)(2,1)}), bf16[1024,2048]{1,0:T(8,128)(2,1)}) %all-gather.11.cloned.1.call-update) | async-done | bytes 4194320 | tf_op jit(solution)/shard_map/all_gather | solution.py:79
  372.8 10.5 %collective-permute-done.46 = bf16[128,2048]{1,0:T(8,128)(2,1)S(1)} collective-permute-done((bf16[128,2048]{1,0:T(8,128)(2,1)S(1)}, bf16[128,2048]{1,0:T(8,128)(2,1)S(1)}, u32[]{:S(2)}, u32[]{:S(2)}) %collective-permute-start.46) | collective-permute-done | bytes 524320 | tf_op jit(solution)/shard_map/ppermute | solution.py:73
  410.7 21.6 %collective-permute-done.50 = bf16[256,2048]{1,0:T(8,128)(2,1)S(1)} collective-permute-done((bf16[256,2048]{1,0:T(8,128)(2,1)S(1)}, bf16[256,2048]{1,0:T(8,128)(2,1)S(1)}, u32[]{:S(2)}, u32[]{:S(2)}) %collective-permute-start.50) | collective-permute-done | bytes 1048608 | tf_op jit(solution)/shard_map/ppermute | solution.py:73
  451.5 10.5 %convolution_convert_fusion = bf16[1024,2048]{1,0:T(8,128)(2,1)} fusion(bf16[2048,1024]{0,1:T(8,128)(2,1)S(1)} %copy-done.28, bf16[2048,2048]{1,0:T(8,128)(2,1)S(1)} %constant_dynamic-update-slice_fusion.26), kind=kOutput, calls=%fused_computation.31 | convolution fusion | flops 8592031744 | bytes 16777216 | tf_op jit(solution)/shard_map/dot_general | solution.py:39
  462.1 20.9 %multiply_convert_fusion.1 = (bf16[2048,1024]{0,1:T(8,128)(2,1)S(1)}, bf16[2048,1024]{0,1:T(8,128)(2,1)}) fusion(f32[2048,2048]{0,1:T(8,128)} %fusion.153, bf16[2048,2048]{1,0:T(8,128)(2,1)} %copy-done.52, bf16[1024,2048]{1,0:T(8,128)(2,1)} %all-gather.11.cloned.1.call-done), kind=kOutput, calls=%fused_computation.12 | convolution fusion | flops 8617197568 | bytes 37748736 | tf_op jit(solution)/shard_map/dot_general | solution.py:35
  485.0 22.8 %fusion.7 = bf16[2048,2048]{1,0:T(8,128)(2,1)} fusion(bf16[2048,2048]{1,0:T(8,128)(2,1)} %constant_dynamic-update-slice_fusion.17, bf16[2048,1024]{0,1:T(8,128)(2,1)S(1)} %get-tuple-element.104, bf16[2048,1024]{0,1:T(8,128)(2,1)} %get-tuple-element.105), kind=kOutput, calls=%fused_computation.22 | convolution fusion | flops 17200840704 | bytes 25165824 | tf_op jit(solution)/shard_map/dot_general | solution.py:39
  507.9 12.8 %fusion.18 = bf16[1024,2048]{1,0:T(8,128)(2,1)S(1)} fusion(bf16[2048,2048]{1,0:T(8,128)(2,1)} %all-gather.9.cloned.1.call-done, bf16[2048,1024]{0,1:T(8,128)(2,1)} %get-tuple-element.105, bf16[2048,1024]{0,1:T(8,128)(2,1)} %copy-done.66), kind=kOutput, calls=%fused_computation.35 | convolution fusion | flops 8600420352 | bytes 20971520 | tf_op jit(solution)/shard_map/dot_general | solution.py:35
  521.7 12.6 %fusion.9 = f32[1024,2048]{1,0:T(8,128)S(1)} fusion(bf16[2048,2048]{1,0:T(8,128)(2,1)} %all-gather.9.cloned.1.call-done, bf16[2048,1024]{0,1:T(8,128)(2,1)} %get-tuple-element.105, bf16[2048,1024]{0,1:T(8,128)(2,1)} %copy-done.66), kind=kOutput, calls=%fused_computation.24 | convolution fusion | flops 8598323200 | bytes 25165824 | tf_op jit(solution)/shard_map/dot_general | solution.py:35
  539.9 10.4 %collective-permute-done.64 = bf16[128,2048]{1,0:T(8,128)(2,1)S(1)} collective-permute-done((bf16[128,2048]{1,0:T(8,128)(2,1)S(1)}, bf16[128,2048]{1,0:T(8,128)(2,1)S(1)}, u32[]{:S(2)}, u32[]{:S(2)}) %collective-permute-start.64) | collective-permute-done | bytes 524320 | tf_op jit(solution)/shard_map/ppermute | solution.py:73
  562.1 10.3 %collective-permute-done.65 = bf16[128,2048]{1,0:T(8,128)(2,1)S(1)} collective-permute-done((bf16[128,2048]{1,0:T(8,128)(2,1)S(1)}, bf16[128,2048]{1,0:T(8,128)(2,1)S(1)}, u32[]{:S(2)}, u32[]{:S(2)}) %collective-permute-start.65) | collective-permute-done | bytes 524320 | tf_op jit(solution)/shard_map/ppermute | solution.py:73
  580.0 22.4 %collective-permute-done.68 = bf16[256,2048]{1,0:T(8,128)(2,1)S(1)} collective-permute-done((bf16[256,2048]{1,0:T(8,128)(2,1)S(1)}, bf16[256,2048]{1,0:T(8,128)(2,1)S(1)}, u32[]{:S(2)}, u32[]{:S(2)}) %collective-permute-start.68) | collective-permute-done | bytes 1048608 | tf_op jit(solution)/shard_map/ppermute | solution.py:73
  642.6 11.1 %multiply_reduce_fusion = (f32[2,2,1024]{2,1,0:T(2,128)S(1)}, f32[2,2,1024,1024]{2,3,1,0:T(8,128)}) fusion(f32[2,2,1024,1024]{2,3,1,0:T(8,128)} %get-tuple-element.231, f32[2,2,1024]{2,1,0:T(2,128)S(1)} %copy-done.60, bf16[2,2,1024,128]{3,2,1,0:T(8,128)(2,1)S(1)} %bitcast.311, bf16[2,2,1024,128]{3,2,1,0:T(8,128)(2,1)S(1)} %bitcast.310), kind=kOutput, calls=%fused_computation.2 | convolution fusion | flops 1086320640 | bytes 35684352 | tf_op jit(solution)/shard_map/rhqd,rhkd->rhqk/dot_general | solution.py:306
  653.7 12.2 %multiply_convert_fusion = bf16[2,2,1024,1024]{2,3,1,0:T(8,128)(2,1)S(1)} fusion(f32[2,2,1024,1024]{2,3,1,0:T(8,128)} %get-tuple-element.233, f32[2,2,1024]{2,1,0:T(2,128)S(1)} %get-tuple-element.232, f32[2,2,1024,1024]{2,3,1,0:T(8,128)} %get-tuple-element.231, f32[2,2,1024]{2,1,0:T(2,128)S(1)} %copy-done.60), kind=kLoop, calls=%fused_computation.1 | loop fusion | flops 16777216 | bytes 41975808 | tf_op jit(solution)/shard_map/convert_element_type | solution.py:309
  721.6 10.4 %convolution_convert_fusion.4 = bf16[2048,768]{1,0:T(8,128)(2,1)} fusion(bf16[2048,2048]{1,0:T(8,128)(2,1)} %copy-done.51, bf16[2048,768]{1,0:T(8,128)(2,1)S(1)} %bitcast.292), kind=kOutput, calls=%fused_computation.36 | convolution fusion | flops 6444023808 | bytes 14680064 | tf_op jit(solution)/shard_map/dot_general | solution.py:39
  761.0 11.3 %collective-permute-done.101 = bf16[2,64,2048]{2,1,0:T(8,128)(2,1)S(1)} collective-permute-done((bf16[2,64,2048]{2,1,0:T(8,128)(2,1)}, bf16[2,64,2048]{2,1,0:T(8,128)(2,1)S(1)}, u32[]{:S(2)}, u32[]{:S(2)}) %collective-permute-start.101) | collective-permute-done | bytes 524320 | tf_op jit(solution)/shard_map/ppermute | solution.py:73
  795.2 11.1 %collective-permute-done.92 = bf16[128,2048]{1,0:T(8,128)(2,1)} collective-permute-done((bf16[128,2048]{1,0:T(8,128)(2,1)}, bf16[128,2048]{1,0:T(8,128)(2,1)}, u32[]{:S(2)}, u32[]{:S(2)}) %collective-permute-start.92) | collective-permute-done | bytes 524320 | tf_op jit(solution)/shard_map/ppermute | solution.py:73
  (622 shorter events, 460.9 us)
Async XLA Ops:
  7.2 111.1 %all-gather.5.cloned.1.call-start = ((), (), s32[]{:S(2)}) async-start(), calls=%async_computation.4 | async-start | bytes 3932160 | tf_op jit(solution)/shard_map/all_gather | solution.py:79
  27.2 145.7 %all-gather.7.cloned.1.call-start = ((), (), s32[]{:S(2)}) async-start(), calls=%async_computation.5 | async-start | bytes 1310720 | tf_op jit(solution)/shard_map/all_gather | solution.py:79
  76.0 195.1 %all-gather.9.cloned.1.call-start = ((), (), s32[]{:S(2)}) async-start(), calls=%async_computation.6 | async-start | bytes 10485760 | tf_op jit(solution)/shard_map/all_gather | solution.py:79
  81.8 24.5 %collective-permute-start.16 = (bf16[2,64,2048]{2,1,0:T(8,128)(2,1)S(1)}, bf16[2,64,2048]{2,1,0:T(8,128)(2,1)}, u32[]{:S(2)}, u32[]{:S(2)}) collective-permute-start(bf16[2,64,2048]{2,1,0:T(8,128)(2,1)S(1)} %get-tuple-element.53), channel_id=1, source_target_pairs={{0,6},{1,7},{2,4},{3,5},{4,2},{5,3},{6,0},{7,1},{8,14},{9,15},{10,... | collective-permute-start | bytes 1572872 | tf_op jit(solution)/shard_map/ppermute | solution.py:73
  118.0 233.5 %all-gather.11.cloned.1.call-start = ((), (), s32[]{:S(2)}) async-start(), calls=%async_computation.7 | async-start | bytes 5242880 | tf_op jit(solution)/shard_map/all_gather | solution.py:79
  185.2 25.1 %collective-permute-start.30 = (bf16[128,2048]{1,0:T(8,128)(2,1)S(1)}, bf16[128,2048]{1,0:T(8,128)(2,1)S(1)}, u32[]{:S(2)}, u32[]{:S(2)}) collective-permute-start(bf16[128,2048]{1,0:T(8,128)(2,1)S(1)} %slice.742), channel_id=1, source_target_pairs={{0,2},{1,3},{2,0},{3,1},{4,6},{5,7},{6,4},{7,5},{8,10},{9,11},{10,... | collective-permute-start | bytes 1572872 | tf_op jit(solution)/shard_map/ppermute | solution.py:73
  223.1 24.2 %collective-permute-start.32 = (bf16[256,2048]{1,0:T(8,128)(2,1)S(1)}, bf16[256,2048]{1,0:T(8,128)(2,1)S(1)}, u32[]{:S(2)}, u32[]{:S(2)}) collective-permute-start(bf16[256,2048]{1,0:T(8,128)(2,1)S(1)} %get-tuple-element.101), channel_id=1, source_target_pairs={{0,4},{1,5},{2,6},{3,7},{4,0},{5,1},{6,2},{7,3},{8,12},{9,13},{10,... | collective-permute-start | bytes 3145736 | tf_op jit(solution)/shard_map/ppermute | solution.py:73
  224.6 24.4 %collective-permute-start.31 = (bf16[256,2048]{1,0:T(8,128)(2,1)S(1)}, bf16[256,2048]{1,0:T(8,128)(2,1)S(1)}, u32[]{:S(2)}, u32[]{:S(2)}) collective-permute-start(bf16[256,2048]{1,0:T(8,128)(2,1)S(1)} %get-tuple-element.101), channel_id=1, source_target_pairs={{0,2},{1,3},{2,0},{3,1},{4,6},{5,7},{6,4},{7,5},{8,10},{9,11},{10,... | collective-permute-start | bytes 3145736 | tf_op jit(solution)/shard_map/ppermute | solution.py:73
  251.0 371.2 %reduce-scatter.5.cloned.1.call-start = ((), (), s32[]{:S(2)}) async-start(), calls=%async_computation.8 | async-start | bytes 5242880 | tf_op jit(solution)/shard_map/reduce_scatter | solution.py:82
  371.5 24.5 %collective-permute-start.48 = (bf16[128,2048]{1,0:T(8,128)(2,1)S(1)}, bf16[128,2048]{1,0:T(8,128)(2,1)S(1)}, u32[]{:S(2)}, u32[]{:S(2)}) collective-permute-start(bf16[128,2048]{1,0:T(8,128)(2,1)S(1)} %slice.740), channel_id=1, source_target_pairs={{0,2},{1,3},{2,0},{3,1},{4,6},{5,7},{6,4},{7,5},{8,10},{9,11},{10,... | collective-permute-start | bytes 1572872 | tf_op jit(solution)/shard_map/ppermute | solution.py:73
  409.3 24.7 %collective-permute-start.49 = (bf16[256,2048]{1,0:T(8,128)(2,1)S(1)}, bf16[256,2048]{1,0:T(8,128)(2,1)S(1)}, u32[]{:S(2)}, u32[]{:S(2)}) collective-permute-start(bf16[256,2048]{1,0:T(8,128)(2,1)S(1)} %get-tuple-element.97), channel_id=1, source_target_pairs={{0,2},{1,3},{2,0},{3,1},{4,6},{5,7},{6,4},{7,5},{8,10},{9,11},{10,... | collective-permute-start | bytes 3145736 | tf_op jit(solution)/shard_map/ppermute | solution.py:73
  462.0 241.9 %reduce-scatter.7.cloned.1.call-start = ((), (), s32[]{:S(2)}) async-start(), calls=%async_computation.9 | async-start | bytes 10485760 | tf_op jit(solution)/shard_map/reduce_scatter | solution.py:82
  507.8 236.4 %reduce-scatter.11.cloned.1.call-start = ((), (), s32[]{:S(2)}) async-start(), calls=%async_computation.11 | async-start | bytes 1310720 | tf_op jit(solution)/shard_map/reduce_scatter | solution.py:82
  537.2 24.9 %collective-permute-start.66 = (bf16[128,2048]{1,0:T(8,128)(2,1)S(1)}, bf16[128,2048]{1,0:T(8,128)(2,1)S(1)}, u32[]{:S(2)}, u32[]{:S(2)}) collective-permute-start(bf16[128,2048]{1,0:T(8,128)(2,1)S(1)} %slice.738), channel_id=1, source_target_pairs={{0,2},{1,3},{2,0},{3,1},{4,6},{5,7},{6,4},{7,5},{8,10},{9,11},{10,... | collective-permute-start | bytes 1572872 | tf_op jit(solution)/shard_map/ppermute | solution.py:73
  577.9 24.5 %collective-permute-start.68 = (bf16[256,2048]{1,0:T(8,128)(2,1)S(1)}, bf16[256,2048]{1,0:T(8,128)(2,1)S(1)}, u32[]{:S(2)}, u32[]{:S(2)}) collective-permute-start(bf16[256,2048]{1,0:T(8,128)(2,1)S(1)} %get-tuple-element.94), channel_id=1, source_target_pairs={{0,4},{1,5},{2,6},{3,7},{4,0},{5,1},{6,2},{7,3},{8,12},{9,13},{10,... | collective-permute-start | bytes 3145736 | tf_op jit(solution)/shard_map/ppermute | solution.py:73
  639.0 155.1 %reduce-scatter.9.cloned.1.call-start = ((), (), s32[]{:S(2)}) async-start(), calls=%async_computation.10 | async-start | bytes 3932160 | tf_op jit(solution)/shard_map/reduce_scatter | solution.py:82
  742.1 30.2 %collective-permute-start.91 = (bf16[256,2048]{1,0:T(8,128)(2,1)}, bf16[256,2048]{1,0:T(8,128)(2,1)S(1)}, u32[]{:S(2)}, u32[]{:S(2)}) collective-permute-start(bf16[256,2048]{1,0:T(8,128)(2,1)} %get-tuple-element.122), channel_id=1, source_target_pairs={{0,1},{1,0},{2,3},{3,2},{4,5},{5,4},{6,7},{7,6},{8,9},{9,8},{10,11... | collective-permute-start | bytes 3145736 | tf_op jit(solution)/shard_map/ppermute | solution.py:73
  742.1 30.2 %collective-permute-start.88 = (bf16[256,2048]{1,0:T(8,128)(2,1)}, bf16[256,2048]{1,0:T(8,128)(2,1)}, u32[]{:S(2)}, u32[]{:S(2)}) collective-permute-start(bf16[256,2048]{1,0:T(8,128)(2,1)} %get-tuple-element.123), channel_id=1, source_target_pairs={{0,1},{1,0},{2,3},{3,2},{4,5},{5,4},{6,7},{7,6},{8,9},{9,8},{10,11... | collective-permute-start | bytes 3145736 | tf_op jit(solution)/shard_map/ppermute | solution.py:73
  742.6 30.4 %collective-permute-start.86 = (bf16[256,2048]{1,0:T(8,128)(2,1)}, bf16[256,2048]{1,0:T(8,128)(2,1)}, u32[]{:S(2)}, u32[]{:S(2)}) collective-permute-start(bf16[256,2048]{1,0:T(8,128)(2,1)} %get-tuple-element.124), channel_id=1, source_target_pairs={{0,1},{1,0},{2,3},{3,2},{4,5},{5,4},{6,7},{7,6},{8,9},{9,8},{10,11... | collective-permute-start | bytes 3145736 | tf_op jit(solution)/shard_map/ppermute | solution.py:73
  747.2 25.1 %collective-permute-start.101 = (bf16[2,64,2048]{2,1,0:T(8,128)(2,1)}, bf16[2,64,2048]{2,1,0:T(8,128)(2,1)S(1)}, u32[]{:S(2)}, u32[]{:S(2)}) collective-permute-start(bf16[2,64,2048]{2,1,0:T(8,128)(2,1)} %get-tuple-element.75), channel_id=1, source_target_pairs={{0,6},{1,7},{2,4},{3,5},{4,2},{5,3},{6,0},{7,1},{8,14},{9,15},{10,... | collective-permute-start | bytes 1572872 | tf_op jit(solution)/shard_map/ppermute | solution.py:73
  761.0 63.3 %collective-permute-start.85 = (bf16[256,2048]{1,0:T(8,128)(2,1)}, bf16[256,2048]{1,0:T(8,128)(2,1)}, u32[]{:S(2)}, u32[]{:S(2)}) collective-permute-start(bf16[256,2048]{1,0:T(8,128)(2,1)} %get-tuple-element.125), channel_id=1, source_target_pairs={{0,1},{1,0},{2,3},{3,2},{4,5},{5,4},{6,7},{7,6},{8,9},{9,8},{10,11... | collective-permute-start | bytes 3145736 | tf_op jit(solution)/shard_map/ppermute | solution.py:73
  780.0 45.3 %collective-permute-start.87 = (bf16[128,2048]{1,0:T(8,128)(2,1)}, bf16[128,2048]{1,0:T(8,128)(2,1)S(1)}, u32[]{:S(2)}, u32[]{:S(2)}) collective-permute-start(bf16[128,2048]{1,0:T(8,128)(2,1)} %slice.737), channel_id=1, source_target_pairs={{0,4},{1,5},{2,6},{3,7},{4,0},{5,1},{6,2},{7,3},{8,12},{9,13},{10,... | collective-permute-start | bytes 1572872 | tf_op jit(solution)/shard_map/ppermute | solution.py:73
  782.0 44.5 %collective-permute-start.94 = (bf16[128,2048]{1,0:T(8,128)(2,1)}, bf16[128,2048]{1,0:T(8,128)(2,1)S(1)}, u32[]{:S(2)}, u32[]{:S(2)}) collective-permute-start(bf16[128,2048]{1,0:T(8,128)(2,1)} %slice.736), channel_id=1, source_target_pairs={{0,2},{1,3},{2,0},{3,1},{4,6},{5,7},{6,4},{7,5},{8,10},{9,11},{10,... | collective-permute-start | bytes 1572872 | tf_op jit(solution)/shard_map/ppermute | solution.py:73
  792.7 35.1 %collective-permute-start.90 = (bf16[128,2048]{1,0:T(8,128)(2,1)}, bf16[128,2048]{1,0:T(8,128)(2,1)}, u32[]{:S(2)}, u32[]{:S(2)}) collective-permute-start(bf16[128,2048]{1,0:T(8,128)(2,1)} %fusion.83), channel_id=1, source_target_pairs={{0,4},{1,5},{2,6},{3,7},{4,0},{5,1},{6,2},{7,3},{8,12},{9,13},{10,... | collective-permute-start | bytes 1572872 | tf_op jit(solution)/shard_map/ppermute | solution.py:73
  (153 other events, 1682.1 us)
Sparse Core Ops, SparseCore 0:
  27.3 64.8 all-gather.4
  93.8 26.6 all-gather.6
  122.0 148.9 all-gather.8
  272.5 78.9 all-gather.10
  462.1 74.7 reduce-scatter.4
  539.2 145.1 reduce-scatter.6
  686.6 27.8 reduce-scatter.10
  732.1 59.4 reduce-scatter.8

commit v8 on v7

--- a/solution.py
+++ b/solution.py
@@ -342,6 +342,7 @@
     grad_input = grad_hidden + c.scatter_tokens(grad_mixed, lambda v: dot_nt(v, full_qkv))
     back_gu = back_gu.astype(F32).reshape(size, n_in, 2, copies, n_ff)
     grad_gate_up = back_gu.transpose(1, 2, 3, 0, 4)
+    sum_qkv = after(sum_qkv, grad_gate_up)
     back_qkv = c.exchange(sum_qkv.reshape(size, n_in, 3 * wide)).astype(F32)
     if pairs:
         grad_qkv = back_qkv.reshape(half_group, 2, n_in, 3, hl, HD).transpose(2, 3, 1, 4, 0, 5)

time: 854 us -> 854 us (level)
    reshape x2 -> x0, local copies, waits for them, and re-layouts: 9.28 us -> none  [per_device(): grad_gate_up.reshape(w_gate_up.shape)]
    transpose x0 -> x2, local copies, waits for them, and re-layouts: none -> 9.28 us  [per_device(): grad_gate_up = back_gu.transpose(1, 2, 3, 0, 4)]
where the time goes in v8:
time: 854 us; the launch traced here: 848 us
  waiting for transfers between devices  354 us (41%)
  matrix products  211 us (25%)
  local copies, waits for them, and re-layouts  105 us (12%)
  other arithmetic  83.6 us (10%)
  starting transfers between devices  77.6 us (9%)
  between operations  16.7 us (2%)
    ppermute x102, waiting for transfers between devices, send(): return lax.ppermute(v, ('rows', 'seq'), pairs)  304 us
    ppermute x102, starting transfers between devices, send(): return lax.ppermute(v, ('rows', 'seq'), pairs)  76.7 us
    dot_general x6, matrix products, dot_nt(): lax.dot_general(a, b, (((1,), (1,)), ((), ())), preferred_element_type=F32)  63.6 us
    dot_general x4, matrix products, dot_tn(): lax.dot_general(a, b, (((0,), (0,)), ((), ())), preferred_element_type=F32)  50.5 us
    dot_general x6, matrix products, dot_nn(): lax.dot_general(a, b, (((1,), (0,)), ((), ())), preferred_element_type=F32)  50.4 us
    all_gather x4, waiting for transfers between devices, gather(): lax.all_gather(block, ('rows', 'seq'), axis=0, tiled=True, axis_index_gro...  49.8 us
    unnamed x185, local copies, waits for them, and re-layouts  47.1 us
  transfers between devices with their start and end apart: 110, of which 51 were waited for; matrix products, arithmetic and copies ran while one was open for 41% of the time, Pallas kernels for 0%

profile of v8, /device:TPU:0, one launch (start us, length us, event | category | flops | bytes accessed | tf_op | source)
XLA Modules:
  0.0 847.5 jit_solution(17932883584614805790)
XLA Ops:
  41.8 12.5 %collective-permute-done.6 = bf16[256,2048]{1,0:T(8,128)(2,1)} collective-permute-done((bf16[256,2048]{1,0:T(8,128)(2,1)S(1)}, bf16[256,2048]{1,0:T(8,128)(2,1)}, u32[]{:S(2)}, u32[]{:S(2)}) %collective-permute-start.6) | collective-permute-done | bytes 1048608 | tf_op jit(solution)/shard_map/ppermute | solution.py:73
  95.6 10.7 %collective-permute-done.16 = bf16[2,64,2048]{2,1,0:T(8,128)(2,1)} collective-permute-done((bf16[2,64,2048]{2,1,0:T(8,128)(2,1)S(1)}, bf16[2,64,2048]{2,1,0:T(8,128)(2,1)}, u32[]{:S(2)}, u32[]{:S(2)}) %collective-permute-start.16) | collective-permute-done | bytes 524320 | tf_op jit(solution)/shard_map/ppermute | solution.py:73
  118.2 10.0 %fusion.151 = (bf16[2048,768]{1,0:T(8,128)(2,1)S(1)}, f32[2048,768]{1,0:T(8,128)S(1)}) fusion(bf16[2048,2048]{1,0:T(8,128)(2,1)} %copy-done.51, bf16[2048,768]{1,0:T(8,128)(2,1)} %all-gather.5.cloned.1.call-done), kind=kOutput, calls=%fused_computation.386 | convolution fusion | flops 6444023808 | bytes 20971520 | tf_op jit(solution)/shard_map/dot_general | solution.py:31
  148.3 11.8 %fusion.152 = (f32[2,2,1024]{2,1,0:T(2,128)S(1)}, f32[2,2,1024,1024]{2,3,1,0:T(8,128)}) fusion(pred[2,1024,1024]{1,2,0:T(8,128)(4,1)} %compare_and_fusion, bf16[2,2,1024,128]{3,2,1,0:T(8,128)(2,1)} %get-tuple-element.154, bf16[2,2,1024,128]{3,2,1,0:T(8,128)(2,1)} %get-tuple-element.153), kind=kOutput, calls=%fused_computation.387 | convolution fusion | flops 1090520064 | bytes 20987904 | tf_op jit(solution)/shard_map/sub | solution.py:243
  188.0 10.5 %collective-permute-done.28 = bf16[128,2048]{1,0:T(8,128)(2,1)S(1)} collective-permute-done((bf16[128,2048]{1,0:T(8,128)(2,1)S(1)}, bf16[128,2048]{1,0:T(8,128)(2,1)S(1)}, u32[]{:S(2)}, u32[]{:S(2)}) %collective-permute-start.28) | collective-permute-done | bytes 524320 | tf_op jit(solution)/shard_map/ppermute | solution.py:73
  210.3 10.1 %collective-permute-done.29 = bf16[128,2048]{1,0:T(8,128)(2,1)S(1)} collective-permute-done((bf16[128,2048]{1,0:T(8,128)(2,1)S(1)}, bf16[128,2048]{1,0:T(8,128)(2,1)S(1)}, u32[]{:S(2)}, u32[]{:S(2)}) %collective-permute-start.29) | collective-permute-done | bytes 524320 | tf_op jit(solution)/shard_map/ppermute | solution.py:73
  225.1 22.2 %collective-permute-done.32 = bf16[256,2048]{1,0:T(8,128)(2,1)S(1)} collective-permute-done((bf16[256,2048]{1,0:T(8,128)(2,1)S(1)}, bf16[256,2048]{1,0:T(8,128)(2,1)S(1)}, u32[]{:S(2)}, u32[]{:S(2)}) %collective-permute-start.32) | collective-permute-done | bytes 1048608 | tf_op jit(solution)/shard_map/ppermute | solution.py:73
  271.0 24.4 %fusion.153 = f32[2048,2048]{0,1:T(8,128)} fusion(bf16[2048,2048]{1,0:T(8,128)(2,1)} %constant_dynamic-update-slice_fusion.17, bf16[2048,2048]{1,0:T(8,128)(2,1)} %all-gather.9.cloned.1.call-done), kind=kOutput, calls=%fused_computation.388 | convolution fusion | flops 17179869184 | bytes 33554432 | tf_op jit(solution)/shard_map/dot_general | solution.py:31
  304.5 47.0 %all-gather.11.cloned.1.call-done = bf16[1024,2048]{1,0:T(8,128)(2,1)} async-done(((bf16[256,2048]{1,0:T(8,128)(2,1)}), bf16[1024,2048]{1,0:T(8,128)(2,1)}) %all-gather.11.cloned.1.call-update) | async-done | bytes 4194320 | tf_op jit(solution)/shard_map/all_gather | solution.py:79
  372.8 10.5 %collective-permute-done.46 = bf16[128,2048]{1,0:T(8,128)(2,1)S(1)} collective-permute-done((bf16[128,2048]{1,0:T(8,128)(2,1)S(1)}, bf16[128,2048]{1,0:T(8,128)(2,1)S(1)}, u32[]{:S(2)}, u32[]{:S(2)}) %collective-permute-start.46) | collective-permute-done | bytes 524320 | tf_op jit(solution)/shard_map/ppermute | solution.py:73
  410.7 21.6 %collective-permute-done.50 = bf16[256,2048]{1,0:T(8,128)(2,1)S(1)} collective-permute-done((bf16[256,2048]{1,0:T(8,128)(2,1)S(1)}, bf16[256,2048]{1,0:T(8,128)(2,1)S(1)}, u32[]{:S(2)}, u32[]{:S(2)}) %collective-permute-start.50) | collective-permute-done | bytes 1048608 | tf_op jit(solution)/shard_map/ppermute | solution.py:73
  451.5 10.5 %convolution_convert_fusion = bf16[1024,2048]{1,0:T(8,128)(2,1)} fusion(bf16[2048,1024]{0,1:T(8,128)(2,1)S(1)} %copy-done.28, bf16[2048,2048]{1,0:T(8,128)(2,1)S(1)} %constant_dynamic-update-slice_fusion.26), kind=kOutput, calls=%fused_computation.31 | convolution fusion | flops 8592031744 | bytes 16777216 | tf_op jit(solution)/shard_map/dot_general | solution.py:39
  462.1 20.9 %multiply_convert_fusion.1 = (bf16[2048,1024]{0,1:T(8,128)(2,1)S(1)}, bf16[2048,1024]{0,1:T(8,128)(2,1)}) fusion(f32[2048,2048]{0,1:T(8,128)} %fusion.153, bf16[2048,2048]{1,0:T(8,128)(2,1)} %copy-done.52, bf16[1024,2048]{1,0:T(8,128)(2,1)} %all-gather.11.cloned.1.call-done), kind=kOutput, calls=%fused_computation.12 | convolution fusion | flops 8617197568 | bytes 37748736 | tf_op jit(solution)/shard_map/dot_general | solution.py:35
  485.0 22.8 %fusion.7 = bf16[2048,2048]{1,0:T(8,128)(2,1)} fusion(bf16[2048,2048]{1,0:T(8,128)(2,1)} %constant_dynamic-update-slice_fusion.17, bf16[2048,1024]{0,1:T(8,128)(2,1)S(1)} %get-tuple-element.106, bf16[2048,1024]{0,1:T(8,128)(2,1)} %get-tuple-element.107), kind=kOutput, calls=%fused_computation.22 | convolution fusion | flops 17200840704 | bytes 25165824 | tf_op jit(solution)/shard_map/dot_general | solution.py:39
  507.9 12.8 %fusion.18 = bf16[1024,2048]{1,0:T(8,128)(2,1)S(1)} fusion(bf16[2048,2048]{1,0:T(8,128)(2,1)} %all-gather.9.cloned.1.call-done, bf16[2048,1024]{0,1:T(8,128)(2,1)} %get-tuple-element.107, bf16[2048,1024]{0,1:T(8,128)(2,1)} %copy-done.66), kind=kOutput, calls=%fused_computation.35 | convolution fusion | flops 8600420352 | bytes 20971520 | tf_op jit(solution)/shard_map/dot_general | solution.py:35
  521.7 12.6 %fusion.9 = f32[1024,2048]{1,0:T(8,128)S(1)} fusion(bf16[2048,2048]{1,0:T(8,128)(2,1)} %all-gather.9.cloned.1.call-done, bf16[2048,1024]{0,1:T(8,128)(2,1)} %get-tuple-element.107, bf16[2048,1024]{0,1:T(8,128)(2,1)} %copy-done.66), kind=kOutput, calls=%fused_computation.24 | convolution fusion | flops 8598323200 | bytes 25165824 | tf_op jit(solution)/shard_map/dot_general | solution.py:35
  539.9 10.4 %collective-permute-done.64 = bf16[128,2048]{1,0:T(8,128)(2,1)S(1)} collective-permute-done((bf16[128,2048]{1,0:T(8,128)(2,1)S(1)}, bf16[128,2048]{1,0:T(8,128)(2,1)S(1)}, u32[]{:S(2)}, u32[]{:S(2)}) %collective-permute-start.64) | collective-permute-done | bytes 524320 | tf_op jit(solution)/shard_map/ppermute | solution.py:73
  562.1 10.3 %collective-permute-done.65 = bf16[128,2048]{1,0:T(8,128)(2,1)S(1)} collective-permute-done((bf16[128,2048]{1,0:T(8,128)(2,1)S(1)}, bf16[128,2048]{1,0:T(8,128)(2,1)S(1)}, u32[]{:S(2)}, u32[]{:S(2)}) %collective-permute-start.65) | collective-permute-done | bytes 524320 | tf_op jit(solution)/shard_map/ppermute | solution.py:73
  580.0 22.4 %collective-permute-done.68 = bf16[256,2048]{1,0:T(8,128)(2,1)S(1)} collective-permute-done((bf16[256,2048]{1,0:T(8,128)(2,1)S(1)}, bf16[256,2048]{1,0:T(8,128)(2,1)S(1)}, u32[]{:S(2)}, u32[]{:S(2)}) %collective-permute-start.68) | collective-permute-done | bytes 1048608 | tf_op jit(solution)/shard_map/ppermute | solution.py:73
  642.6 11.1 %multiply_reduce_fusion = (f32[2,2,1024]{2,1,0:T(2,128)S(1)}, f32[2,2,1024,1024]{2,3,1,0:T(8,128)}) fusion(f32[2,2,1024,1024]{2,3,1,0:T(8,128)} %get-tuple-element.233, f32[2,2,1024]{2,1,0:T(2,128)S(1)} %copy-done.60, bf16[2,2,1024,128]{3,2,1,0:T(8,128)(2,1)S(1)} %bitcast.312, bf16[2,2,1024,128]{3,2,1,0:T(8,128)(2,1)S(1)} %bitcast.311), kind=kOutput, calls=%fused_computation.2 | convolution fusion | flops 1086320640 | bytes 35684352 | tf_op jit(solution)/shard_map/rhqd,rhkd->rhqk/dot_general | solution.py:306
  653.7 12.2 %multiply_convert_fusion = bf16[2,2,1024,1024]{2,3,1,0:T(8,128)(2,1)S(1)} fusion(f32[2,2,1024,1024]{2,3,1,0:T(8,128)} %get-tuple-element.235, f32[2,2,1024]{2,1,0:T(2,128)S(1)} %get-tuple-element.234, f32[2,2,1024,1024]{2,3,1,0:T(8,128)} %get-tuple-element.233, f32[2,2,1024]{2,1,0:T(2,128)S(1)} %copy-done.60), kind=kLoop, calls=%fused_computation.1 | loop fusion | flops 16777216 | bytes 41975808 | tf_op jit(solution)/shard_map/convert_element_type | solution.py:309
  721.6 10.4 %convolution_convert_fusion.4 = bf16[2048,768]{1,0:T(8,128)(2,1)} fusion(bf16[2048,2048]{1,0:T(8,128)(2,1)} %copy-done.51, bf16[2048,768]{1,0:T(8,128)(2,1)S(1)} %bitcast.293), kind=kOutput, calls=%fused_computation.36 | convolution fusion | flops 6444023808 | bytes 14680064 | tf_op jit(solution)/shard_map/dot_general | solution.py:39
  761.0 11.3 %collective-permute-done.97 = bf16[2,64,2048]{2,1,0:T(8,128)(2,1)S(1)} collective-permute-done((bf16[2,64,2048]{2,1,0:T(8,128)(2,1)}, bf16[2,64,2048]{2,1,0:T(8,128)(2,1)S(1)}, u32[]{:S(2)}, u32[]{:S(2)}) %collective-permute-start.97) | collective-permute-done | bytes 524320 | tf_op jit(solution)/shard_map/ppermute | solution.py:73
  795.2 11.1 %collective-permute-done.92 = bf16[128,2048]{1,0:T(8,128)(2,1)} collective-permute-done((bf16[128,2048]{1,0:T(8,128)(2,1)}, bf16[128,2048]{1,0:T(8,128)(2,1)}, u32[]{:S(2)}, u32[]{:S(2)}) %collective-permute-start.92) | collective-permute-done | bytes 524320 | tf_op jit(solution)/shard_map/ppermute | solution.py:73
  (622 shorter events, 460.9 us)
Async XLA Ops:
  7.2 111.1 %all-gather.5.cloned.1.call-start = ((), (), s32[]{:S(2)}) async-start(), calls=%async_computation.4 | async-start | bytes 3932160 | tf_op jit(solution)/shard_map/all_gather | solution.py:79
  27.2 145.7 %all-gather.7.cloned.1.call-start = ((), (), s32[]{:S(2)}) async-start(), calls=%async_computation.5 | async-start | bytes 1310720 | tf_op jit(solution)/shard_map/all_gather | solution.py:79
  76.0 195.1 %all-gather.9.cloned.1.call-start = ((), (), s32[]{:S(2)}) async-start(), calls=%async_computation.6 | async-start | bytes 10485760 | tf_op jit(solution)/shard_map/all_gather | solution.py:79
  81.8 24.5 %collective-permute-start.16 = (bf16[2,64,2048]{2,1,0:T(8,128)(2,1)S(1)}, bf16[2,64,2048]{2,1,0:T(8,128)(2,1)}, u32[]{:S(2)}, u32[]{:S(2)}) collective-permute-start(bf16[2,64,2048]{2,1,0:T(8,128)(2,1)S(1)} %get-tuple-element.54), channel_id=1, source_target_pairs={{0,6},{1,7},{2,4},{3,5},{4,2},{5,3},{6,0},{7,1},{8,14},{9,15},{10,... | collective-permute-start | bytes 1572872 | tf_op jit(solution)/shard_map/ppermute | solution.py:73
  118.0 233.5 %all-gather.11.cloned.1.call-start = ((), (), s32[]{:S(2)}) async-start(), calls=%async_computation.7 | async-start | bytes 5242880 | tf_op jit(solution)/shard_map/all_gather | solution.py:79
  185.2 25.1 %collective-permute-start.30 = (bf16[128,2048]{1,0:T(8,128)(2,1)S(1)}, bf16[128,2048]{1,0:T(8,128)(2,1)S(1)}, u32[]{:S(2)}, u32[]{:S(2)}) collective-permute-start(bf16[128,2048]{1,0:T(8,128)(2,1)S(1)} %slice.742), channel_id=1, source_target_pairs={{0,2},{1,3},{2,0},{3,1},{4,6},{5,7},{6,4},{7,5},{8,10},{9,11},{10,... | collective-permute-start | bytes 1572872 | tf_op jit(solution)/shard_map/ppermute | solution.py:73
  223.1 24.2 %collective-permute-start.32 = (bf16[256,2048]{1,0:T(8,128)(2,1)S(1)}, bf16[256,2048]{1,0:T(8,128)(2,1)S(1)}, u32[]{:S(2)}, u32[]{:S(2)}) collective-permute-start(bf16[256,2048]{1,0:T(8,128)(2,1)S(1)} %get-tuple-element.103), channel_id=1, source_target_pairs={{0,4},{1,5},{2,6},{3,7},{4,0},{5,1},{6,2},{7,3},{8,12},{9,13},{10,... | collective-permute-start | bytes 3145736 | tf_op jit(solution)/shard_map/ppermute | solution.py:73
  224.6 24.4 %collective-permute-start.31 = (bf16[256,2048]{1,0:T(8,128)(2,1)S(1)}, bf16[256,2048]{1,0:T(8,128)(2,1)S(1)}, u32[]{:S(2)}, u32[]{:S(2)}) collective-permute-start(bf16[256,2048]{1,0:T(8,128)(2,1)S(1)} %get-tuple-element.103), channel_id=1, source_target_pairs={{0,2},{1,3},{2,0},{3,1},{4,6},{5,7},{6,4},{7,5},{8,10},{9,11},{10,... | collective-permute-start | bytes 3145736 | tf_op jit(solution)/shard_map/ppermute | solution.py:73
  251.0 371.2 %reduce-scatter.5.cloned.1.call-start = ((), (), s32[]{:S(2)}) async-start(), calls=%async_computation.8 | async-start | bytes 5242880 | tf_op jit(solution)/shard_map/reduce_scatter | solution.py:82
  371.5 24.5 %collective-permute-start.48 = (bf16[128,2048]{1,0:T(8,128)(2,1)S(1)}, bf16[128,2048]{1,0:T(8,128)(2,1)S(1)}, u32[]{:S(2)}, u32[]{:S(2)}) collective-permute-start(bf16[128,2048]{1,0:T(8,128)(2,1)S(1)} %slice.740), channel_id=1, source_target_pairs={{0,2},{1,3},{2,0},{3,1},{4,6},{5,7},{6,4},{7,5},{8,10},{9,11},{10,... | collective-permute-start | bytes 1572872 | tf_op jit(solution)/shard_map/ppermute | solution.py:73
  409.3 24.7 %collective-permute-start.49 = (bf16[256,2048]{1,0:T(8,128)(2,1)S(1)}, bf16[256,2048]{1,0:T(8,128)(2,1)S(1)}, u32[]{:S(2)}, u32[]{:S(2)}) collective-permute-start(bf16[256,2048]{1,0:T(8,128)(2,1)S(1)} %get-tuple-element.99), channel_id=1, source_target_pairs={{0,2},{1,3},{2,0},{3,1},{4,6},{5,7},{6,4},{7,5},{8,10},{9,11},{10,... | collective-permute-start | bytes 3145736 | tf_op jit(solution)/shard_map/ppermute | solution.py:73
  462.0 241.9 %reduce-scatter.7.cloned.1.call-start = ((), (), s32[]{:S(2)}) async-start(), calls=%async_computation.9 | async-start | bytes 10485760 | tf_op jit(solution)/shard_map/reduce_scatter | solution.py:82
  507.8 236.4 %reduce-scatter.11.cloned.1.call-start = ((), (), s32[]{:S(2)}) async-start(), calls=%async_computation.11 | async-start | bytes 1310720 | tf_op jit(solution)/shard_map/reduce_scatter | solution.py:82
  537.2 24.9 %collective-permute-start.66 = (bf16[128,2048]{1,0:T(8,128)(2,1)S(1)}, bf16[128,2048]{1,0:T(8,128)(2,1)S(1)}, u32[]{:S(2)}, u32[]{:S(2)}) collective-permute-start(bf16[128,2048]{1,0:T(8,128)(2,1)S(1)} %slice.738), channel_id=1, source_target_pairs={{0,2},{1,3},{2,0},{3,1},{4,6},{5,7},{6,4},{7,5},{8,10},{9,11},{10,... | collective-permute-start | bytes 1572872 | tf_op jit(solution)/shard_map/ppermute | solution.py:73
  577.9 24.5 %collective-permute-start.68 = (bf16[256,2048]{1,0:T(8,128)(2,1)S(1)}, bf16[256,2048]{1,0:T(8,128)(2,1)S(1)}, u32[]{:S(2)}, u32[]{:S(2)}) collective-permute-start(bf16[256,2048]{1,0:T(8,128)(2,1)S(1)} %get-tuple-element.96), channel_id=1, source_target_pairs={{0,4},{1,5},{2,6},{3,7},{4,0},{5,1},{6,2},{7,3},{8,12},{9,13},{10,... | collective-permute-start | bytes 3145736 | tf_op jit(solution)/shard_map/ppermute | solution.py:73
  639.0 155.1 %reduce-scatter.9.cloned.1.call-start = ((), (), s32[]{:S(2)}) async-start(), calls=%async_computation.10 | async-start | bytes 3932160 | tf_op jit(solution)/shard_map/reduce_scatter | solution.py:82
  742.1 30.2 %collective-permute-start.91 = (bf16[256,2048]{1,0:T(8,128)(2,1)}, bf16[256,2048]{1,0:T(8,128)(2,1)S(1)}, u32[]{:S(2)}, u32[]{:S(2)}) collective-permute-start(bf16[256,2048]{1,0:T(8,128)(2,1)} %get-tuple-element.124), channel_id=1, source_target_pairs={{0,1},{1,0},{2,3},{3,2},{4,5},{5,4},{6,7},{7,6},{8,9},{9,8},{10,11... | collective-permute-start | bytes 3145736 | tf_op jit(solution)/shard_map/ppermute | solution.py:73
  742.1 30.2 %collective-permute-start.88 = (bf16[256,2048]{1,0:T(8,128)(2,1)}, bf16[256,2048]{1,0:T(8,128)(2,1)}, u32[]{:S(2)}, u32[]{:S(2)}) collective-permute-start(bf16[256,2048]{1,0:T(8,128)(2,1)} %get-tuple-element.125), channel_id=1, source_target_pairs={{0,1},{1,0},{2,3},{3,2},{4,5},{5,4},{6,7},{7,6},{8,9},{9,8},{10,11... | collective-permute-start | bytes 3145736 | tf_op jit(solution)/shard_map/ppermute | solution.py:73
  742.6 30.4 %collective-permute-start.86 = (bf16[256,2048]{1,0:T(8,128)(2,1)}, bf16[256,2048]{1,0:T(8,128)(2,1)}, u32[]{:S(2)}, u32[]{:S(2)}) collective-permute-start(bf16[256,2048]{1,0:T(8,128)(2,1)} %get-tuple-element.126), channel_id=1, source_target_pairs={{0,1},{1,0},{2,3},{3,2},{4,5},{5,4},{6,7},{7,6},{8,9},{9,8},{10,11... | collective-permute-start | bytes 3145736 | tf_op jit(solution)/shard_map/ppermute | solution.py:73
  747.2 25.1 %collective-permute-start.97 = (bf16[2,64,2048]{2,1,0:T(8,128)(2,1)}, bf16[2,64,2048]{2,1,0:T(8,128)(2,1)S(1)}, u32[]{:S(2)}, u32[]{:S(2)}) collective-permute-start(bf16[2,64,2048]{2,1,0:T(8,128)(2,1)} %get-tuple-element.70), channel_id=1, source_target_pairs={{0,6},{1,7},{2,4},{3,5},{4,2},{5,3},{6,0},{7,1},{8,14},{9,15},{10,... | collective-permute-start | bytes 1572872 | tf_op jit(solution)/shard_map/ppermute | solution.py:73
  761.0 63.3 %collective-permute-start.85 = (bf16[256,2048]{1,0:T(8,128)(2,1)}, bf16[256,2048]{1,0:T(8,128)(2,1)}, u32[]{:S(2)}, u32[]{:S(2)}) collective-permute-start(bf16[256,2048]{1,0:T(8,128)(2,1)} %get-tuple-element.127), channel_id=1, source_target_pairs={{0,1},{1,0},{2,3},{3,2},{4,5},{5,4},{6,7},{7,6},{8,9},{9,8},{10,11... | collective-permute-start | bytes 3145736 | tf_op jit(solution)/shard_map/ppermute | solution.py:73
  780.0 45.3 %collective-permute-start.87 = (bf16[128,2048]{1,0:T(8,128)(2,1)}, bf16[128,2048]{1,0:T(8,128)(2,1)S(1)}, u32[]{:S(2)}, u32[]{:S(2)}) collective-permute-start(bf16[128,2048]{1,0:T(8,128)(2,1)} %slice.737), channel_id=1, source_target_pairs={{0,4},{1,5},{2,6},{3,7},{4,0},{5,1},{6,2},{7,3},{8,12},{9,13},{10,... | collective-permute-start | bytes 1572872 | tf_op jit(solution)/shard_map/ppermute | solution.py:73
  782.0 44.5 %collective-permute-start.94 = (bf16[128,2048]{1,0:T(8,128)(2,1)}, bf16[128,2048]{1,0:T(8,128)(2,1)S(1)}, u32[]{:S(2)}, u32[]{:S(2)}) collective-permute-start(bf16[128,2048]{1,0:T(8,128)(2,1)} %slice.736), channel_id=1, source_target_pairs={{0,2},{1,3},{2,0},{3,1},{4,6},{5,7},{6,4},{7,5},{8,10},{9,11},{10,... | collective-permute-start | bytes 1572872 | tf_op jit(solution)/shard_map/ppermute | solution.py:73
  792.7 35.1 %collective-permute-start.90 = (bf16[128,2048]{1,0:T(8,128)(2,1)}, bf16[128,2048]{1,0:T(8,128)(2,1)}, u32[]{:S(2)}, u32[]{:S(2)}) collective-permute-start(bf16[128,2048]{1,0:T(8,128)(2,1)} %fusion.83), channel_id=1, source_target_pairs={{0,4},{1,5},{2,6},{3,7},{4,0},{5,1},{6,2},{7,3},{8,12},{9,13},{10,... | collective-permute-start | bytes 1572872 | tf_op jit(solution)/shard_map/ppermute | solution.py:73
  (153 other events, 1682.1 us)
Sparse Core Ops, SparseCore 0:
  27.3 64.8 all-gather.4
  93.8 26.6 all-gather.6
  122.0 148.9 all-gather.8
  272.5 78.9 all-gather.10
  462.1 74.7 reduce-scatter.4
  539.2 145.1 reduce-scatter.6
  686.6 27.8 reduce-scatter.10
  732.1 59.4 reduce-scatter.8
